TPU v7x, 256 devices: a whole 4x4x8 slice. The times are simulated.
256 devices in a mesh: gz: 8 (over z_lo, core), gx: 32 (over x, z_hi, y).
Axes of the slice: x: 4, y: 4, z: 8 (z_hi: 2, z_lo: 4; z = z_hi * 4 + z_lo), core: 2. Of those that a mesh axis runs over, the one named last changes fastest.
Arguments:
- state: float32 [6, 128, 8192], P(None, 'gz', 'gx'), may hold values from -5 to 5, as said below
- state_cot: float32 [6, 128, 8192], P(None, 'gz', 'gx'), may hold values from -6 to 6
- w_in: bfloat16 [128, 12], replicated, may hold values from -1.75 to 1.75
- w_mid: bfloat16 [128, 128], replicated, may hold values from -0.5 to 0.5
- w_out: bfloat16 [6, 128], replicated, may hold values from -0.5 to 0.5
- radiation: float32 [128, 128], replicated, may hold values from -0.5 to 0.5
- fall_rate: float32 [8192], P('gx'), may hold values from 20 to 2000
- active: int32 [8192], P('gx'), may hold values 0 or 1
Outputs:
- new_state: float32 [6, 128, 8192], P(None, 'gz', 'gx')
- state_grad: float32 [6, 128, 8192], P(None, 'gz', 'gx')
- grad_in: float32 [128, 12], replicated
- grad_mid: float32 [128, 128], replicated
- grad_out: float32 [6, 128], replicated
Inputs may be any that keep to these rules, and one draw needn't show every extreme that they name: `state`: fields come in the order u, v, w, theta, total water, rain water; rain water lies between 0.05 and 1.
All inputs are finite; a program needn't handle non-finite values. No bound on the sum of `active` on one device may be relied on, other than what follows from the above.
Results may differ from a plain program's by a relative error of at most 0.00045.
The roundings to bfloat16 on the way count: a program that leaves them out, or rounds other values in their place, can miss the bound.
Values sent between devices are 32-bit elements; how exact they have to be, the bound alone decides.
No kernel may reach another device: no remote copies, remote signals or barrier semaphores. Data moves between devices by JAX's collectives and lax.ppermute only.
A program may use at most 64 MiB of HBM per device.

v0:
```python
import jax
import jax.numpy as jnp
from jax import lax
from jax.sharding import PartitionSpec as P

NY = 64


DIFFUSION = 0.1
TIME_STEP = 0.25
CLOSURE_GAIN = 1.0
HEATING_GAIN = 1.0
FALL_GAIN = 1.0


def prefix(shard, axis, combine, identity, reverse):
    length, index = (lax.axis_size(axis), lax.axis_index(axis))
    everything = jax.tree.map(lambda part: lax.all_gather(part, axis), shard)
    start = jax.tree.map(
        lambda part, zero: jnp.broadcast_to(jnp.asarray(zero, part.dtype), part.shape),
        shard,
        identity,
    )

    def step(k, before):
        at = length - 1 - k if reverse else k
        reached = at > index if reverse else at < index
        new = combine(before, jax.tree.map(lambda part: part[at], everything))
        return jax.tree.map(lambda a, b: jnp.where(reached, a, b), new, before)

    return lax.fori_loop(0, length, step, start)


def passed_along(shard, axis, by):
    length = lax.axis_size(axis)
    return lax.ppermute(shard, axis, [(i, (i + by) % length) for i in range(length)])


def padded_2(shard, sides, width):
    for axis, dim in sides:
        size, length = (lax.axis_size(axis), shard.shape[dim])
        up = [(i, (i + 1) % size) for i in range(size)]
        down = [(j, i) for i, j in up]
        last = lax.slice_in_dim(shard, length - width, length, axis=dim)
        first = lax.slice_in_dim(shard, 0, width, axis=dim)
        before = lax.ppermute(last, axis, up)
        after = lax.ppermute(first, axis, down)
        shard = jnp.concatenate([before, shard, after], axis=dim)
    return shard


def contract(left, right, left_dim, right_dim):
    return lax.dot_general(
        left, right, (((left_dim,), (right_dim,)), ((), ())), preferred_element_type=jnp.float32
    )


def mlp_forward(features, w_in, w_mid, w_out):
    hidden_one = jnp.tanh(jnp.dot(w_in, features, preferred_element_type=jnp.float32)).astype(
        jnp.bfloat16
    )
    hidden_two = jnp.tanh(jnp.dot(w_mid, hidden_one, preferred_element_type=jnp.float32)).astype(
        jnp.bfloat16
    )
    return jnp.dot(w_out, hidden_two, preferred_element_type=jnp.float32)


def mlp_backward(features, out_cot, w_in, w_mid, w_out):
    tanh_one = jnp.tanh(jnp.dot(w_in, features, preferred_element_type=jnp.float32))
    hidden_one = tanh_one.astype(jnp.bfloat16)
    tanh_two = jnp.tanh(jnp.dot(w_mid, hidden_one, preferred_element_type=jnp.float32))
    hidden_two = tanh_two.astype(jnp.bfloat16)
    term_out = contract(out_cot, hidden_two, 1, 1)
    pre_two = (contract(w_out, out_cot, 0, 0) * (1.0 - tanh_two * tanh_two)).astype(jnp.bfloat16)
    term_mid = contract(pre_two, hidden_one, 1, 1)
    pre_one = (contract(w_mid, pre_two, 0, 0) * (1.0 - tanh_one * tanh_one)).astype(jnp.bfloat16)
    term_in = contract(pre_one, features, 1, 1)
    feature_cot = contract(w_in, pre_one, 0, 0)
    return (feature_cot, (term_in, term_mid, term_out))


def interior(padded):
    return padded[..., 2 * NY : padded.shape[-1] - 2 * NY]


def dynamics(padded):
    columns = padded.shape[-1] - 4 * NY

    def along_x(offset):
        first_col = 2 * NY + offset * NY
        return padded[..., first_col : first_col + columns]

    center = along_x(0)
    y_place = jnp.arange(columns) % NY
    y_last = y_place == NY - 1
    y_first = y_place == 0
    y_plus = jnp.where(y_last, jnp.roll(center, NY - 1, -1), jnp.roll(center, -1, -1))
    y_minus = jnp.where(y_first, jnp.roll(center, 1 - NY, -1), jnp.roll(center, 1, -1))
    x_plus, x_minus = (along_x(1), along_x(-1))
    deriv_x = (8.0 * (x_plus - x_minus) - (along_x(2) - along_x(-2))) / 12.0
    deriv_y = (y_plus - y_minus) / 2.0
    laplace = x_plus + x_minus + y_plus + y_minus - 4.0 * center
    return (-(center[0] * deriv_x + center[1] * deriv_y) + DIFFUSION * laplace, deriv_x)


def compose(earlier, later):
    return (later[0] * earlier[0], later[1] + later[0] * earlier[1])


def running_maps(source, retained):
    factors = jnp.broadcast_to(retained, source.shape)
    return lax.associative_scan(compose, (factors, source), axis=0)


def sediment_forward(rain_water, fall_speed):
    fresh_share = 1.0 / (1.0 + fall_speed)
    retained = fall_speed / (1.0 + fall_speed)
    factors, values = running_maps(jnp.flip(fresh_share * rain_water, 0), retained)
    inflow = prefix(
        (factors[-1], values[-1]),
        "gz",
        compose,
        (jnp.ones_like(fall_speed), jnp.zeros_like(fall_speed)),
        True,
    )
    return jnp.flip(values + factors * inflow[1], 0)


def sediment_adjoint(source, fall_speed):
    fresh_share = 1.0 / (1.0 + fall_speed)
    retained = fall_speed / (1.0 + fall_speed)
    factors, values = running_maps(fresh_share * source, retained)
    inflow = prefix(
        (factors[-1], values[-1]),
        "gz",
        compose,
        (jnp.ones_like(fall_speed), jnp.zeros_like(fall_speed)),
        False,
    )
    return values + factors * inflow[1]


def heating(theta, radiation):
    levels = theta.shape[0]
    own_rows = lax.dynamic_slice_in_dim(radiation, lax.axis_index("gz") * levels, levels, 0)
    return jnp.dot(
        own_rows,
        lax.all_gather(theta, "gz", axis=0, tiled=True),
        precision=lax.Precision.HIGHEST,
        preferred_element_type=jnp.float32,
    )


def heating_adjoint(lead_theta, radiation):
    levels = lead_theta.shape[0]
    own_rows = lax.dynamic_slice_in_dim(radiation, lax.axis_index("gz") * levels, levels, 0)
    return lax.psum_scatter(
        lax.dot_general(
            own_rows,
            lead_theta,
            (((0,), (0,)), ((), ())),
            precision=lax.Precision.HIGHEST,
            preferred_element_type=jnp.float32,
        ),
        "gz",
        scatter_dimension=0,
        tiled=True,
    )


def tendency(padded, w_in, w_mid, w_out, radiation, fall_speed, live):
    moved, deriv_x = dynamics(padded)
    center = interior(padded)
    fields, levels, columns = center.shape
    features = (
        jnp.concatenate([center, deriv_x], 0)
        .astype(jnp.bfloat16)
        .reshape(2 * fields, levels * columns)
    )
    closure = mlp_forward(features, w_in, w_mid, w_out).reshape(fields, levels, columns)
    total = moved + CLOSURE_GAIN * closure
    total = total.at[3].add(HEATING_GAIN * heating(center[3], radiation))
    fallen = sediment_forward(center[5], fall_speed)
    return total.at[5].add(FALL_GAIN * live * (fallen - center[5]))


def adjoint_tendency(padded, lead, w_in, w_mid, w_out, radiation, fall_speed, live):
    outputs, pullback = jax.vjp(dynamics, padded)
    center = interior(padded)
    fields, levels, columns = center.shape
    features = (
        jnp.concatenate([center, outputs[1]], 0)
        .astype(jnp.bfloat16)
        .reshape(2 * fields, levels * columns)
    )
    out_cot = (CLOSURE_GAIN * lead).astype(jnp.bfloat16).reshape(fields, levels * columns)
    feature_cot, grads = mlp_backward(features, out_cot, w_in, w_mid, w_out)
    feature_cot = feature_cot.reshape(2 * fields, levels, columns)
    padded_cot = pullback((lead, feature_cot[fields:]))[0]
    rim_width = 2 * NY
    from_next = passed_along(padded_cot[..., :rim_width], "gx", -1)
    from_prev = passed_along(padded_cot[..., padded_cot.shape[-1] - rim_width :], "gx", 1)
    result = interior(padded_cot) + feature_cot[:fields]
    result = result.at[..., :rim_width].add(from_prev)
    result = result.at[..., columns - rim_width :].add(from_next)
    result = result.at[3].add(HEATING_GAIN * heating_adjoint(lead[3], radiation))
    masked = live * lead[5]
    return (result.at[5].add(FALL_GAIN * (sediment_adjoint(masked, fall_speed) - masked)), grads)


def on_device(state, state_cot, w_in, w_mid, w_out, radiation, fall_rate, active):
    live = active.astype(jnp.float32)

    def extend(fields):
        return padded_2(fields, (("gx", 2),), 2 * NY)

    def section_tendency(padded):
        return tendency(padded, w_in, w_mid, w_out, radiation, fall_rate, live)

    def section_adjoint(padded, lead):
        return adjoint_tendency(padded, lead, w_in, w_mid, w_out, radiation, fall_rate, live)

    padded_zero = extend(state)
    section_one = state + TIME_STEP * section_tendency(padded_zero)
    padded_one = extend(section_one)
    section_two = 0.75 * state + 0.25 * (section_one + TIME_STEP * section_tendency(padded_one))
    padded_two = extend(section_two)
    new_state = state / 3.0 + 2.0 / 3.0 * (section_two + TIME_STEP * section_tendency(padded_two))
    lead_two = 2.0 / 3.0 * state_cot
    grad_state = state_cot / 3.0
    back_two, grads_two = section_adjoint(padded_two, lead_two)
    cot_two = lead_two + TIME_STEP * back_two
    lead_one = 0.25 * cot_two
    grad_state = grad_state + 0.75 * cot_two
    back_one, grads_one = section_adjoint(padded_one, lead_one)
    cot_one = lead_one + TIME_STEP * back_one
    back_zero, grads_zero = section_adjoint(padded_zero, cot_one)
    grad_state = grad_state + cot_one + TIME_STEP * back_zero
    totals = lax.psum(
        (
            TIME_STEP * (grads_two[0] + grads_one[0] + grads_zero[0]),
            TIME_STEP * (grads_two[1] + grads_one[1] + grads_zero[1]),
            TIME_STEP * (grads_two[2] + grads_one[2] + grads_zero[2]),
        ),
        ("gz", "gx"),
    )
    return (new_state, grad_state, totals[0], totals[1], totals[2])


def solution(mesh):
    placed = (P(None, "gz", "gx"), P(None, "gz", "gx"), P(), P(), P(), P(), P("gx"), P("gx"))
    return jax.shard_map(
        on_device,
        mesh=mesh,
        in_specs=placed,
        out_specs=(P(None, "gz", "gx"), P(None, "gz", "gx"), P(), P(), P()),
        check_vma=False,
    )
```

profile of v0, /device:TPU:1, one launch (start us, length us, event | category | flops | bytes accessed | tf_op | source)
XLA Modules:
  0.0 674.6 jit_solution(1791743276329991955)
XLA Ops:
  8.1 12.5 %collective-permute-start = (f32[6,16,128]{2,1,0:T(8,128)S(1)}, f32[6,16,128]{2,1,0:T(8,128)S(1)}, u32[]{:S(2)}, u32[]{:S(2)}) collective-permute-start(f32[6,16,128]{2,1,0:T(8,128)S(1)} %get-tuple-element.1230), channel_id=1, source_target_pairs={{1,0},{2,1},{3,2},{4,3},{5,4},{6,5},{7,6},{8,7},{9,8},{10,9},{11,1... | collective-permute-start | bytes 147464 | tf_op jit(solution)/shard_map/ppermute | solution.py:47
  21.9 1.4 bitcast_multiply_fusion
  23.6 1.5 fusion.147
  25.2 1.5 fusion.146
  27.7 1.6 fusion.145
  30.5 11.1 %all-gather.3 = f32[8,1,256]{2,1,0:T(1,128)S(1)} all-gather(f32[1,1,256]{2,1,0:T(1,128)S(1)} %add_bitcast_fusion.6), channel_id=1, replica_groups=mesh['gz'=8,'gx'=32] {'gz'}, dimensions={0}, use_global_device_ids=true | all-gather | bytes 9216 | tf_op jit(solution)/shard_map/all_gather | solution.py:18
  41.6 8.7 %all-gather.4 = f32[8,1,256]{2,1,0:T(1,128)S(1)} all-gather(f32[1,1,256]{2,1,0:T(1,128)S(1)} %add_bitcast_fusion.5), channel_id=1, replica_groups=mesh['gz'=8,'gx'=32] {'gz'}, dimensions={0}, use_global_device_ids=true | all-gather | bytes 9216 | tf_op jit(solution)/shard_map/all_gather | solution.py:18
  51.5 14.0 %all-gather = f32[1,128,256]{2,1,0:T(8,128)S(1)} all-gather(f32[1,16,256]{2,1,0:T(8,128)S(1)} %slice-done), channel_id=2, replica_groups=mesh['gz'=8,'gx'=32] {'gz'}, dimensions={1}, use_global_device_ids=true | all-gather | bytes 147456 | tf_op jit(solution)/shard_map/all_gather | solution.py:148
  73.2 10.1 %all-gather.5 = f32[8,1,256]{2,1,0:T(1,128)S(1)} all-gather(f32[1,1,256]{2,1,0:T(1,128)S(1)} %add_bitcast_fusion.4), channel_id=1, replica_groups=mesh['gz'=8,'gx'=32] {'gz'}, dimensions={0}, use_global_device_ids=true | all-gather | bytes 9216 | tf_op jit(solution)/shard_map/all_gather | solution.py:18
  83.8 9.9 %collective-permute-start.2 = (f32[6,16,128]{2,1,0:T(8,128)S(1)}, f32[6,16,128]{2,1,0:T(8,128)S(1)}, u32[]{:S(2)}, u32[]{:S(2)}) collective-permute-start(f32[6,16,128]{2,1,0:T(8,128)S(1)} %get-tuple-element.1214), channel_id=1, source_target_pairs={{1,0},{2,1},{3,2},{4,3},{5,4},{6,5},{7,6},{8,7},{9,8},{10,9},{11,1... | collective-permute-start | bytes 147464 | tf_op jit(solution)/shard_map/ppermute | solution.py:47
  93.8 14.3 %all-gather.1 = f32[1,128,256]{2,1,0:T(8,128)S(1)} all-gather(f32[1,16,256]{2,1,0:T(8,128)S(1)} %get-tuple-element.1172), channel_id=3, replica_groups=mesh['gz'=8,'gx'=32] {'gz'}, dimensions={1}, use_global_device_ids=true | all-gather | bytes 147456 | tf_op jit(solution)/shard_map/all_gather | solution.py:148
  113.3 9.9 %collective-permute-start.4 = (f32[6,16,128]{2,1,0:T(8,128)S(1)}, f32[6,16,128]{2,1,0:T(8,128)S(1)}, u32[]{:S(2)}, u32[]{:S(2)}) collective-permute-start(f32[6,16,128]{2,1,0:T(8,128)S(1)} %get-tuple-element.1193), channel_id=1, source_target_pairs={{1,0},{2,1},{3,2},{4,3},{5,4},{6,5},{7,6},{8,7},{9,8},{10,9},{11,1... | collective-permute-start | bytes 147464 | tf_op jit(solution)/shard_map/ppermute | solution.py:47
  123.2 15.5 %all-gather.2 = f32[1,128,256]{2,1,0:T(8,128)} all-gather(f32[1,16,256]{2,1,0:T(8,128)S(1)} %get-tuple-element.1188), channel_id=4, replica_groups=mesh['gz'=8,'gx'=32] {'gz'}, dimensions={1}, use_global_device_ids=true | all-gather | bytes 147456 | tf_op jit(solution)/shard_map/all_gather | solution.py:148
  138.7 1.5 broadcast_multiply_fusion
  153.3 8.7 %all-gather.7 = f32[8,1,256]{2,1,0:T(1,128)S(1)} all-gather(f32[1,1,256]{2,1,0:T(1,128)S(1)} %add_bitcast_fusion.2), channel_id=1, replica_groups=mesh['gz'=8,'gx'=32] {'gz'}, dimensions={0}, use_global_device_ids=true | all-gather | bytes 9216 | tf_op jit(solution)/shard_map/all_gather | solution.py:18
  162.1 8.8 %while.111 = (s32[]{:T(128)}, f32[256]{0:T(256)}, s32[]{:T(128)}, f32[8,256]{1,0:T(8,128)S(1)}, f32[8,256]{1,0:T(8,128)S(1)}, /*index=5*/s32[]{:T(128)}, s32[]{:T(128)}) while((s32[]{:T(128)}, f32[256]{0:T(256)}, s32[]{:T(128)}, f32[8,256]{1,0:T(8,128)S(1)}, f32[8,256]{1,0:T(8,128)S(1)}, /*index=5*/s32[]{:T(128)}, ...), condition=%wide.region_10.11_spmd.clone, body=%wide.region_9.10_spmd.clone.sunk | while | flops 1028 | bytes 8301 | solution.py:31
  170.9 9.9 %collective-permute-start.7 = (f32[6,16,128]{2,1,0:T(8,128)S(1)}, f32[6,16,128]{2,1,0:T(8,128)S(1)}, u32[]{:S(2)}, u32[]{:S(2)}) collective-permute-start(f32[6,16,128]{2,1,0:T(8,128)S(1)} %get-tuple-element.1127), channel_id=1, source_target_pairs={{0,31},{1,0},{2,1},{3,2},{4,3},{5,4},{6,5},{7,6},{8,7},{9,8},{10,9... | collective-permute-start | bytes 147464 | tf_op jit(solution)/shard_map/ppermute | solution.py:36
  180.9 11.1 %collective-permute-done.6 = f32[6,16,128]{2,1,0:T(8,128)S(1)} collective-permute-done((f32[6,16,128]{2,1,0:T(8,128)S(1)}, f32[6,16,128]{2,1,0:T(8,128)S(1)}, u32[]{:S(2)}, u32[]{:S(2)}) %collective-permute-start.6) | collective-permute-done | bytes 49184 | tf_op jit(solution)/shard_map/ppermute | solution.py:36
  192.0 12.1 %reduce-scatter.4.cloned.1.call-done = f32[16,256]{1,0:T(8,128)} async-done(((f32[128,256]{1,0:T(8,128)}), f32[16,256]{1,0:T(8,128)}) %reduce-scatter.4.cloned.1.call-update) | async-done | bytes 16400 | tf_op jit(solution)/shard_map/reduce_scatter | solution.py:157
  211.1 2.2 fusion.2
  218.2 1.8 pad.467
  220.1 1.9 pad.468
  221.9 1.3 add.1082
  225.2 1.9 pad.470
  227.0 1.3 add.1084
  230.4 1.9 pad.472
  233.0 12.0 %all-gather.8 = f32[8,1,256]{2,1,0:T(1,128)S(1)} all-gather(f32[1,1,256]{2,1,0:T(1,128)S(1)} %add_bitcast_fusion.1), channel_id=1, replica_groups=mesh['gz'=8,'gx'=32] {'gz'}, dimensions={0}, use_global_device_ids=true | all-gather | bytes 9216 | tf_op jit(solution)/shard_map/all_gather | solution.py:18
  245.6 15.3 %while.112 = (s32[]{:T(128)}, f32[256]{0:T(256)}, s32[]{:T(128)}, f32[8,256]{1,0:T(8,128)}, f32[8,256]{1,0:T(8,128)}, /*index=5*/s32[]{:T(128)}, s32[]{:T(128)}) while((s32[]{:T(128)}, f32[256]{0:T(256)}, s32[]{:T(128)}, f32[8,256]{1,0:T(8,128)}, f32[8,256]{1,0:T(8,128)}, /*index=5*/s32[]{:T(128)}, s32[]{:T(128)}) %tuple.457), condition=%wide.region_15.16_spmd.clone, body=%wide.region_14.15_spmd.clone.sunk | while | flops 1028 | bytes 8301 | solution.py:31
  260.9 2.6 convolution_add_fusion.5
  263.5 2.4 convolution_add_fusion.1
  266.9 7.8 %collective-permute-start.9 = (f32[6,16,128]{2,1,0:T(8,128)}, f32[6,16,128]{2,1,0:T(8,128)S(1)}, u32[]{:S(2)}, u32[]{:S(2)}) collective-permute-start(f32[6,16,128]{2,1,0:T(8,128)} %get-tuple-element.1125), channel_id=1, source_target_pairs={{0,31},{1,0},{2,1},{3,2},{4,3},{5,4},{6,5},{7,6},{8,7},{9,8},{10,9... | collective-permute-start | bytes 147464 | tf_op jit(solution)/shard_map/ppermute | solution.py:36
  275.7 10.3 %collective-permute-done.8 = f32[6,16,128]{2,1,0:T(8,128)S(1)} collective-permute-done((f32[6,16,128]{2,1,0:T(8,128)}, f32[6,16,128]{2,1,0:T(8,128)S(1)}, u32[]{:S(2)}, u32[]{:S(2)}) %collective-permute-start.8) | collective-permute-done | bytes 49184 | tf_op jit(solution)/shard_map/ppermute | solution.py:36
  286.1 12.3 %reduce-scatter.6.cloned.1.call-done = f32[16,256]{1,0:T(8,128)} async-done(((f32[128,256]{1,0:T(8,128)}), f32[16,256]{1,0:T(8,128)}) %reduce-scatter.6.cloned.1.call-update) | async-done | bytes 16400 | tf_op jit(solution)/shard_map/reduce_scatter | solution.py:157
  299.9 1.6 multiply_reduce_fusion.1
  328.3 1.3 add.1046
  330.2 1.3 fusion.92
  332.1 1.3 pad_maximum_fusion.19
  334.2 1.9 pad.495
  336.8 12.1 %all-gather.9 = f32[8,1,256]{2,1,0:T(1,128)S(1)} all-gather(f32[1,1,256]{2,1,0:T(1,128)S(1)} %add_bitcast_fusion), channel_id=1, replica_groups=mesh['gz'=8,'gx'=32] {'gz'}, dimensions={0}, use_global_device_ids=true | all-gather | bytes 9216 | tf_op jit(solution)/shard_map/all_gather | solution.py:18
  349.4 14.0 %while.113 = (s32[]{:T(128)}, f32[256]{0:T(256)}, s32[]{:T(128)}, f32[8,256]{1,0:T(8,128)}, f32[8,256]{1,0:T(8,128)}, /*index=5*/s32[]{:T(128)}, s32[]{:T(128)}) while((s32[]{:T(128)}, f32[256]{0:T(256)}, s32[]{:T(128)}, f32[8,256]{1,0:T(8,128)}, f32[8,256]{1,0:T(8,128)}, /*index=5*/s32[]{:T(128)}, s32[]{:T(128)}) %tuple.458), condition=%wide.region_20.21_spmd.clone, body=%wide.region_19.20_spmd.clone.sunk | while | flops 1028 | bytes 8301 | solution.py:31
  364.2 10.4 %all-gather.6 = f32[8,1,256]{2,1,0:T(1,128)S(1)} all-gather(f32[1,1,256]{2,1,0:T(1,128)S(1)} %add_bitcast_fusion.3), channel_id=1, replica_groups=mesh['gz'=8,'gx'=32] {'gz'}, dimensions={0}, use_global_device_ids=true | all-gather | bytes 9216 | tf_op jit(solution)/shard_map/all_gather | solution.py:18
  375.1 14.2 %while.110 = (s32[]{:T(128)}, f32[256]{0:T(256)}, s32[]{:T(128)}, f32[8,256]{1,0:T(8,128)}, f32[8,256]{1,0:T(8,128)}, /*index=5*/s32[]{:T(128)}, s32[]{:T(128)}, s32[]{:T(128)}, s32[]{:T(128)}) while((s32[]{:T(128)}, f32[256]{0:T(256)}, s32[]{:T(128)}, f32[8,256]{1,0:T(8,128)}, f32[8,256]{1,0:T(8,128)}, /*index=5*/s32[]{:T(128)}, ...), condition=%wide.region_5.6_spmd.clone, body=%wide.region_4.5_spmd.clone.sunk | while | flops 1032 | bytes 8363 | solution.py:31
  389.5 1.8 fusion.14
  391.5 2.5 fusion.6
  395.7 8.6 %collective-permute-start.11 = (f32[6,16,128]{2,1,0:T(8,128)S(1)}, f32[6,16,128]{2,1,0:T(8,128)S(1)}, u32[]{:S(2)}, u32[]{:S(2)}) collective-permute-start(f32[6,16,128]{2,1,0:T(8,128)S(1)} %copy-done.103), channel_id=1, source_target_pairs={{0,31},{1,0},{2,1},{3,2},{4,3},{5,4},{6,5},{7,6},{8,7},{9,8},{10,9... | collective-permute-start | bytes 147464 | tf_op jit(solution)/shard_map/ppermute | solution.py:36
  404.7 73.1 %all-reduce.101 = (f32[128,12]{0,1:T(8,128)}, f32[6,128]{1,0:T(8,128)}) all-reduce(f32[128,12]{0,1:T(8,128)S(1)} %fusion.13, f32[6,128]{1,0:T(8,128)S(1)} %copy-done.124), channel_id=1, replica_groups=mesh['gz'=8,'gx'=32] {'gz','gx'}, use_global_device_ids=true, to_apply=%region_21.22 | all-reduce | flops 2304 | bytes 18432 | tf_op jit(solution)/shard_map/psum | solution.py:239
  480.0 186.6 %all-reduce.104.cloned.1.call-done = f32[128,128]{1,0:T(8,128)} async-done(((f32[128,128]{1,0:T(8,128)}), f32[128,128]{1,0:T(8,128)}) %all-reduce.104.cloned.1.call-update) | async-done | bytes 65552 | tf_op jit(solution)/shard_map/psum | solution.py:239
  666.6 1.5 copy.127
  (725 shorter events, 139.6 us)
Async XLA Ops:
  7.2 62.3 %copy-start = (f32[128,128]{1,0:T(8,128)S(1)}, f32[128,128]{1,0:T(8,128)}, u32[]{:S(2)}) copy-start(f32[128,128]{1,0:T(8,128)} %param.61) | copy-start | bytes 196612
  7.2 44.3 %slice-start = ((f32[6,16,256]{2,1,0:T(8,128)}), f32[1,16,256]{2,1,0:T(8,128)S(1)}, s32[]{:S(2)}) async-start(f32[6,16,256]{2,1,0:T(8,128)} %param.56), calls=%async_computation.7 | async-start | bytes 32768 | tf_op jit(solution)/shard_map/slice | solution.py:182
  7.2 58.3 %copy-start.8 = (f32[6,16,256]{2,1,0:T(8,128)S(1)}, f32[6,16,256]{2,1,0:T(8,128)}, u32[]{:S(2)}) copy-start(f32[6,16,256]{2,1,0:T(8,128)} %param.56) | copy-start | bytes 294916
  7.2 58.5 %copy-start.63 = (bf16[128,12]{0,1:T(8,128)(2,1)S(1)}, bf16[128,12]{0,1:T(8,128)(2,1)}, u32[]{:S(2)}) copy-start(bf16[128,12]{0,1:T(8,128)(2,1)} %param.58) | copy-start | bytes 9220
  7.2 196.9 %reduce-scatter.4.cloned.1.call-start = ((), (), s32[]{:S(2)}) async-start(), calls=%async_computation.3 | async-start | bytes 147456 | tf_op jit(solution)/shard_map/reduce_scatter | solution.py:157
  8.1 57.4 %collective-permute-start = (f32[6,16,128]{2,1,0:T(8,128)S(1)}, f32[6,16,128]{2,1,0:T(8,128)S(1)}, u32[]{:S(2)}, u32[]{:S(2)}) collective-permute-start(f32[6,16,128]{2,1,0:T(8,128)S(1)} %get-tuple-element.1230), channel_id=1, source_target_pairs={{1,0},{2,1},{3,2},{4,3},{5,4},{6,5},{7,6},{8,7},{9,8},{10,9},{11,1... | collective-permute-start | bytes 147464 | tf_op jit(solution)/shard_map/ppermute | solution.py:47
  20.6 44.9 %collective-permute-start.1 = (f32[6,16,128]{2,1,0:T(8,128)S(1)}, f32[6,16,128]{2,1,0:T(8,128)S(1)}, u32[]{:S(2)}, u32[]{:S(2)}) collective-permute-start(f32[6,16,128]{2,1,0:T(8,128)S(1)} %get-tuple-element.1231), channel_id=1, source_target_pairs={{0,1},{1,2},{2,3},{3,4},{4,5},{5,6},{6,7},{7,8},{8,9},{9,10},{10,1... | collective-permute-start | bytes 147464 | tf_op jit(solution)/shard_map/ppermute | solution.py:46
  21.9 119.7 %copy-start.66 = (f32[256]{0:T(256)}, f32[256]{0:T(256)S(1)}, u32[]{:S(2)}) copy-start(f32[256]{0:T(256)S(1)} %get-tuple-element.1104) | copy-start | bytes 3076
  21.9 130.7 %copy-start.60 = (f32[256]{0:T(256)}, f32[256]{0:T(256)S(1)}, u32[]{:S(2)}) copy-start(f32[256]{0:T(256)S(1)} %get-tuple-element.1105) | copy-start | bytes 3076
  23.3 118.3 %copy-start.47 = (f32[256]{0:T(256)}, f32[256]{0:T(256)S(1)}, u32[]{:S(2)}) copy-start(f32[256]{0:T(256)S(1)} %get-tuple-element.1275) | copy-start | bytes 3076
  30.0 110.2 %copy-start.71 = (f32[256]{0:T(256)}, f32[256]{0:T(256)S(1)}, u32[]{:S(2)}) copy-start(f32[256]{0:T(256)S(1)} %convert_element_type.59) | copy-start | bytes 3076
  50.3 15.9 %copy-start.16 = (bf16[128,128]{1,0:T(8,128)(2,1)S(1)}, bf16[128,128]{1,0:T(8,128)(2,1)}, u32[]{:S(2)}) copy-start(bf16[128,128]{1,0:T(8,128)(2,1)} %param.59) | copy-start | bytes 98308
  50.8 154.0 %copy-start.32 = (f32[16,256]{1,0:T(8,128)}, f32[16,256]{1,0:T(8,128)S(1)}, u32[]{:S(2)}) copy-start(f32[16,256]{1,0:T(8,128)S(1)} %get-tuple-element.1103) | copy-start | bytes 49156
  72.9 36.3 %copy-start.26 = (bf16[1,6,16,256]{3,1,2,0:T(8,128)(2,1)}, bf16[1,6,16,256]{3,1,2,0:T(8,128)(2,1)S(1)}, u32[]{:S(2)}) copy-start(bf16[1,6,16,256]{3,1,2,0:T(8,128)(2,1)S(1)} %copy.23) | copy-start | bytes 147460
  83.8 24.2 %collective-permute-start.2 = (f32[6,16,128]{2,1,0:T(8,128)S(1)}, f32[6,16,128]{2,1,0:T(8,128)S(1)}, u32[]{:S(2)}, u32[]{:S(2)}) collective-permute-start(f32[6,16,128]{2,1,0:T(8,128)S(1)} %get-tuple-element.1214), channel_id=1, source_target_pairs={{1,0},{2,1},{3,2},{4,3},{5,4},{6,5},{7,6},{8,7},{9,8},{10,9},{11,1... | collective-permute-start | bytes 147464 | tf_op jit(solution)/shard_map/ppermute | solution.py:47
  93.8 14.3 %collective-permute-start.3 = (f32[6,16,128]{2,1,0:T(8,128)S(1)}, f32[6,16,128]{2,1,0:T(8,128)S(1)}, u32[]{:S(2)}, u32[]{:S(2)}) collective-permute-start(f32[6,16,128]{2,1,0:T(8,128)S(1)} %get-tuple-element.1215), channel_id=1, source_target_pairs={{0,1},{1,2},{2,3},{3,4},{4,5},{5,6},{6,7},{7,8},{8,9},{9,10},{10,1... | collective-permute-start | bytes 147464 | tf_op jit(solution)/shard_map/ppermute | solution.py:46
  110.6 28.1 %copy-start.11 = (f32[6,16,256]{2,1,0:T(8,128)S(1)}, f32[6,16,256]{2,1,0:T(8,128)}, u32[]{:S(2)}) copy-start(f32[6,16,256]{2,1,0:T(8,128)} %param.57) | copy-start | bytes 294916
  112.0 28.2 %copy-start.107 = (f32[256]{0:T(256)S(1)}, f32[256]{0:T(256)}, u32[]{:S(2)}) copy-start(f32[256]{0:T(256)} %copy-done.105) | copy-start | bytes 3076
  112.0 29.6 %copy-start.94 = (f32[256]{0:T(256)S(1)}, f32[256]{0:T(256)}, u32[]{:S(2)}) copy-start(f32[256]{0:T(256)} %copy-done.92) | copy-start | bytes 3076
  113.3 25.4 %collective-permute-start.4 = (f32[6,16,128]{2,1,0:T(8,128)S(1)}, f32[6,16,128]{2,1,0:T(8,128)S(1)}, u32[]{:S(2)}, u32[]{:S(2)}) collective-permute-start(f32[6,16,128]{2,1,0:T(8,128)S(1)} %get-tuple-element.1193), channel_id=1, source_target_pairs={{1,0},{2,1},{3,2},{4,3},{5,4},{6,5},{7,6},{8,7},{9,8},{10,9},{11,1... | collective-permute-start | bytes 147464 | tf_op jit(solution)/shard_map/ppermute | solution.py:47
  123.2 15.5 %collective-permute-start.5 = (f32[6,16,128]{2,1,0:T(8,128)S(1)}, f32[6,16,128]{2,1,0:T(8,128)S(1)}, u32[]{:S(2)}, u32[]{:S(2)}) collective-permute-start(f32[6,16,128]{2,1,0:T(8,128)S(1)} %get-tuple-element.1194), channel_id=1, source_target_pairs={{0,1},{1,2},{2,3},{3,4},{4,5},{5,6},{6,7},{7,8},{8,9},{9,10},{10,1... | collective-permute-start | bytes 147464 | tf_op jit(solution)/shard_map/ppermute | solution.py:46
  150.4 54.4 %copy-start.72 = (f32[256]{0:T(256)S(1)}, f32[256]{0:T(256)}, u32[]{:S(2)}) copy-start(f32[256]{0:T(256)} %copy-done.71) | copy-start | bytes 3076
  150.7 57.6 %copy-start.48 = (f32[256]{0:T(256)S(1)}, f32[256]{0:T(256)}, u32[]{:S(2)}) copy-start(f32[256]{0:T(256)} %copy-done.47) | copy-start | bytes 3076
  150.9 57.4 %copy-start.95 = (f32[256]{0:T(256)S(1)}, f32[256]{0:T(256)}, u32[]{:S(2)}) copy-start(f32[256]{0:T(256)} %copy-done.92) | copy-start | bytes 3076
  150.9 60.2 %copy-start.75 = (bf16[6,128]{1,0:T(8,128)(2,1)S(1)}, bf16[6,128]{1,0:T(8,128)(2,1)}, u32[]{:S(2)}) copy-start(bf16[6,128]{1,0:T(8,128)(2,1)} %param.60) | copy-start | bytes 4612
  170.9 34.0 %copy-start.59 = (f32[8,256]{1,0:T(8,128)}, f32[8,256]{1,0:T(8,128)S(1)}, u32[]{:S(2)}) copy-start(f32[8,256]{1,0:T(8,128)S(1)} %get-tuple-element.1659) | copy-start | bytes 24580
  170.9 127.5 %reduce-scatter.6.cloned.1.call-start = ((), (), s32[]{:S(2)}) async-start(), calls=%async_computation.4 | async-start | bytes 147456 | tf_op jit(solution)/shard_map/reduce_scatter | solution.py:157
  170.9 21.1 %collective-permute-start.7 = (f32[6,16,128]{2,1,0:T(8,128)S(1)}, f32[6,16,128]{2,1,0:T(8,128)S(1)}, u32[]{:S(2)}, u32[]{:S(2)}) collective-permute-start(f32[6,16,128]{2,1,0:T(8,128)S(1)} %get-tuple-element.1127), channel_id=1, source_target_pairs={{0,31},{1,0},{2,1},{3,2},{4,3},{5,4},{6,5},{7,6},{8,7},{9,8},{10,9... | collective-permute-start | bytes 147464 | tf_op jit(solution)/shard_map/ppermute | solution.py:36
  180.9 11.1 %collective-permute-start.6 = (f32[6,16,128]{2,1,0:T(8,128)S(1)}, f32[6,16,128]{2,1,0:T(8,128)S(1)}, u32[]{:S(2)}, u32[]{:S(2)}) collective-permute-start(f32[6,16,128]{2,1,0:T(8,128)S(1)} %get-tuple-element.1128), channel_id=1, source_target_pairs={{0,1},{1,2},{2,3},{3,4},{4,5},{5,6},{6,7},{7,8},{8,9},{9,10},{10,1... | collective-permute-start | bytes 147464 | tf_op jit(solution)/shard_map/ppermute | solution.py:36
  230.4 30.5 %copy-start.77 = (f32[16,256]{1,0:T(8,128)}, f32[16,256]{1,0:T(8,128)S(1)}, u32[]{:S(2)}) copy-start(f32[16,256]{1,0:T(8,128)S(1)} %pad.471) | copy-start | bytes 49156
  263.5 35.6 %copy-start.33 = (f32[16,256]{1,0:T(8,128)S(1)}, f32[16,256]{1,0:T(8,128)}, u32[]{:S(2)}) copy-start(f32[16,256]{1,0:T(8,128)} %copy-done.32) | copy-start | bytes 49156
  266.8 48.6 %copy-start.96 = (f32[16,256]{1,0:T(8,128)S(1)}, f32[16,256]{1,0:T(8,128)}, u32[]{:S(2)}) copy-start(f32[16,256]{1,0:T(8,128)} %get-tuple-element.1162) | copy-start | bytes 49156
  266.8 48.6 %copy-start.118 = (pred[256]{0:T(512)(128)(4,1)S(1)}, pred[256]{0:T(512)(128)(4,1)}, u32[]{:S(2)}) copy-start(pred[256]{0:T(512)(128)(4,1)} %get-tuple-element.1278) | copy-start | bytes 772
  266.8 48.6 %copy-start.123 = (pred[256]{0:T(512)(128)(4,1)S(1)}, pred[256]{0:T(512)(128)(4,1)}, u32[]{:S(2)}) copy-start(pred[256]{0:T(512)(128)(4,1)} %get-tuple-element.1279) | copy-start | bytes 772
  266.8 49.6 %copy-start.76 = (bf16[6,128]{1,0:T(8,128)(2,1)S(1)}, bf16[6,128]{1,0:T(8,128)(2,1)}, u32[]{:S(2)}) copy-start(bf16[6,128]{1,0:T(8,128)(2,1)} %param.60) | copy-start | bytes 4612
  266.8 211.0 %reduce-scatter.8.cloned.1.call-start = ((), (), s32[]{:S(2)}) async-start(), calls=%async_computation.5 | async-start | bytes 147456 | tf_op jit(solution)/shard_map/reduce_scatter | solution.py:157
  266.9 19.2 %collective-permute-start.9 = (f32[6,16,128]{2,1,0:T(8,128)}, f32[6,16,128]{2,1,0:T(8,128)S(1)}, u32[]{:S(2)}, u32[]{:S(2)}) collective-permute-start(f32[6,16,128]{2,1,0:T(8,128)} %get-tuple-element.1125), channel_id=1, source_target_pairs={{0,31},{1,0},{2,1},{3,2},{4,3},{5,4},{6,5},{7,6},{8,7},{9,8},{10,9... | collective-permute-start | bytes 147464 | tf_op jit(solution)/shard_map/ppermute | solution.py:36
  274.7 11.3 %collective-permute-start.8 = (f32[6,16,128]{2,1,0:T(8,128)}, f32[6,16,128]{2,1,0:T(8,128)S(1)}, u32[]{:S(2)}, u32[]{:S(2)}) collective-permute-start(f32[6,16,128]{2,1,0:T(8,128)} %get-tuple-element.1126), channel_id=1, source_target_pairs={{0,1},{1,2},{2,3},{3,4},{4,5},{5,6},{6,7},{7,8},{8,9},{9,10},{10,1... | collective-permute-start | bytes 147464 | tf_op jit(solution)/shard_map/ppermute | solution.py:36
  334.2 15.3 %copy-start.78 = (f32[16,256]{1,0:T(8,128)}, f32[16,256]{1,0:T(8,128)S(1)}, u32[]{:S(2)}) copy-start(f32[16,256]{1,0:T(8,128)S(1)} %pad.494) | copy-start | bytes 49156
  389.4 277.2 %all-reduce.104.cloned.1.call-start = ((), (), s32[]{:S(2)}) async-start(), calls=%async_computation.6 | async-start | bytes 131072 | tf_op jit(solution)/shard_map/psum | solution.py:239
  394.0 84.6 %copy-start.15 = (f32[6,16,256]{2,1,0:T(8,128)S(1)}, f32[6,16,256]{2,1,0:T(8,128)}, u32[]{:S(2)}) copy-start(f32[6,16,256]{2,1,0:T(8,128)} %copy-done.13) | copy-start | bytes 294916
  394.0 84.6 %copy-start.73 = (f32[256]{0:T(256)S(1)}, f32[256]{0:T(256)}, u32[]{:S(2)}) copy-start(f32[256]{0:T(256)} %copy-done.71) | copy-start | bytes 3076
  394.0 84.6 %copy-start.79 = (f32[16,256]{1,0:T(8,128)S(1)}, f32[16,256]{1,0:T(8,128)}, u32[]{:S(2)}) copy-start(f32[16,256]{1,0:T(8,128)} %copy-done.78) | copy-start | bytes 49156
  394.0 84.6 %copy-start.80 = (f32[16,256]{1,0:T(8,128)S(1)}, f32[16,256]{1,0:T(8,128)}, u32[]{:S(2)}) copy-start(f32[16,256]{1,0:T(8,128)} %pad.495) | copy-start | bytes 49156
  394.0 84.6 %copy-start.110 = (f32[256]{0:T(256)S(1)}, f32[256]{0:T(256)}, u32[]{:S(2)}) copy-start(f32[256]{0:T(256)} %get-tuple-element.904) | copy-start | bytes 3076
  394.0 84.6 %copy-start.12 = (f32[6,16,256]{2,1,0:T(8,128)S(1)}, f32[6,16,256]{2,1,0:T(8,128)}, u32[]{:S(2)}) copy-start(f32[6,16,256]{2,1,0:T(8,128)} %param.57) | copy-start | bytes 294916
  394.1 83.7 %collective-permute-start.10 = (f32[6,16,128]{2,1,0:T(8,128)S(1)}, f32[6,16,128]{2,1,0:T(8,128)S(1)}, u32[]{:S(2)}, u32[]{:S(2)}) collective-permute-start(f32[6,16,128]{2,1,0:T(8,128)S(1)} %copy-done.104), channel_id=1, source_target_pairs={{0,1},{1,2},{2,3},{3,4},{4,5},{5,6},{6,7},{7,8},{8,9},{9,10},{10,1... | collective-permute-start | bytes 147464 | tf_op jit(solution)/shard_map/ppermute | solution.py:36
  395.7 82.1 %collective-permute-start.11 = (f32[6,16,128]{2,1,0:T(8,128)S(1)}, f32[6,16,128]{2,1,0:T(8,128)S(1)}, u32[]{:S(2)}, u32[]{:S(2)}) collective-permute-start(f32[6,16,128]{2,1,0:T(8,128)S(1)} %copy-done.103), channel_id=1, source_target_pairs={{0,31},{1,0},{2,1},{3,2},{4,3},{5,4},{6,5},{7,6},{8,7},{9,8},{10,9... | collective-permute-start | bytes 147464 | tf_op jit(solution)/shard_map/ppermute | solution.py:36
  (106 other events, 383.8 us)
Sparse Core Ops, SparseCore 0:
  171.0 33.0 reduce-scatter.3
  267.0 31.3 reduce-scatter.5
  389.5 30.6 reduce-scatter.7
  427.1 239.4 all-reduce.103
where the time goes:
time: 680 us; the launch traced here: 675 us
  waiting for transfers between devices  232 us (34%)
  blocking collectives  190 us (28%)
  other arithmetic  85.1 us (13%)
  local copies, waits for them, and re-layouts  63.4 us (9%)
  starting transfers between devices  60.1 us (9%)
  matrix products  26.9 us (4%)
  between operations  16.2 us (2%)
    psum x1, waiting for transfers between devices, on_device(): lax.psum((TIME_STEP * (grads_two[0] + grads_one[0] + grads_zero[0]), TIME...  187 us
    psum x1, blocking collectives, on_device(): lax.psum((TIME_STEP * (grads_two[0] + grads_one[0] + grads_zero[0]), TIME...  73.1 us
    all_gather x7, blocking collectives, prefix(): everything = jax.tree.map(lambda part: lax.all_gather(part, axis), shard)  73 us
    all_gather x3, blocking collectives, heating(): lax.all_gather(theta, 'gz', axis=0, tiled=True)  43.7 us
    select_n x48, other arithmetic, step(): return jax.tree.map(lambda a, b: jnp.where(reached, a, b), new, before)  35.2 us
    ppermute x3, starting transfers between devices, padded_2(): after = lax.ppermute(first, axis, down)  32.3 us
    ppermute x6, starting transfers between devices, passed_along(): lax.ppermute(shard, axis, [(i, (i + by) % length) for i in range(length)])  27.5 us
    reduce_scatter x3, waiting for transfers between devices, heating_adjoint(): lax.psum_scatter(lax.dot_general(own_rows, lead_theta, (((0,), (0,)), (()...  24.4 us
  transfers between devices with their start and end apart: 16, of which 5 were waited for; matrix products, arithmetic and copies ran while one was open for 3% of the time, Pallas kernels for 0%

commit v1 on v0

v1 whole, which is shorter than its diff:
```python
import jax
import jax.numpy as jnp
import numpy as np
from jax import lax
from jax.experimental import pallas as pl
from jax.experimental.pallas import tpu as pltpu
from jax.sharding import PartitionSpec as P

NF = 6
LEV = 128
OWN_X = 4
OWN_Y = 8
GZ = 8
GX = 32
DIFFUSION = 0.1
STEP = 0.25
F32 = jnp.float32
BF16 = jnp.bfloat16
HIGHEST = lax.Precision.HIGHEST
CHUNK = 20
PACK = 16


class Patch:
    def __init__(self, ref, x0, nx, y0, ny):
        self.ref, self.x0, self.nx, self.y0, self.ny = ref, x0, nx, y0, ny

    def at(self, x, y):
        start = ((x - self.x0) * self.ny + (y - self.y0)) * 8
        return start if isinstance(start, int) else pl.multiple_of(start, 8)

    def get(self, x, y, n):
        return self.ref[pl.ds(self.at(x, y), n * 8), :].reshape(n, 8, LEV)

    def put(self, x, y, value):
        n = value.shape[0]
        self.ref[pl.ds(self.at(x, y), n * 8), :] = value.reshape(n * 8, LEV)

    def field(self, x, y, n, which):
        return self.ref[pl.ds(self.at(x, y) + which, n, stride=8), :]

    def add_field(self, x, y, which, value):
        n = value.shape[0]
        place = pl.ds(self.at(x, y) + which, n, stride=8)
        self.ref[place, :] = self.ref[place, :] + value


def dot(a, b):
    return lax.dot_general(a, b, (((1,), (0,)), ((), ())), preferred_element_type=F32)


def dot_nt(a, b):
    return lax.dot_general(a, b, (((1,), (1,)), ((), ())), preferred_element_type=F32)


def to_lanes(tiles):
    return jnp.concatenate([tiles[i] for i in range(tiles.shape[0])], axis=1)


def to_tiles(wide):
    count = wide.shape[1] // LEV
    return jnp.concatenate([wide[None, :, i * LEV : (i + 1) * LEV] for i in range(count)], axis=0)


def deriv_x(get):
    return (8.0 * (get(1) - get(-1)) - (get(2) - get(-2))) * (1.0 / 12.0)


def features_of(center, along_x):
    return to_lanes(jnp.concatenate([center, along_x], axis=1).astype(BF16))


def hidden(w, features):
    tanh_one = jnp.tanh(dot(w["in"][...], features))
    hidden_one = tanh_one.astype(BF16)
    tanh_two = jnp.tanh(dot(w["mid"][...], hidden_one))
    return tanh_one, hidden_one, tanh_two, tanh_two.astype(BF16)


def closure_of(w, hidden_two):
    return to_tiles(dot(w["out"][...], hidden_two)[:8, :])


def moved_of(fields, x, y, n, center, along_x):
    y_plus, y_minus = fields.get(x, y + 1, n), fields.get(x, y - 1, n)
    x_sum = fields.get(x + 1, y, n) + fields.get(x - 1, y, n)
    along_y = (y_plus - y_minus) * 0.5
    laplace = x_sum + y_plus + y_minus - 4.0 * center
    return -(center[:, 0:1] * along_x + center[:, 1:2] * along_y) + DIFFUSION * laplace


def forward_tiles(w, fields, x, y, n):
    center = fields.get(x, y, n)
    along_x = deriv_x(lambda k: fields.get(x + k, y, n))
    total = moved_of(fields, x, y, n, center, along_x)
    parts = []
    for lo in range(0, n, 8):
        hi = min(n, lo + 8)
        features = features_of(center[lo:hi], along_x[lo:hi])
        parts.append(closure_of(w, hidden(w, features)[3]))
    return center, total + (jnp.concatenate(parts, axis=0) if len(parts) > 1 else parts[0])


def shifted(value, by):
    lane = lax.broadcasted_iota(jnp.int32, value.shape, 1)
    if by > 0:
        return jnp.where(lane >= by, pltpu.roll(value, by, 1), 0.0)
    return jnp.where(lane < LEV + by, pltpu.roll(value, LEV + by, 1), 0.0)


def settle(source, fall_rate, sign):
    fresh = 1.0 / (1.0 + fall_rate)
    factor = fall_rate * fresh
    value = fresh * source
    step = 1
    while step < LEV:
        value = value + factor * shifted(value, sign * step)
        factor = factor * factor
        step *= 2
    return value


def column_terms(patch, xs, y, n, fall, live, radiation, packs, adjoint):
    p_theta, p_rain, p_fall, p_live = packs
    for i, x in enumerate(xs):
        rows = pl.ds(i * PACK, n)
        p_theta[rows, :] = patch.field(x, y, n, 3)
        p_rain[rows, :] = patch.field(x, y, n, 5)
        source = pl.ds((x + 4) * 18 + y + 5, n)
        p_fall[rows, :] = fall[source, :]
        p_live[rows, :] = live[source, :]
    size = len(xs) * PACK
    theta, rain = p_theta[0:size, :], p_rain[0:size, :]
    fall_rate, mask = p_fall[0:size, :], p_live[0:size, :]
    contract = ((1,), (0,)) if adjoint else ((1,), (1,))
    p_theta[0:size, :] = lax.dot_general(
        theta, radiation[...], (contract, ((), ())), precision=HIGHEST, preferred_element_type=F32
    )
    if adjoint:
        masked = mask * rain
        p_rain[0:size, :] = settle(masked, fall_rate, 1) - masked
    else:
        p_rain[0:size, :] = mask * (settle(rain, fall_rate, -1) - rain)


def add_columns(patch, xs, y, n, packs, gain):
    for i, x in enumerate(xs):
        patch.add_field(x, y, 3, gain * packs[0][pl.ds(i * PACK, n), :])
        patch.add_field(x, y, 5, gain * packs[1][pl.ds(i * PACK, n), :])


def backward_tiles(w, fields, lead, x, spans, spread, direct, sums, emit):
    centers = [fields.get(x, y, n) for y, n in spans]
    slopes = [deriv_x(lambda k, y=y, n=n: fields.get(x + k, y, n)) for y, n in spans]
    leads = [lead.get(x, y, n) for y, n in spans]
    center = jnp.concatenate(centers, axis=0) if len(spans) > 1 else centers[0]
    along_x = jnp.concatenate(slopes, axis=0) if len(spans) > 1 else slopes[0]
    lam = jnp.concatenate(leads, axis=0) if len(spans) > 1 else leads[0]
    features = features_of(center, along_x)
    out_cot = to_lanes(jnp.concatenate([lam, jnp.zeros_like(lam)], axis=1).astype(BF16))
    tanh_one, hidden_one, tanh_two, hidden_two = hidden(w, features)
    pre_two = (dot(w["out_t"][...], out_cot) * (1.0 - tanh_two * tanh_two)).astype(BF16)
    pre_one = (dot(w["mid_t"][...], pre_two) * (1.0 - tanh_one * tanh_one)).astype(BF16)
    feature_cot = dot(w["in_t"][...], pre_one)
    if sums is not None:
        sums[0:128, :] += dot_nt(pre_two, hidden_one)
        sums[128:144, :] += dot_nt(features, pre_one)
        sums[144:160, :] += dot_nt(out_cot, hidden_two)
    own = to_tiles(feature_cot[0:8, :])
    other = center[:, 0:1] * lam - to_tiles(feature_cot[8:16, :])
    first = 0
    for y, n in spans:
        spread.put(x, y, other[first : first + n])
        direct.put(x, y, own[first : first + n])
        first += n
    if emit is not None:
        emit(x, center, along_x, hidden_two)


def closure_backward(w, fields, lead, x_lo, x_hi, y_lo, y_hi, spread, direct, sums, emit=None):
    whole = [(y_lo, y_hi - y_lo)]
    rim = [(y, n) for y, n in ((y_lo, -y_lo), (OWN_Y, y_hi - OWN_Y)) if n > 0]

    def own_x(x, carry):
        backward_tiles(w, fields, lead, x, [(0, OWN_Y)], spread, direct, sums, emit)
        if rim:
            backward_tiles(w, fields, lead, x, rim, spread, direct, None, None)
        return carry

    def rim_x(i, carry):
        x = x_lo - 2 + i + jnp.where(i < 2 - x_lo, 0, OWN_X)
        backward_tiles(w, fields, lead, x, whole, spread, direct, None, None)
        return carry

    lax.fori_loop(0, OWN_X, own_x, 0)
    lax.fori_loop(0, x_hi - x_lo + 4 - OWN_X, rim_x, 0)


def adjoint_tiles(fields, lead, x, y, n, spread, direct):
    lam = lead.get(x, y, n)
    up, down = lead.get(x, y + 1, n), lead.get(x, y - 1, n)
    s_up, s_down = fields.get(x, y + 1, n), fields.get(x, y - 1, n)
    laplace = lead.get(x + 1, y, n) + lead.get(x - 1, y, n) + up + down - 4.0 * lam
    result = deriv_x(lambda k: spread.get(x + k, y, n)) + direct.get(x, y, n) + DIFFUSION * laplace
    result = result + 0.5 * (s_up[:, 1:2] * up - s_down[:, 1:2] * down)
    along_x = deriv_x(lambda k: fields.get(x + k, y, n))
    along_y = (s_up - s_down) * 0.5
    to_u = jnp.sum(lam * along_x, axis=1, keepdims=True)
    to_v = jnp.sum(lam * along_y, axis=1, keepdims=True)
    row = lax.broadcasted_iota(jnp.int32, lam.shape, 1)
    return lam, result - jnp.where(row == 0, to_u, 0.0) - jnp.where(row == 1, to_v, 0.0)


def weights_of(bundle):
    return {
        "mid": bundle.at[0:128, :],
        "mid_t": bundle.at[128:256, :],
        "in_t": bundle.at[256:272, :],
        "out": bundle.at[272:288, :],
    }


def split_three(value):
    high = value.astype(BF16)
    rest = value - high.astype(F32)
    middle = rest.astype(BF16)
    return high, middle, (rest - middle.astype(F32)).astype(BF16)


def pick(value, chosen):
    high, middle, low = split_three(value)
    return dot(high, chosen) + dot(middle, chosen) + dot(low, chosen)


def first_table():
    table = np.zeros((GZ, LEV), np.int32)
    for block in range(GZ):
        for x in range(OWN_X):
            for y in range(18):
                table[block, x * 18 + y] = x * 64 + (8 * block - 5 + y) % 64
            for y in range(14):
                table[block, 72 + x * 14 + y] = 256 + x * 64 + (8 * block - 3 + y) % 64
    return table


def pack_kernel(table, state, cot, fall, live, out, left):
    left[0:96, 0:256] = state[...].reshape(96, 256)
    left[0:96, 256:512] = cot[...].reshape(96, 256)
    left[96:104, :] = jnp.zeros((8, 512), F32)
    left[96:97, 0:256] = fall[...]
    left[97:98, 0:256] = live[...].astype(F32)
    parts = split_three(left[...])
    place = lax.broadcasted_iota(jnp.int32, (512, LEV), 0)
    for block in range(GZ):
        chosen = jnp.where(place == table[block : block + 1, :], 1.0, 0.0).astype(BF16)
        out[block] = dot(parts[0], chosen) + dot(parts[1], chosen) + dot(parts[2], chosen)


def turn_kernel(got, to_next, to_prev):
    for which in range(NF):
        blocks = [got[k, which * 16 : which * 16 + 16, :] for k in range(GZ)]
        turned = jnp.concatenate(blocks, axis=0).T
        to_next[which * 72 : which * 72 + 72, :] = turned[0:72]
        to_prev[which * 72 : which * 72 + 72, :] = turned[0:72]
        to_next[432 + which * 28 : 460 + which * 28, :] = turned[100:128]
        to_prev[432 + which * 28 : 460 + which * 28, :] = turned[72:100]
    to_next[600:608, :] = got[0, 96:104, :]
    to_prev[600:608, :] = got[0, 96:104, :]


def forward_kernel(
    own, own_prev, before, after, bundle, w_in, w_out_t, radiation,
    state, cot, fall, live, one, to_next, to_prev,
    two, p_theta, p_rain, p_fall, p_live,
):
    w = weights_of(bundle) | {"in": w_in, "out_t": w_out_t}
    packs = (p_theta, p_rain, p_fall, p_live)
    state[...] = jnp.zeros(state.shape, F32)
    cot[...] = jnp.zeros(cot.shape, F32)
    for place, source in enumerate((before, own, after)):
        for which in range(NF):
            columns = source[which * 72 : which * 72 + 72, :]
            state[pl.ds(place * 576 + which, 72, stride=8), :] = columns
        rows = pl.ds(place * 72, 72)
        fall[rows, :] = jnp.broadcast_to(source[600:601, :], (LEV, LEV)).T[0:72]
        live[rows, :] = jnp.broadcast_to(source[601:602, :], (LEV, LEV)).T[0:72]
    for place, source in enumerate((before, own_prev, own, after)):
        for which in range(NF):
            columns = source[432 + which * 28 : 460 + which * 28, :]
            cot[pl.ds(place * 224 + which, 28, stride=8), :] = columns
    s_zero = Patch(state, -4, 12, -5, 18)
    s_one = Patch(one, -2, 8, -4, 16)
    s_two = Patch(two, 0, 4, -3, 14)

    def stage_one(i, carry):
        x = i - 2
        center, total = forward_tiles(w, s_zero, x, -4, 16)
        s_one.put(x, -4, center + STEP * total)
        return carry

    lax.fori_loop(0, 8, stage_one, 0)
    xs = range(-2, 6)
    column_terms(s_zero, xs, -4, 16, fall, live, radiation, packs, False)
    add_columns(s_one, xs, -4, 16, packs, STEP)

    def stage_two(x, carry):
        center, total = forward_tiles(w, s_one, x, -3, 14)
        s_two.put(x, -3, 0.75 * s_zero.get(x, -3, 14) + 0.25 * (center + STEP * total))
        return carry

    lax.fori_loop(0, 4, stage_two, 0)
    xs = range(4)
    column_terms(s_one, xs, -3, 14, fall, live, radiation, packs, False)
    add_columns(s_two, xs, -3, 14, packs, 0.25 * STEP)
    for which in range(NF):
        columns = two[pl.ds(which, 56, stride=8), :]
        to_next[which * 56 : which * 56 + 56, :] = columns
        to_prev[which * 56 : which * 56 + 56, :] = columns
        for i in range(4):
            rows = pl.ds(336 + which * 48 + i * 12, 12)
            to_next[rows, :] = s_one.field(i - 2, -2, 12, which)
            to_prev[rows, :] = s_one.field(i + 2, -2, 12, which)


def middle_kernel(
    own, before, after, bundle, w_in, w_out_t, radiation, state, cot, fall, live,
    cot_two, to_both, new_state, sums,
    two, lead, spread, direct, p_theta, p_rain, p_fall, p_live,
):
    w = weights_of(bundle) | {"in": w_in, "out_t": w_out_t}
    packs = (p_theta, p_rain, p_fall, p_live)
    two[...] = jnp.zeros(two.shape, F32)
    for place, source in enumerate((before, own, after)):
        for which in range(NF):
            columns = source[which * 56 : which * 56 + 56, :]
            two[pl.ds(place * 448 + which, 56, stride=8), :] = columns
    lead[...] = (2.0 / 3.0) * cot[...]
    sums[...] = jnp.zeros(sums.shape, F32)
    s_zero = Patch(state, -4, 12, -5, 18)
    s_two = Patch(two, -4, 12, -3, 14)
    lam = Patch(lead, -2, 8, -3, 14)
    spread_at, direct_at = Patch(spread, -2, 8, -2, 12), Patch(direct, -2, 8, -2, 12)
    c_two = Patch(cot_two, 0, 4, -2, 12)
    new = Patch(new_state, 0, 4, 0, 8)

    def emit(x, center, along_x, hidden_two):
        total = moved_of(s_two, x, 0, OWN_Y, center, along_x) + closure_of(w, hidden_two)
        old = s_zero.get(x, 0, OWN_Y)
        new.put(x, 0, old * (1.0 / 3.0) + (2.0 / 3.0) * (center + STEP * total))

    closure_backward(w, s_two, lam, 0, 4, -2, 10, spread_at, direct_at, sums, emit)
    xs = range(4)
    column_terms(s_two, xs, 0, 8, fall, live, radiation, packs, False)
    add_columns(new, xs, 0, 8, packs, (2.0 / 3.0) * STEP)

    def gather(x, carry):
        center, result = adjoint_tiles(s_two, lam, x, -2, 12, spread_at, direct_at)
        c_two.put(x, -2, center + STEP * result)
        return carry

    lax.fori_loop(0, 4, gather, 0)
    column_terms(lam, xs, -2, 12, fall, live, radiation, packs, True)
    add_columns(c_two, xs, -2, 12, packs, STEP)
    for which in range(NF):
        to_both[which * 48 : which * 48 + 48, :] = cot_two[pl.ds(which, 48, stride=8), :]


def last_kernel(
    own, before, after, one, one_before, one_after, bundle, w_in, w_out_t, radiation,
    state, cot, fall, live, new_state, sums_two,
    out,
    wide, lead, c_one, spread, direct, spread_zero, direct_zero, grad, sums,
    p_theta, p_rain, p_fall, p_live,
):
    w = weights_of(bundle) | {"in": w_in, "out_t": w_out_t}
    packs = (p_theta, p_rain, p_fall, p_live)
    wide[...] = jnp.zeros(wide.shape, F32)
    lead[...] = jnp.zeros(lead.shape, F32)
    for which in range(NF):
        rows = slice(336 + which * 48, 384 + which * 48)
        wide[pl.ds(which, 48, stride=8), :] = one_before[rows, :]
        wide[pl.ds(1152 + which, 48, stride=8), :] = one_after[rows, :]
        rows = slice(which * 48, which * 48 + 48)
        lead[pl.ds(which, 48, stride=8), :] = 0.25 * before[rows, :]
        lead[pl.ds(768 + which, 48, stride=8), :] = 0.25 * after[rows, :]
    s_own = Patch(one, -2, 8, -4, 16)
    for i in range(8):
        wide[pl.ds((i + 4) * 96, 96), :] = one[pl.ds(s_own.at(i - 2, -2), 96), :]
    lead[384:768, :] = 0.25 * own[...]
    sums[...] = sums_two[...]
    s_zero = Patch(state, -4, 12, -5, 18)
    s_one = Patch(wide, -6, 16, -2, 12)
    lam_one = Patch(lead, -4, 12, -2, 12)
    lam_zero = Patch(c_one, -2, 8, -1, 10)
    spread_at, direct_at = Patch(spread, -4, 12, -1, 10), Patch(direct, -4, 12, -1, 10)
    closure_backward(w, s_one, lam_one, -2, 6, -1, 9, spread_at, direct_at, sums)

    def gather_one(i, carry):
        x = i - 2
        center, result = adjoint_tiles(s_one, lam_one, x, -1, 10, spread_at, direct_at)
        lam_zero.put(x, -1, center + STEP * result)
        return carry

    lax.fori_loop(0, 8, gather_one, 0)
    xs = range(-2, 6)
    column_terms(lam_one, xs, -1, 10, fall, live, radiation, packs, True)
    add_columns(lam_zero, xs, -1, 10, packs, STEP)

    spread_z, direct_z = Patch(spread_zero, -2, 8, 0, 8), Patch(direct_zero, -2, 8, 0, 8)
    closure_backward(w, s_zero, lam_zero, 0, 4, 0, 8, spread_z, direct_z, sums)
    c_zero, c_two = Patch(cot, -2, 8, -3, 14), Patch(own, 0, 4, -2, 12)
    final = Patch(grad, 0, 4, 0, 8)

    def gather_zero(x, carry):
        center, result = adjoint_tiles(s_zero, lam_zero, x, 0, 8, spread_z, direct_z)
        known = c_zero.get(x, 0, 8) * (1.0 / 3.0) + 0.75 * c_two.get(x, 0, 8)
        final.put(x, 0, known + center + STEP * result)
        return carry

    lax.fori_loop(0, 4, gather_zero, 0)
    xs = range(4)
    column_terms(lam_zero, xs, 0, 8, fall, live, radiation, packs, True)
    add_columns(final, xs, 0, 8, packs, STEP)
    for pair in range(3):
        rows = []
        for source in (new_state, grad):
            for which in (2 * pair, 2 * pair + 1):
                rows.append(source[pl.ds(which, 32, stride=8), :])
        turned = jnp.concatenate(rows, axis=0).T
        for block in range(GZ):
            out[block, pair * 16 : pair * 16 + 16, :] = turned[block * 16 : block * 16 + 16]
    for block in range(GZ):
        out[block, 48:68, :] = STEP * sums[block * CHUNK : (block + 1) * CHUNK, :]


def last_table():
    chosen = np.zeros((256, 256), np.float32)
    for block in range(GZ):
        for x in range(OWN_X):
            for y in range(OWN_Y):
                chosen[block * 32 + x * 8 + y, x * 64 + block * 8 + y] = 1.0
    return chosen


def unpack_kernel(got, chosen, new_state, grad, chunk):
    total = got[0, 48:68, :]
    for block in range(1, GZ):
        total = total + got[block, 48:68, :]
    chunk[...] = total
    for index, out in enumerate((new_state, grad)):
        for half in range(2):
            lanes = slice((2 * index + half) * 32, (2 * index + half + 1) * 32)
            row = jnp.concatenate([got[k, 0:48, lanes] for k in range(GZ)], axis=1)
            placed = pick(row, chosen[...])
            for pair in range(3):
                out[2 * pair + half] = placed[pair * 16 : pair * 16 + 16]


def call(kernel, outs, scratch, *operands):
    vmem = pl.BlockSpec(memory_space=pltpu.VMEM)
    return pl.pallas_call(
        kernel,
        out_shape=[jax.ShapeDtypeStruct(shape, F32) for shape in outs],
        in_specs=[vmem] * len(operands),
        out_specs=[vmem] * len(outs),
        scratch_shapes=[pltpu.VMEM(shape, F32) for shape in scratch],
        compiler_params=pltpu.CompilerParams(vmem_limit_bytes=48 << 20),
    )(*operands)


def passed_along(shard, by):
    return lax.ppermute(shard, "gx", [(i, (i + by) % GX) for i in range(GX)])


def on_device(state, state_cot, w_in, w_mid, w_out, radiation, fall_rate, active):
    packs = [(8 * PACK, LEV)] * 4
    in_wide = jnp.concatenate(
        [jnp.pad(w_in[:, :NF], ((0, 0), (0, 2))), jnp.pad(w_in[:, NF:], ((0, 0), (0, 2)))], axis=1
    )
    out_wide = jnp.pad(w_out, ((0, 10), (0, 0)))
    bundle = jnp.concatenate([w_mid, w_mid.T, in_wide.T, out_wide], axis=0)
    weights = (bundle, in_wide, out_wide.T, radiation)

    (packed,) = call(
        pack_kernel,
        [(GZ, 104, LEV)],
        [(104, 512)],
        jnp.asarray(first_table()),
        state,
        state_cot,
        fall_rate.reshape(1, 256),
        active.reshape(1, 256),
    )
    got = lax.all_to_all(packed, "gz", 0, 0)
    own, own_prev = call(turn_kernel, [(608, LEV), (608, LEV)], [], got)
    before, after = passed_along(own, 1), passed_along(own_prev, -1)
    zero, cot, fall, live, one, to_next, to_prev = call(
        forward_kernel,
        [(1728, LEV), (896, LEV), (216, LEV), (216, LEV), (1024, LEV), (624, LEV), (624, LEV)],
        [(448, LEV)] + packs,
        own,
        own_prev,
        before,
        after,
        *weights,
    )
    one_before, one_after = passed_along(to_next, 1), passed_along(to_prev, -1)
    cot_two, to_both, new_state, sums = call(
        middle_kernel,
        [(384, LEV), (288, LEV), (256, LEV), (GZ * CHUNK, LEV)],
        [(1344, LEV), (896, LEV), (768, LEV), (768, LEV)] + packs,
        to_next,
        one_before,
        one_after,
        *weights,
        zero,
        cot,
        fall,
        live,
    )
    two_before, two_after = passed_along(to_both, 1), passed_along(to_both, -1)
    (sent,) = call(
        last_kernel,
        [(GZ, 68, LEV)],
        [(1536, LEV), (1152, LEV), (640, LEV), (960, LEV), (960, LEV), (512, LEV), (512, LEV)]
        + [(256, LEV), (GZ * CHUNK, LEV)]
        + packs,
        cot_two,
        two_before,
        two_after,
        one,
        one_before,
        one_after,
        *weights,
        zero,
        cot,
        fall,
        live,
        new_state,
        sums,
    )
    got = lax.all_to_all(sent, "gz", 0, 0)
    new_state, grad_state, chunk = call(
        unpack_kernel,
        [(NF, 16, 256), (NF, 16, 256), (CHUNK, LEV)],
        [],
        got,
        jnp.asarray(last_table(), BF16),
    )
    spread = lax.all_to_all(jnp.broadcast_to(chunk, (GX, CHUNK, LEV)), "gx", 0, 0)
    added = jnp.sum(spread, axis=0)
    totals = lax.all_to_all(jnp.broadcast_to(added, (GZ, CHUNK, LEV)), "gz", 0, 0)
    totals = totals.reshape(GZ * CHUNK, LEV)
    grad_in = totals[128:144].T
    grad_in = jnp.concatenate([grad_in[:, 0:NF], grad_in[:, 8 : 8 + NF]], axis=1)
    return (new_state, grad_state, grad_in, totals[0:128], totals[144:150])


def solution(mesh):
    placed = (P(None, "gz", "gx"), P(None, "gz", "gx"), P(), P(), P(), P(), P("gx"), P("gx"))
    return jax.shard_map(
        on_device,
        mesh=mesh,
        in_specs=placed,
        out_specs=(P(None, "gz", "gx"), P(None, "gz", "gx"), P(), P(), P()),
        check_vma=False,
    )
```

time: 680 us -> 180 us (0.26)
  waiting for transfers between devices: 232 us -> 50.7 us
  blocking collectives: 190 us -> 45.2 us
  other arithmetic: 85.1 us -> 0.74 us
  local copies, waits for them, and re-layouts: 63.4 us -> 5.98 us
  Pallas kernels: 0 us -> 46.9 us
  starting transfers between devices: 60.1 us -> 28.8 us
  matrix products: 26.9 us -> 0 us
  between operations: 16.2 us -> 0.75 us
    psum x1 -> x0, waiting for transfers between devices: 187 us -> none  [on_device(): lax.psum((TIME_STEP * (grads_two[0] + grads_one[0] + grads_zero[0]), TIME...]
    all_gather x10 -> x0, blocking collectives: 117 us -> none  [the longest x7 73 us: prefix(): everything = jax.tree.map(lambda part: lax.all_gather(part, axis), shard)]
    psum x1 -> x0, blocking collectives: 73.1 us -> none  [on_device(): lax.psum((TIME_STEP * (grads_two[0] + grads_one[0] + grads_zero[0]), TIME...]
    pallas_call x0 -> x6, Pallas kernels: none -> 46.9 us  [call(): pl.pallas_call(kernel, out_shape=[jax.ShapeDtypeStruct(shape, F32) for sh...]
    all_to_all x0 -> x3, blocking collectives: none -> 45.2 us  [the longest x1 17.6 us: on_device(): lax.all_to_all(jnp.broadcast_to(chunk, (GX, CHUNK, LEV)), 'gx', 0, 0)]
    ppermute x12 -> x6, starting transfers between devices: 59.9 us -> 21.3 us  [passed_along(): return lax.ppermute(shard, 'gx', [(i, (i + by) % GX) for i in range(GX)])]
    select_n x49 -> x0, other arithmetic: 35.3 us -> none  [the longest x48 35.2 us: step(): return jax.tree.map(lambda a, b: jnp.where(reached, a, b), new, before)]
    dot_general x33 -> x0, matrix products: 26.9 us -> none  [the longest x18 18.9 us: contract(): lax.dot_general(left, right, (((left_dim,), (right_dim,)), ((), ())), pre...]
  transfers between devices with their start and end apart: 16 -> 7, of which waited for: 5 -> 6; matrix products, arithmetic and copies ran while one was open for 3% -> 0% of each run, Pallas kernels for 0% -> 0%
where the time goes in v1:
time: 180 us; the launch traced here: 179 us
  waiting for transfers between devices  50.7 us (28%)
  Pallas kernels  46.9 us (26%)
  blocking collectives  45.2 us (25%)
  starting transfers between devices  28.8 us (16%)
  local copies, waits for them, and re-layouts  5.98 us (3%)
    pallas_call x6, Pallas kernels, call(): pl.pallas_call(kernel, out_shape=[jax.ShapeDtypeStruct(shape, F32) for sh...  46.9 us
    ppermute x6, waiting for transfers between devices, passed_along(): return lax.ppermute(shard, 'gx', [(i, (i + by) % GX) for i in range(GX)])  39 us
    ppermute x6, starting transfers between devices, passed_along(): return lax.ppermute(shard, 'gx', [(i, (i + by) % GX) for i in range(GX)])  21.3 us
    all_to_all x1, blocking collectives, on_device(): lax.all_to_all(jnp.broadcast_to(chunk, (GX, CHUNK, LEV)), 'gx', 0, 0)  17.6 us
    all_to_all x1, blocking collectives, on_device(): got = lax.all_to_all(sent, 'gz', 0, 0)  16 us
    all_to_all x1, waiting for transfers between devices, on_device(): got = lax.all_to_all(packed, 'gz', 0, 0)  11.7 us
    all_to_all x1, blocking collectives, on_device(): lax.all_to_all(jnp.broadcast_to(added, (GZ, CHUNK, LEV)), 'gz', 0, 0)  11.6 us
    all_to_all x1, starting transfers between devices, on_device(): got = lax.all_to_all(packed, 'gz', 0, 0)  7.53 us
  transfers between devices with their start and end apart: 7, of which 6 were waited for; matrix products, arithmetic and copies ran while one was open for 0% of the time, Pallas kernels for 0%

profile of v1, /device:TPU:1, one launch (start us, length us, event | category | flops | bytes accessed | tf_op | source)
XLA Modules:
  0.0 179.1 jit_solution(972728303020365586)
XLA Ops:
  0.6 0.0 copy-start.4
  0.6 0.0 copy-start.6
  0.7 0.0 copy-start.5
  0.7 0.7 copy-done.4
  1.3 0.0 copy-done.6
  1.3 0.0 copy-done.5
  1.3 0.0 copy-start.2
  1.3 0.9 copy-done.2
  2.2 0.9 copy-done.3
  3.1 1.7 shard_map.137
  4.8 7.5 %all-to-all-start = ((f32[8,104,128]{2,1,0:T(8,128)}), f32[8,104,128]{2,1,0:T(8,128)S(1)}, u32[]{:S(2)}, u32[]{:S(2)}) async-start(f32[8,104,128]{2,1,0:T(8,128)} %shard_map.137), calls=%async_computation | async-start | bytes 851968 | tf_op jit(solution)/shard_map/all_to_all | solution.py:494
  12.3 0.0 copy-done.8
  12.4 0.6 copy-done.10
  13.0 0.1 slice_select_fusion
  13.1 11.7 %all-to-all-done.got = f32[8,104,128]{2,1,0:T(8,128)S(1)} async-done(((f32[8,104,128]{2,1,0:T(8,128)}), f32[8,104,128]{2,1,0:T(8,128)S(1)}, u32[]{:S(2)}, u32[]{:S(2)}) %all-to-all-start) | async-done | bytes 426016 | tf_op jit(solution)/shard_map/all_to_all | solution.py:494
  24.7 0.2 shard_map.138
  24.9 1.4 collective-permute-start
  26.3 8.3 %collective-permute-start.1 = (f32[608,128]{1,0:T(8,128)S(1)}, f32[608,128]{1,0:T(8,128)S(1)}, u32[]{:S(2)}, u32[]{:S(2)}) collective-permute-start(f32[608,128]{1,0:T(8,128)S(1)} %get-tuple-element.22.own_prev), channel_id=1, source_target_pairs={{0,31},{1,0},{2,1},{3,2},{4,3},{5,4},{6,5},{7,6},{8,7},{9,8},{10,9... | collective-permute-start | bytes 933896 | tf_op jit(solution)/shard_map/ppermute | solution.py:472
  34.6 0.1 copy.42.w_in
  34.7 0.6 copy-done.9
  35.3 0.1 copy.40
  35.4 0.1 copy.47
  35.5 0.5 copy-done.7
  36.0 0.1 copy.39
  36.2 0.0 copy-start
  36.2 11.6 %collective-permute-done.before = f32[608,128]{1,0:T(8,128)S(1)} collective-permute-done((f32[608,128]{1,0:T(8,128)S(1)}, f32[608,128]{1,0:T(8,128)S(1)}, u32[]{:S(2)}, u32[]{:S(2)}) %collective-permute-start) | collective-permute-done | bytes 311328 | tf_op jit(solution)/shard_map/ppermute | solution.py:472
  47.8 0.0 collective-permute-done.1.after
  47.8 0.0 copy-done
  47.8 12.0 %shard_map.139 = (f32[1728,128]{1,0:T(8,128)S(1)}, f32[896,128]{1,0:T(8,128)S(1)}, f32[216,128]{1,0:T(8,128)S(1)}, f32[216,128]{1,0:T(8,128)S(1)}, f32[1024,128]...) custom-call(f32[608,128]{1,0:T(8,128)S(1)} %get-tuple-element.21.own, ...), custom_call_target="tpu_custom_call" | custom-call | tf_op jit(solution)/shard_map/pallas_call | solution.py:461
  59.9 10.1 %collective-permute-start.3 = (f32[624,128]{1,0:T(8,128)S(1)}, f32[624,128]{1,0:T(8,128)S(1)}, u32[]{:S(2)}, u32[]{:S(2)}) collective-permute-start(f32[624,128]{1,0:T(8,128)S(1)} %get-tuple-element.24), channel_id=1, source_target_pairs={{0,31},{1,0},{2,1},{3,2},{4,3},{5,4},{6,5},{7,6},{8,7},{9,8},{10,9... | collective-permute-start | bytes 958472 | tf_op jit(solution)/shard_map/ppermute | solution.py:472
  69.9 0.0 collective-permute-start.2
  69.9 6.4 %collective-permute-done.3.after.one_after = f32[624,128]{1,0:T(8,128)S(1)} collective-permute-done((f32[624,128]{1,0:T(8,128)S(1)}, f32[624,128]{1,0:T(8,128)S(1)}, u32[]{:S(2)}, u32[]{:S(2)}) %collective-permute-start.3) | collective-permute-done | bytes 319520 | tf_op jit(solution)/shard_map/ppermute | solution.py:472
  76.3 10.0 %collective-permute-done.2.before.one_before = f32[624,128]{1,0:T(8,128)S(1)} collective-permute-done((f32[624,128]{1,0:T(8,128)S(1)}, f32[624,128]{1,0:T(8,128)S(1)}, u32[]{:S(2)}, u32[]{:S(2)}) %collective-permute-start.2) | collective-permute-done | bytes 319520 | tf_op jit(solution)/shard_map/ppermute | solution.py:472
  86.3 11.0 %shard_map.140 = (f32[384,128]{1,0:T(8,128)S(1)}, f32[288,128]{1,0:T(8,128)S(1)}, f32[256,128]{1,0:T(8,128)S(1)}, f32[160,128]{1,0:T(8,128)S(1)}) custom-call(f32[624,128]{1,0:T(8,128)S(1)} %get-tuple-element.23.own, f32[624,128]{1,0:T(8,128)S(1)} %collective-permute-done.2.before.one_before, f32[624,128]{1,0:T(8,128)S(1)} %collective-permute-done.3.after.one_after, ...), custom_call_target="tpu_custom_call" | custom-call | tf_op jit(solution)/shard_map/pallas_call | solution.py:461
  97.4 0.4 collective-permute-start.5
  97.8 1.1 collective-permute-start.4
  98.9 2.5 %collective-permute-done.5.after = f32[288,128]{1,0:T(8,128)S(1)} collective-permute-done((f32[288,128]{1,0:T(8,128)S(1)}, f32[288,128]{1,0:T(8,128)S(1)}, u32[]{:S(2)}, u32[]{:S(2)}) %collective-permute-start.5) | collective-permute-done | bytes 147488 | tf_op jit(solution)/shard_map/ppermute | solution.py:472
  101.4 8.4 %collective-permute-done.4.before = f32[288,128]{1,0:T(8,128)S(1)} collective-permute-done((f32[288,128]{1,0:T(8,128)S(1)}, f32[288,128]{1,0:T(8,128)S(1)}, u32[]{:S(2)}, u32[]{:S(2)}) %collective-permute-start.4) | collective-permute-done | bytes 147488 | tf_op jit(solution)/shard_map/ppermute | solution.py:472
  109.9 20.9 %shard_map.141 = f32[8,68,128]{2,1,0:T(8,128)S(1)} custom-call(f32[384,128]{1,0:T(8,128)S(1)} %get-tuple-element.29.own, f32[288,128]{1,0:T(8,128)S(1)} %collective-permute-done.4.before, f32[288,128]{1,0:T(8,128)S(1)} %collective-permute-done.5.after, f32[1024,128]{1,0:T(8,128)S(1)} %get-tuple-element.31.one, ...), custom_call_target="tpu_custom_call" | custom-call | tf_op jit(solution)/shard_map/pallas_call | solution.py:461
  130.8 0.0 copy-start.1
  130.8 16.0 %all_to_all.20.got = f32[8,68,128]{2,1,0:T(8,128)S(1)} all-to-all(f32[8,68,128]{2,1,0:T(8,128)S(1)} %shard_map.141), channel_id=1, replica_groups=mesh['gz'=8,'gx'=32] {'gz'}, dimensions={0} | all-to-all | bytes 557056 | tf_op jit(solution)/shard_map/all_to_all | solution.py:542
  146.8 0.0 copy-done.1
  146.8 1.1 shard_map.142
  147.9 17.6 %all_to_all.21 = f32[32,20,128]{2,1,0:T(8,128)S(1)} all-to-all(f32[32,20,128]{2,1,0:T(8,128)S(1)} %broadcast_in_dim.6), channel_id=1, replica_groups=mesh['gz'=8,'gx'=32] {'gx'}, dimensions={0} | all-to-all | bytes 655360 | tf_op jit(solution)/shard_map/all_to_all | solution.py:550
  165.6 11.6 %all_to_all.22 = f32[8,20,128]{2,1,0:T(8,128)S(1)} all-to-all(f32[8,20,128]{2,1,0:T(8,128)S(1)} %broadcast_in_dim.7), channel_id=1, replica_groups=mesh['gz'=8,'gx'=32] {'gz'}, dimensions={0} | all-to-all | bytes 163840 | tf_op jit(solution)/shard_map/all_to_all | solution.py:552
  177.2 0.6 slice.33
  177.8 0.6 slice.32
  178.4 0.6 pad_maximum_fusion.1
  (16 shorter events, 0.1 us)
Async XLA Ops:
  0.6 0.7 copy-start.4
  0.6 0.7 copy-start.6
  0.7 0.7 copy-start.5
  1.3 0.9 copy-start.2
  2.2 0.9 copy-start.3
  4.8 7.5 %copy-start.8 = (bf16[128,12]{0,1:T(8,128)(2,1)S(1)}, bf16[128,12]{0,1:T(8,128)(2,1)}, u32[]{:S(2)}) copy-start(bf16[128,12]{0,1:T(8,128)(2,1)} %param.12) | copy-start | bytes 9220
  4.8 19.9 %all-to-all-start = ((f32[8,104,128]{2,1,0:T(8,128)}), f32[8,104,128]{2,1,0:T(8,128)S(1)}, u32[]{:S(2)}, u32[]{:S(2)}) async-start(f32[8,104,128]{2,1,0:T(8,128)} %shard_map.137), calls=%async_computation | async-start | bytes 851968 | tf_op jit(solution)/shard_map/all_to_all | solution.py:494
  12.4 0.7 copy-start.10
  24.9 22.9 %collective-permute-start = (f32[608,128]{1,0:T(8,128)S(1)}, f32[608,128]{1,0:T(8,128)S(1)}, u32[]{:S(2)}, u32[]{:S(2)}) collective-permute-start(f32[608,128]{1,0:T(8,128)S(1)} %get-tuple-element.21.own), channel_id=1, source_target_pairs={{0,1},{1,2},{2,3},{3,4},{4,5},{5,6},{6,7},{7,8},{8,9},{9,10},{10,1... | collective-permute-start | bytes 933896 | tf_op jit(solution)/shard_map/ppermute | solution.py:472
  26.3 21.5 %collective-permute-start.1 = (f32[608,128]{1,0:T(8,128)S(1)}, f32[608,128]{1,0:T(8,128)S(1)}, u32[]{:S(2)}, u32[]{:S(2)}) collective-permute-start(f32[608,128]{1,0:T(8,128)S(1)} %get-tuple-element.22.own_prev), channel_id=1, source_target_pairs={{0,31},{1,0},{2,1},{3,2},{4,3},{5,4},{6,5},{7,6},{8,7},{9,8},{10,9... | collective-permute-start | bytes 933896 | tf_op jit(solution)/shard_map/ppermute | solution.py:472
  34.6 0.7 copy-start.9
  35.3 0.8 copy-start.7
  36.2 11.7 %copy-start = (f32[128,128]{1,0:T(8,128)S(1)}, f32[128,128]{1,0:T(8,128)}, u32[]{:S(2)}) copy-start(f32[128,128]{1,0:T(8,128)} %radiation.5) | copy-start | bytes 196612
  59.9 16.5 %collective-permute-start.3 = (f32[624,128]{1,0:T(8,128)S(1)}, f32[624,128]{1,0:T(8,128)S(1)}, u32[]{:S(2)}, u32[]{:S(2)}) collective-permute-start(f32[624,128]{1,0:T(8,128)S(1)} %get-tuple-element.24), channel_id=1, source_target_pairs={{0,31},{1,0},{2,1},{3,2},{4,3},{5,4},{6,5},{7,6},{8,7},{9,8},{10,9... | collective-permute-start | bytes 958472 | tf_op jit(solution)/shard_map/ppermute | solution.py:472
  69.9 16.4 %collective-permute-start.2 = (f32[624,128]{1,0:T(8,128)S(1)}, f32[624,128]{1,0:T(8,128)S(1)}, u32[]{:S(2)}, u32[]{:S(2)}) collective-permute-start(f32[624,128]{1,0:T(8,128)S(1)} %get-tuple-element.23.own), channel_id=1, source_target_pairs={{0,1},{1,2},{2,3},{3,4},{4,5},{5,6},{6,7},{7,8},{8,9},{9,10},{10,1... | collective-permute-start | bytes 958472 | tf_op jit(solution)/shard_map/ppermute | solution.py:472
  97.4 4.1 %collective-permute-start.5 = (f32[288,128]{1,0:T(8,128)S(1)}, f32[288,128]{1,0:T(8,128)S(1)}, u32[]{:S(2)}, u32[]{:S(2)}) collective-permute-start(f32[288,128]{1,0:T(8,128)S(1)} %get-tuple-element.30), channel_id=1, source_target_pairs={{0,31},{1,0},{2,1},{3,2},{4,3},{5,4},{6,5},{7,6},{8,7},{9,8},{10,9... | collective-permute-start | bytes 442376 | tf_op jit(solution)/shard_map/ppermute | solution.py:472
  97.8 12.1 %collective-permute-start.4 = (f32[288,128]{1,0:T(8,128)S(1)}, f32[288,128]{1,0:T(8,128)S(1)}, u32[]{:S(2)}, u32[]{:S(2)}) collective-permute-start(f32[288,128]{1,0:T(8,128)S(1)} %get-tuple-element.30), channel_id=1, source_target_pairs={{0,1},{1,2},{2,3},{3,4},{4,5},{5,6},{6,7},{7,8},{8,9},{9,10},{10,1... | collective-permute-start | bytes 442376 | tf_op jit(solution)/shard_map/ppermute | solution.py:472
  130.8 16.0 %copy-start.1 = (bf16[256,256]{1,0:T(8,128)(2,1)S(1)}, bf16[256,256]{1,0:T(8,128)(2,1)}, u32[]{:S(2)}) copy-start(bf16[256,256]{1,0:T(8,128)(2,1)} %constant.12.clone.chosen) | copy-start | bytes 393220

commit v2 on v1

--- a/solution.py
+++ b/solution.py
@@ -18,6 +18,8 @@
 BF16 = jnp.bfloat16
 HIGHEST = lax.Precision.HIGHEST
 CHUNK = 20
+GROUP_ONE, GROUP_TWO = 4, 4
+GROUP_B2, GROUP_B1, GROUP_B0 = (4, 2), (4, 4), (4, 2)
 PACK = 16
 
 
@@ -89,16 +91,19 @@
     return -(center[:, 0:1] * along_x + center[:, 1:2] * along_y) + DIFFUSION * laplace
 
 
-def forward_tiles(w, fields, x, y, n):
-    center = fields.get(x, y, n)
-    along_x = deriv_x(lambda k: fields.get(x + k, y, n))
-    total = moved_of(fields, x, y, n, center, along_x)
-    parts = []
-    for lo in range(0, n, 8):
-        hi = min(n, lo + 8)
-        features = features_of(center[lo:hi], along_x[lo:hi])
-        parts.append(closure_of(w, hidden(w, features)[3]))
-    return center, total + (jnp.concatenate(parts, axis=0) if len(parts) > 1 else parts[0])
+def joined(parts):
+    return jnp.concatenate(parts, axis=0) if len(parts) > 1 else parts[0]
+
+
+def forward_tiles(w, fields, xs, y, n):
+    centers = [fields.get(x, y, n) for x in xs]
+    slopes = [deriv_x(lambda k, x=x: fields.get(x + k, y, n)) for x in xs]
+    closure = closure_of(w, hidden(w, features_of(joined(centers), joined(slopes)))[3])
+    result = []
+    for i, x in enumerate(xs):
+        moved = moved_of(fields, x, y, n, centers[i], slopes[i])
+        result.append((x, centers[i], moved + closure[i * n : i * n + n]))
+    return result
 
 
 def shifted(value, by):
@@ -149,51 +154,61 @@
         patch.add_field(x, y, 5, gain * packs[1][pl.ds(i * PACK, n), :])
 
 
-def backward_tiles(w, fields, lead, x, spans, spread, direct, sums, emit):
-    centers = [fields.get(x, y, n) for y, n in spans]
-    slopes = [deriv_x(lambda k, y=y, n=n: fields.get(x + k, y, n)) for y, n in spans]
-    leads = [lead.get(x, y, n) for y, n in spans]
-    center = jnp.concatenate(centers, axis=0) if len(spans) > 1 else centers[0]
-    along_x = jnp.concatenate(slopes, axis=0) if len(spans) > 1 else slopes[0]
-    lam = jnp.concatenate(leads, axis=0) if len(spans) > 1 else leads[0]
-    features = features_of(center, along_x)
+def backward_tiles(w, fields, lead, xs, y, n, spread, direct, sums, emit):
+    centers = [fields.get(x, y, n) for x in xs]
+    slopes = [deriv_x(lambda k, x=x: fields.get(x + k, y, n)) for x in xs]
+    center, lam = joined(centers), joined([lead.get(x, y, n) for x in xs])
+    features = features_of(center, joined(slopes))
     out_cot = to_lanes(jnp.concatenate([lam, jnp.zeros_like(lam)], axis=1).astype(BF16))
     tanh_one, hidden_one, tanh_two, hidden_two = hidden(w, features)
     pre_two = (dot(w["out_t"][...], out_cot) * (1.0 - tanh_two * tanh_two)).astype(BF16)
     pre_one = (dot(w["mid_t"][...], pre_two) * (1.0 - tanh_one * tanh_one)).astype(BF16)
     feature_cot = dot(w["in_t"][...], pre_one)
-    if sums is not None:
-        sums[0:128, :] += dot_nt(pre_two, hidden_one)
-        sums[128:144, :] += dot_nt(features, pre_one)
-        sums[144:160, :] += dot_nt(out_cot, hidden_two)
     own = to_tiles(feature_cot[0:8, :])
     other = center[:, 0:1] * lam - to_tiles(feature_cot[8:16, :])
-    first = 0
-    for y, n in spans:
-        spread.put(x, y, other[first : first + n])
-        direct.put(x, y, own[first : first + n])
-        first += n
+    for i, x in enumerate(xs):
+        spread.put(x, y, other[i * n : i * n + n])
+        direct.put(x, y, own[i * n : i * n + n])
+    if sums is None:
+        return
+
+    def kept(value):
+        if n == OWN_Y:
+            return value
+        first = [(i * n - y) * LEV for i in range(len(xs))]
+        return jnp.concatenate([value[:, k : k + OWN_Y * LEV] for k in first], axis=1)
+
+    kept_one = kept(pre_one)
+    kept_two = kept(hidden_two)
+    sums[0:128, :] += dot_nt(kept(pre_two), kept(hidden_one))
+    sums[128:144, :] += dot_nt(kept(features), kept_one)
+    sums[144:160, :] += dot_nt(kept(out_cot), kept_two)
     if emit is not None:
-        emit(x, center, along_x, hidden_two)
-
-
-def closure_backward(w, fields, lead, x_lo, x_hi, y_lo, y_hi, spread, direct, sums, emit=None):
-    whole = [(y_lo, y_hi - y_lo)]
-    rim = [(y, n) for y, n in ((y_lo, -y_lo), (OWN_Y, y_hi - OWN_Y)) if n > 0]
-
-    def own_x(x, carry):
-        backward_tiles(w, fields, lead, x, [(0, OWN_Y)], spread, direct, sums, emit)
-        if rim:
-            backward_tiles(w, fields, lead, x, rim, spread, direct, None, None)
+        closure = closure_of(w, kept_two)
+        for i, x in enumerate(xs):
+            tiles = slice(-y, OWN_Y - y)
+            emit(x, centers[i][tiles], slopes[i][tiles], closure[i * OWN_Y : (i + 1) * OWN_Y])
+
+
+def closure_backward(
+    w, fields, lead, x_lo, x_hi, y_lo, y_hi, spread, direct, sums, emit=None, own_group=2, rim_group=2
+):
+    n = y_hi - y_lo
+
+    def own_x(i, carry):
+        xs = [i * own_group + j for j in range(own_group)]
+        backward_tiles(w, fields, lead, xs, y_lo, n, spread, direct, sums, emit)
         return carry
 
     def rim_x(i, carry):
-        x = x_lo - 2 + i + jnp.where(i < 2 - x_lo, 0, OWN_X)
-        backward_tiles(w, fields, lead, x, whole, spread, direct, None, None)
+        first = x_lo - 2 + i * rim_group
+        first = first + jnp.where(first < 0, 0, OWN_X)
+        xs = [first + j for j in range(rim_group)]
+        backward_tiles(w, fields, lead, xs, y_lo, n, spread, direct, None, None)
         return carry
 
-    lax.fori_loop(0, OWN_X, own_x, 0)
-    lax.fori_loop(0, x_hi - x_lo + 4 - OWN_X, rim_x, 0)
+    lax.fori_loop(0, OWN_X // own_group, own_x, 0)
+    lax.fori_loop(0, (x_hi - x_lo + 4 - OWN_X) // rim_group, rim_x, 0)
 
 
 def adjoint_tiles(fields, lead, x, y, n, spread, direct):
@@ -250,81 +265,75 @@
     left[96:97, 0:256] = fall[...]
     left[97:98, 0:256] = live[...].astype(F32)
     parts = split_three(left[...])
-    place = lax.broadcasted_iota(jnp.int32, (512, LEV), 0)
+    turn = 32 * turned_half(lax.axis_index("gx"))
+    place = lax.broadcasted_iota(jnp.int32, (512, LEV), 0) ^ turn
     for block in range(GZ):
         chosen = jnp.where(place == table[block : block + 1, :], 1.0, 0.0).astype(BF16)
         out[block] = dot(parts[0], chosen) + dot(parts[1], chosen) + dot(parts[2], chosen)
 
 
-def turn_kernel(got, to_next, to_prev):
+def turn_kernel(got, own, next_cot, prev_cot):
     for which in range(NF):
         blocks = [got[k, which * 16 : which * 16 + 16, :] for k in range(GZ)]
         turned = jnp.concatenate(blocks, axis=0).T
-        to_next[which * 72 : which * 72 + 72, :] = turned[0:72]
-        to_prev[which * 72 : which * 72 + 72, :] = turned[0:72]
-        to_next[432 + which * 28 : 460 + which * 28, :] = turned[100:128]
-        to_prev[432 + which * 28 : 460 + which * 28, :] = turned[72:100]
-    to_next[600:608, :] = got[0, 96:104, :]
-    to_prev[600:608, :] = got[0, 96:104, :]
+        own[which * 72 : which * 72 + 72, :] = turned[0:72]
+        next_cot[which * 28 : which * 28 + 28, :] = turned[100:128]
+        prev_cot[which * 28 : which * 28 + 28, :] = turned[72:100]
+    own[432:440, :] = got[0, 96:104, :]
 
 
 def forward_kernel(
-    own, own_prev, before, after, bundle, w_in, w_out_t, radiation,
-    state, cot, fall, live, one, to_next, to_prev,
+    own, before, after, bundle, w_in, w_out_t, radiation,
+    state, fall, live, one, to_both, next_one, prev_one,
     two, p_theta, p_rain, p_fall, p_live,
 ):
     w = weights_of(bundle) | {"in": w_in, "out_t": w_out_t}
     packs = (p_theta, p_rain, p_fall, p_live)
     state[...] = jnp.zeros(state.shape, F32)
-    cot[...] = jnp.zeros(cot.shape, F32)
     for place, source in enumerate((before, own, after)):
         for which in range(NF):
             columns = source[which * 72 : which * 72 + 72, :]
             state[pl.ds(place * 576 + which, 72, stride=8), :] = columns
         rows = pl.ds(place * 72, 72)
-        fall[rows, :] = jnp.broadcast_to(source[600:601, :], (LEV, LEV)).T[0:72]
-        live[rows, :] = jnp.broadcast_to(source[601:602, :], (LEV, LEV)).T[0:72]
-    for place, source in enumerate((before, own_prev, own, after)):
-        for which in range(NF):
-            columns = source[432 + which * 28 : 460 + which * 28, :]
-            cot[pl.ds(place * 224 + which, 28, stride=8), :] = columns
+        fall[rows, :] = jnp.broadcast_to(source[432:433, :], (LEV, LEV)).T[0:72]
+        live[rows, :] = jnp.broadcast_to(source[433:434, :], (LEV, LEV)).T[0:72]
     s_zero = Patch(state, -4, 12, -5, 18)
     s_one = Patch(one, -2, 8, -4, 16)
     s_two = Patch(two, 0, 4, -3, 14)
 
     def stage_one(i, carry):
-        x = i - 2
-        center, total = forward_tiles(w, s_zero, x, -4, 16)
-        s_one.put(x, -4, center + STEP * total)
+        xs = [i * GROUP_ONE - 2 + j for j in range(GROUP_ONE)]
+        for x, center, total in forward_tiles(w, s_zero, xs, -4, 16):
+            s_one.put(x, -4, center + STEP * total)
         return carry
 
-    lax.fori_loop(0, 8, stage_one, 0)
+    lax.fori_loop(0, 8 // GROUP_ONE, stage_one, 0)
     xs = range(-2, 6)
     column_terms(s_zero, xs, -4, 16, fall, live, radiation, packs, False)
     add_columns(s_one, xs, -4, 16, packs, STEP)
 
-    def stage_two(x, carry):
-        center, total = forward_tiles(w, s_one, x, -3, 14)
-        s_two.put(x, -3, 0.75 * s_zero.get(x, -3, 14) + 0.25 * (center + STEP * total))
+    def stage_two(i, carry):
+        xs = [i * GROUP_TWO + j for j in range(GROUP_TWO)]
+        for x, center, total in forward_tiles(w, s_one, xs, -3, 14):
+            s_two.put(x, -3, 0.75 * s_zero.get(x, -3, 14) + 0.25 * (center + STEP * total))
         return carry
 
-    lax.fori_loop(0, 4, stage_two, 0)
+    lax.fori_loop(0, 4 // GROUP_TWO, stage_two, 0)
     xs = range(4)
     column_terms(s_one, xs, -3, 14, fall, live, radiation, packs, False)
     add_columns(s_two, xs, -3, 14, packs, 0.25 * STEP)
     for which in range(NF):
-        columns = two[pl.ds(which, 56, stride=8), :]
-        to_next[which * 56 : which * 56 + 56, :] = columns
-        to_prev[which * 56 : which * 56 + 56, :] = columns
+        to_both[which * 56 : which * 56 + 56, :] = two[pl.ds(which, 56, stride=8), :]
         for i in range(4):
-            rows = pl.ds(336 + which * 48 + i * 12, 12)
-            to_next[rows, :] = s_one.field(i - 2, -2, 12, which)
-            to_prev[rows, :] = s_one.field(i + 2, -2, 12, which)
+            rows = pl.ds(which * 48 + i * 12, 12)
+            next_one[rows, :] = s_one.field(i - 2, -2, 12, which)
+            prev_one[rows, :] = s_one.field(i + 2, -2, 12, which)
 
 
 def middle_kernel(
-    own, before, after, bundle, w_in, w_out_t, radiation, state, cot, fall, live,
-    cot_two, to_both, new_state, sums,
+    own, before, after, cot_before, prev_cot, next_cot, cot_after,
+    bundle, w_in, w_out_t, radiation, state, fall, live,
+    cot_two, to_both, new_state, known, sums,
     two, lead, spread, direct, p_theta, p_rain, p_fall, p_live,
 ):
     w = weights_of(bundle) | {"in": w_in, "out_t": w_out_t}
@@ -334,7 +343,11 @@
         for which in range(NF):
             columns = source[which * 56 : which * 56 + 56, :]
             two[pl.ds(place * 448 + which, 56, stride=8), :] = columns
-    lead[...] = (2.0 / 3.0) * cot[...]
+    lead[...] = jnp.zeros(lead.shape, F32)
+    for place, source in enumerate((cot_before, prev_cot, next_cot, cot_after)):
+        for which in range(NF):
+            columns = source[which * 28 : which * 28 + 28, :]
+            lead[pl.ds(place * 224 + which, 28, stride=8), :] = (2.0 / 3.0) * columns
     sums[...] = jnp.zeros(sums.shape, F32)
     s_zero = Patch(state, -4, 12, -5, 18)
     s_two = Patch(two, -4, 12, -3, 14)
@@ -343,12 +356,12 @@
     c_two = Patch(cot_two, 0, 4, -2, 12)
     new = Patch(new_state, 0, 4, 0, 8)
 
-    def emit(x, center, along_x, hidden_two):
-        total = moved_of(s_two, x, 0, OWN_Y, center, along_x) + closure_of(w, hidden_two)
+    def emit(x, center, along_x, closure):
+        total = moved_of(s_two, x, 0, OWN_Y, center, along_x) + closure
         old = s_zero.get(x, 0, OWN_Y)
         new.put(x, 0, old * (1.0 / 3.0) + (2.0 / 3.0) * (center + STEP * total))
 
-    closure_backward(w, s_two, lam, 0, 4, -2, 10, spread_at, direct_at, sums, emit)
+    closure_backward(w, s_two, lam, 0, 4, -2, 10, spread_at, direct_at, sums, emit, *GROUP_B2)
     xs = range(4)
     column_terms(s_two, xs, 0, 8, fall, live, radiation, packs, False)
     add_columns(new, xs, 0, 8, packs, (2.0 / 3.0) * STEP)
@@ -361,13 +374,16 @@
     lax.fori_loop(0, 4, gather, 0)
     column_terms(lam, xs, -2, 12, fall, live, radiation, packs, True)
     add_columns(c_two, xs, -2, 12, packs, STEP)
+    base = Patch(known, 0, 4, 0, 8)
+    for x in xs:
+        base.put(x, 0, 0.5 * lam.get(x, 0, 8) + 0.75 * c_two.get(x, 0, 8))
     for which in range(NF):
         to_both[which * 48 : which * 48 + 48, :] = cot_two[pl.ds(which, 48, stride=8), :]
 
 
 def last_kernel(
     own, before, after, one, one_before, one_after, bundle, w_in, w_out_t, radiation,
-    state, cot, fall, live, new_state, sums_two,
+    state, fall, live, new_state, known, sums_two,
     out,
     wide, lead, c_one, spread, direct, spread_zero, direct_zero, grad, sums,
     p_theta, p_rain, p_fall, p_live,
@@ -377,10 +393,9 @@
     wide[...] = jnp.zeros(wide.shape, F32)
     lead[...] = jnp.zeros(lead.shape, F32)
     for which in range(NF):
-        rows = slice(336 + which * 48, 384 + which * 48)
+        rows = slice(which * 48, which * 48 + 48)
         wide[pl.ds(which, 48, stride=8), :] = one_before[rows, :]
         wide[pl.ds(1152 + which, 48, stride=8), :] = one_after[rows, :]
-        rows = slice(which * 48, which * 48 + 48)
         lead[pl.ds(which, 48, stride=8), :] = 0.25 * before[rows, :]
         lead[pl.ds(768 + which, 48, stride=8), :] = 0.25 * after[rows, :]
     s_own = Patch(one, -2, 8, -4, 16)
@@ -393,7 +408,7 @@
     lam_one = Patch(lead, -4, 12, -2, 12)
     lam_zero = Patch(c_one, -2, 8, -1, 10)
     spread_at, direct_at = Patch(spread, -4, 12, -1, 10), Patch(direct, -4, 12, -1, 10)
-    closure_backward(w, s_one, lam_one, -2, 6, -1, 9, spread_at, direct_at, sums)
+    closure_backward(w, s_one, lam_one, -2, 6, -1, 9, spread_at, direct_at, sums, None, *GROUP_B1)
 
     def gather_one(i, carry):
         x = i - 2
@@ -407,14 +422,13 @@
     add_columns(lam_zero, xs, -1, 10, packs, STEP)
 
     spread_z, direct_z = Patch(spread_zero, -2, 8, 0, 8), Patch(direct_zero, -2, 8, 0, 8)
-    closure_backward(w, s_zero, lam_zero, 0, 4, 0, 8, spread_z, direct_z, sums)
-    c_zero, c_two = Patch(cot, -2, 8, -3, 14), Patch(own, 0, 4, -2, 12)
+    closure_backward(w, s_zero, lam_zero, 0, 4, 0, 8, spread_z, direct_z, sums, None, *GROUP_B0)
+    base = Patch(known, 0, 4, 0, 8)
     final = Patch(grad, 0, 4, 0, 8)
 
     def gather_zero(x, carry):
         center, result = adjoint_tiles(s_zero, lam_zero, x, 0, 8, spread_z, direct_z)
-        known = c_zero.get(x, 0, 8) * (1.0 / 3.0) + 0.75 * c_two.get(x, 0, 8)
-        final.put(x, 0, known + center + STEP * result)
+        final.put(x, 0, base.get(x, 0, 8) + center + STEP * result)
         return carry
 
     lax.fori_loop(0, 4, gather_zero, 0)
@@ -447,16 +461,25 @@
     for block in range(1, GZ):
         total = total + got[block, 48:68, :]
     chunk[...] = total
+    turn = 4 * turned_half(lax.axis_index("gx"))
     for index, out in enumerate((new_state, grad)):
         for half in range(2):
             lanes = slice((2 * index + half) * 32, (2 * index + half + 1) * 32)
-            row = jnp.concatenate([got[k, 0:48, lanes] for k in range(GZ)], axis=1)
+            row = jnp.concatenate([got[k ^ turn, 0:48, lanes] for k in range(GZ)], axis=1)
             placed = pick(row, chosen[...])
             for pair in range(3):
                 out[2 * pair + half] = placed[pair * 16 : pair * 16 + 16]
 
 
-def call(kernel, outs, scratch, *operands):
+def finish_kernel(got, grad_in, grad_mid, grad_out):
+    total = got[...].reshape(GZ * CHUNK, LEV)
+    grad_mid[...] = total[0:128]
+    rows = [total[128:134], total[136:142], jnp.zeros((116, LEV), F32)]
+    grad_in[...] = jnp.concatenate(rows, axis=0).T[:, 0:12]
+    grad_out[...] = total[144:150]
+
+
+def call(kernel, outs, scratch, *operands, giga=0):
     vmem = pl.BlockSpec(memory_space=pltpu.VMEM)
     return pl.pallas_call(
         kernel,
@@ -464,12 +487,25 @@
         in_specs=[vmem] * len(operands),
         out_specs=[vmem] * len(outs),
         scratch_shapes=[pltpu.VMEM(shape, F32) for shape in scratch],
+        cost_estimate=pl.CostEstimate(flops=giga * 10**9, transcendentals=0, bytes_accessed=10**6)
+        if giga
+        else None,
         compiler_params=pltpu.CompilerParams(vmem_limit_bytes=48 << 20),
     )(*operands)
 
 
+def turned_half(slab):
+    return (slab // 4) % 2
+
+
 def passed_along(shard, by):
-    return lax.ppermute(shard, "gx", [(i, (i + by) % GX) for i in range(GX)])
+    pairs = []
+    for block in range(GZ):
+        for slab in range(GX):
+            other = (slab + by) % GX
+            place = block ^ (4 * (turned_half(slab) ^ turned_half(other)))
+            pairs.append((block * GX + slab, place * GX + other))
+    return lax.ppermute(shard, ("gz", "gx"), pairs)
 
 
 def on_device(state, state_cot, w_in, w_mid, w_out, radiation, fall_rate, active):
@@ -492,33 +528,39 @@
         active.reshape(1, 256),
     )
     got = lax.all_to_all(packed, "gz", 0, 0)
-    own, own_prev = call(turn_kernel, [(608, LEV), (608, LEV)], [], got)
-    before, after = passed_along(own, 1), passed_along(own_prev, -1)
-    zero, cot, fall, live, one, to_next, to_prev = call(
+    own, next_cot, prev_cot = call(turn_kernel, [(440, LEV), (168, LEV), (168, LEV)], [], got)
+    before, after = passed_along(own, 1), passed_along(own, -1)
+    cot_before, cot_after = passed_along(next_cot, 1), passed_along(prev_cot, -1)
+    zero, fall, live, one, two, next_one, prev_one = call(
         forward_kernel,
-        [(1728, LEV), (896, LEV), (216, LEV), (216, LEV), (1024, LEV), (624, LEV), (624, LEV)],
+        [(1728, LEV), (216, LEV), (216, LEV), (1024, LEV), (336, LEV), (288, LEV), (288, LEV)],
         [(448, LEV)] + packs,
         own,
-        own_prev,
         before,
         after,
         *weights,
-    )
-    one_before, one_after = passed_along(to_next, 1), passed_along(to_prev, -1)
-    cot_two, to_both, new_state, sums = call(
+        giga=12,
+    )
+    two_before, two_after = passed_along(two, 1), passed_along(two, -1)
+    one_before, one_after = passed_along(next_one, 1), passed_along(prev_one, -1)
+    cot_two, to_both, new_state, known, sums = call(
         middle_kernel,
-        [(384, LEV), (288, LEV), (256, LEV), (GZ * CHUNK, LEV)],
+        [(384, LEV), (288, LEV), (256, LEV), (256, LEV), (GZ * CHUNK, LEV)],
         [(1344, LEV), (896, LEV), (768, LEV), (768, LEV)] + packs,
-        to_next,
-        one_before,
-        one_after,
+        two,
+        two_before,
+        two_after,
+        cot_before,
+        prev_cot,
+        next_cot,
+        cot_after,
         *weights,
         zero,
-        cot,
         fall,
         live,
-    )
-    two_before, two_after = passed_along(to_both, 1), passed_along(to_both, -1)
+        giga=11,
+    )
+    lead_before, lead_after = passed_along(to_both, 1), passed_along(to_both, -1)
     (sent,) = call(
         last_kernel,
         [(GZ, 68, LEV)],
@@ -526,18 +568,19 @@
         + [(256, LEV), (GZ * CHUNK, LEV)]
         + packs,
         cot_two,
-        two_before,
-        two_after,
+        lead_before,
+        lead_after,
         one,
         one_before,
         one_after,
         *weights,
         zero,
-        cot,
         fall,
         live,
         new_state,
+        known,
         sums,
+        giga=20,
     )
     got = lax.all_to_all(sent, "gz", 0, 0)
     new_state, grad_state, chunk = call(
@@ -550,10 +593,8 @@
     spread = lax.all_to_all(jnp.broadcast_to(chunk, (GX, CHUNK, LEV)), "gx", 0, 0)
     added = jnp.sum(spread, axis=0)
     totals = lax.all_to_all(jnp.broadcast_to(added, (GZ, CHUNK, LEV)), "gz", 0, 0)
-    totals = totals.reshape(GZ * CHUNK, LEV)
-    grad_in = totals[128:144].T
-    grad_in = jnp.concatenate([grad_in[:, 0:NF], grad_in[:, 8 : 8 + NF]], axis=1)
-    return (new_state, grad_state, grad_in, totals[0:128], totals[144:150])
+    grads = call(finish_kernel, [(128, 2 * NF), (128, LEV), (NF, LEV)], [], totals)
+    return (new_state, grad_state, *grads)
 
 
 def solution(mesh):

time: 180 us -> 155 us (0.86)
  Pallas kernels: 46.9 us -> 28.2 us
  waiting for transfers between devices: 50.7 us -> 36.4 us
  blocking collectives: 45.2 us -> 50.7 us
  starting transfers between devices: 28.8 us -> 32.6 us
    pallas_call x6 -> x7, Pallas kernels: 46.9 us -> 28.2 us  [call(): pl.pallas_call(kernel, out_shape=[jax.ShapeDtypeStruct(shape, F32) for sh...]
    ppermute x6 -> x10, waiting for transfers between devices: 39 us -> 26.3 us  [passed_along(): return lax.ppermute(shard, ('gz', 'gx'), pairs)]
    all_to_all x1, blocking collectives: 16 us -> 21.5 us  [on_device(): got = lax.all_to_all(sent, 'gz', 0, 0)]
    ppermute x6 -> x10, starting transfers between devices: 21.3 us -> 25 us  [passed_along(): return lax.ppermute(shard, ('gz', 'gx'), pairs)]
    unnamed x25 -> x26, local copies, waits for them, and re-layouts: 4.56 us -> 5.23 us
  transfers between devices with their start and end apart: 7 -> 11, of which waited for: 6 -> 6; matrix products, arithmetic and copies ran while one was open for 0% -> 0% of each run, Pallas kernels for 0% -> 4%
where the time goes in v2:
time: 155 us; the launch traced here: 154 us
  blocking collectives  50.7 us (33%)
  waiting for transfers between devices  36.4 us (23%)
  starting transfers between devices  32.6 us (21%)
  Pallas kernels  28.2 us (18%)
  local copies, waits for them, and re-layouts  5.41 us (3%)
    pallas_call x7, Pallas kernels, call(): pl.pallas_call(kernel, out_shape=[jax.ShapeDtypeStruct(shape, F32) for sh...  28.2 us
    ppermute x10, waiting for transfers between devices, passed_along(): return lax.ppermute(shard, ('gz', 'gx'), pairs)  26.3 us
    ppermute x10, starting transfers between devices, passed_along(): return lax.ppermute(shard, ('gz', 'gx'), pairs)  25 us
    all_to_all x1, blocking collectives, on_device(): got = lax.all_to_all(sent, 'gz', 0, 0)  21.5 us
    all_to_all x1, blocking collectives, on_device(): lax.all_to_all(jnp.broadcast_to(chunk, (GX, CHUNK, LEV)), 'gx', 0, 0)  17.6 us
    all_to_all x1, blocking collectives, on_device(): lax.all_to_all(jnp.broadcast_to(added, (GZ, CHUNK, LEV)), 'gz', 0, 0)  11.6 us
    all_to_all x1, waiting for transfers between devices, on_device(): got = lax.all_to_all(packed, 'gz', 0, 0)  10.1 us
    all_to_all x1, starting transfers between devices, on_device(): got = lax.all_to_all(packed, 'gz', 0, 0)  7.53 us
  transfers between devices with their start and end apart: 11, of which 6 were waited for; matrix products, arithmetic and copies ran while one was open for 0% of the time, Pallas kernels for 4%

profile of v2, /device:TPU:1, one launch (start us, length us, event | category | flops | bytes accessed | tf_op | source)
XLA Modules:
  0.0 154.3 jit_solution(11252397092323066478)
XLA Ops:
  0.6 0.0 copy-start.3
  0.7 0.7 copy-done.3
  1.3 0.0 copy-done.5
  1.3 0.0 copy-done.4
  1.3 0.9 copy-done.1
  2.2 0.9 copy-done.2
  3.1 1.7 %shard_map.137 = f32[8,104,128]{2,1,0:T(8,128)} custom-call(s32[8,128]{1,0:T(8,128)S(1)} %copy-done.3, f32[6,16,256]{2,1,0:T(8,128)S(1)} %copy-done.1, f32[6,16,256]{2,1,0:T(8,128)S(1)} %copy-done.2, f32[1,256]{1,0:T(1,128)S(1)} %bitcast.7, s32[1,256]{1,0:T(1,128)S(1)} %bitcast.8), custom_call_target="tpu_custom_call" | custom-call | tf_op jit(solution)/shard_map/pallas_call | solution.py:484
  4.8 7.5 %all-to-all-start = ((f32[8,104,128]{2,1,0:T(8,128)}), f32[8,104,128]{2,1,0:T(8,128)S(1)}, u32[]{:S(2)}, u32[]{:S(2)}) async-start(f32[8,104,128]{2,1,0:T(8,128)} %shard_map.137), calls=%async_computation | async-start | bytes 851968 | tf_op jit(solution)/shard_map/all_to_all | solution.py:530
  12.4 0.6 copy-done.10
  13.0 0.1 slice_select_fusion
  13.1 0.1 copy.39.w_in
  13.2 0.6 copy-done.9
  13.8 0.1 copy.37
  13.9 0.1 copy.45
  14.0 0.5 copy-done.7
  14.5 0.1 copy.36
  14.6 10.1 %all-to-all-done.got = f32[8,104,128]{2,1,0:T(8,128)S(1)} async-done(((f32[8,104,128]{2,1,0:T(8,128)}), f32[8,104,128]{2,1,0:T(8,128)S(1)}, u32[]{:S(2)}, u32[]{:S(2)}) %all-to-all-start) | async-done | bytes 426016 | tf_op jit(solution)/shard_map/all_to_all | solution.py:530
  24.7 0.2 shard_map.138
  24.9 6.3 %collective-permute-start.1 = (f32[440,128]{1,0:T(8,128)S(1)}, f32[440,128]{1,0:T(8,128)S(1)}, u32[]{:S(2)}, u32[]{:S(2)}) collective-permute-start(f32[440,128]{1,0:T(8,128)S(1)} %get-tuple-element.26.own), channel_id=1, source_target_pairs={{0,159},{1,0},{2,1},{3,2},{4,131},{5,4},{6,5},{7,6},{8,135},{9,8},... | collective-permute-start | bytes 675848 | tf_op jit(solution)/shard_map/ppermute | solution.py:508
  31.2 0.0 collective-permute-start
  31.2 0.0 copy-start.6
  31.2 8.4 %collective-permute-done.1.after = f32[440,128]{1,0:T(8,128)S(1)} collective-permute-done((f32[440,128]{1,0:T(8,128)S(1)}, f32[440,128]{1,0:T(8,128)S(1)}, u32[]{:S(2)}, u32[]{:S(2)}) %collective-permute-start.1) | collective-permute-done | bytes 225312 | tf_op jit(solution)/shard_map/ppermute | solution.py:508
  39.6 3.6 %collective-permute-done.before = f32[440,128]{1,0:T(8,128)S(1)} collective-permute-done((f32[440,128]{1,0:T(8,128)S(1)}, f32[440,128]{1,0:T(8,128)S(1)}, u32[]{:S(2)}, u32[]{:S(2)}) %collective-permute-start) | collective-permute-done | bytes 225312 | tf_op jit(solution)/shard_map/ppermute | solution.py:508
  43.2 6.0 %shard_map.139 = (f32[1728,128]{1,0:T(8,128)S(1)}, f32[216,128]{1,0:T(8,128)S(1)}, f32[216,128]{1,0:T(8,128)S(1)}, f32[1024,128]{1,0:T(8,128)S(1)}, f32[336,128]...) custom-call(f32[440,128]{1,0:T(8,128)S(1)} %get-tuple-element.26.own, ...), custom_call_target="tpu_custom_call" | custom-call | flops 12000000000 | bytes 1000000 | tf_op jit(solution)/shard_map/pallas_call | solution.py:484
  49.2 5.2 %collective-permute-start.3 = (f32[336,128]{1,0:T(8,128)S(1)}, f32[336,128]{1,0:T(8,128)S(1)}, u32[]{:S(2)}, u32[]{:S(2)}) collective-permute-start(f32[336,128]{1,0:T(8,128)S(1)} %get-tuple-element.27.own), channel_id=1, source_target_pairs={{0,159},{1,0},{2,1},{3,2},{4,131},{5,4},{6,5},{7,6},{8,135},{9,8},... | collective-permute-start | bytes 516104 | tf_op jit(solution)/shard_map/ppermute | solution.py:508
  54.4 0.0 collective-permute-start.2
  54.4 0.0 collective-permute-start.4
  54.4 7.8 %collective-permute-start.5 = (f32[168,128]{1,0:T(8,128)S(1)}, f32[168,128]{1,0:T(8,128)S(1)}, u32[]{:S(2)}, u32[]{:S(2)}) collective-permute-start(f32[168,128]{1,0:T(8,128)S(1)} %get-tuple-element.29.prev_cot), channel_id=1, source_target_pairs={{0,159},{1,0},{2,1},{3,2},{4,131},{5,4},{6,5},{7,6},{8,135},{9,8},... | collective-permute-start | bytes 258056 | tf_op jit(solution)/shard_map/ppermute | solution.py:508
  62.2 0.0 collective-permute-start.8
  62.2 4.0 %collective-permute-done.4.cot_before = f32[168,128]{1,0:T(8,128)S(1)} collective-permute-done((f32[168,128]{1,0:T(8,128)S(1)}, f32[168,128]{1,0:T(8,128)S(1)}, u32[]{:S(2)}, u32[]{:S(2)}) %collective-permute-start.4) | collective-permute-done | bytes 86048 | tf_op jit(solution)/shard_map/ppermute | solution.py:508
  66.2 3.8 %collective-permute-start.9 = (f32[288,128]{1,0:T(8,128)S(1)}, f32[288,128]{1,0:T(8,128)S(1)}, u32[]{:S(2)}, u32[]{:S(2)}) collective-permute-start(f32[288,128]{1,0:T(8,128)S(1)} %get-tuple-element.37), channel_id=1, source_target_pairs={{0,159},{1,0},{2,1},{3,2},{4,131},{5,4},{6,5},{7,6},{8,135},{9,8},... | collective-permute-start | bytes 442376 | tf_op jit(solution)/shard_map/ppermute | solution.py:508
  70.0 0.0 collective-permute-done.5.cot_after
  70.0 0.0 collective-permute-done.3.after
  70.0 6.8 %shard_map.140 = (f32[384,128]{1,0:T(8,128)S(1)}, f32[288,128]{1,0:T(8,128)S(1)}, f32[256,128]{1,0:T(8,128)S(1)}, f32[256,128]{1,0:T(8,128)S(1)}, f32[160,128]{1,0:T(8,128)S(1)}) custom-call(f32[336,128]{1,0:T(8,128)S(1)} %get-tuple-element.27.own, f32[336,128]{1,0:T(8,128)S(1)} %collective-permute-done.2.before, ...), custom_call_target="tpu_custom_call" | custom-call | flops 11000000512 | bytes 1000000 | tf_op jit(solution)/shard_map/pallas_call | solution.py:484
  76.8 2.0 %collective-permute-start.7 = (f32[288,128]{1,0:T(8,128)S(1)}, f32[288,128]{1,0:T(8,128)S(1)}, u32[]{:S(2)}, u32[]{:S(2)}) collective-permute-start(f32[288,128]{1,0:T(8,128)S(1)} %get-tuple-element.34), channel_id=1, source_target_pairs={{0,159},{1,0},{2,1},{3,2},{4,131},{5,4},{6,5},{7,6},{8,135},{9,8},... | collective-permute-start | bytes 442376 | tf_op jit(solution)/shard_map/ppermute | solution.py:508
  78.8 0.0 collective-permute-start.6
  78.8 0.0 collective-permute-done.8.one_before
  78.8 0.0 collective-permute-done.9.one_after
  78.8 5.2 %collective-permute-done.7.after = f32[288,128]{1,0:T(8,128)S(1)} collective-permute-done((f32[288,128]{1,0:T(8,128)S(1)}, f32[288,128]{1,0:T(8,128)S(1)}, u32[]{:S(2)}, u32[]{:S(2)}) %collective-permute-start.7) | collective-permute-done | bytes 147488 | tf_op jit(solution)/shard_map/ppermute | solution.py:508
  84.0 5.2 %collective-permute-done.6.before = f32[288,128]{1,0:T(8,128)S(1)} collective-permute-done((f32[288,128]{1,0:T(8,128)S(1)}, f32[288,128]{1,0:T(8,128)S(1)}, u32[]{:S(2)}, u32[]{:S(2)}) %collective-permute-start.6) | collective-permute-done | bytes 147488 | tf_op jit(solution)/shard_map/ppermute | solution.py:508
  89.1 11.9 %shard_map.141 = f32[8,68,128]{2,1,0:T(8,128)S(1)} custom-call(f32[384,128]{1,0:T(8,128)S(1)} %get-tuple-element.33.own, f32[288,128]{1,0:T(8,128)S(1)} %collective-permute-done.6.before, f32[288,128]{1,0:T(8,128)S(1)} %collective-permute-done.7.after, f32[1024,128]{1,0:T(8,128)S(1)} %get-tuple-element.35.one, ...), custom_call_target="tpu_custom_call" | custom-call | flops 20000000000 | bytes 1000000 | tf_op jit(solution)/shard_map/pallas_call | solution.py:484
  101.0 0.0 copy-start
  101.0 21.5 %all_to_all.20.got = f32[8,68,128]{2,1,0:T(8,128)S(1)} all-to-all(f32[8,68,128]{2,1,0:T(8,128)S(1)} %shard_map.141), channel_id=1, replica_groups=mesh['gz'=8,'gx'=32] {'gz'}, dimensions={0} | all-to-all | bytes 557056 | tf_op jit(solution)/shard_map/all_to_all | solution.py:585
  122.5 1.1 shard_map.142
  123.7 17.6 %all_to_all.21 = f32[32,20,128]{2,1,0:T(8,128)S(1)} all-to-all(f32[32,20,128]{2,1,0:T(8,128)S(1)} %broadcast_in_dim.6), channel_id=1, replica_groups=mesh['gz'=8,'gx'=32] {'gx'}, dimensions={0} | all-to-all | bytes 655360 | tf_op jit(solution)/shard_map/all_to_all | solution.py:593
  141.3 11.6 %all_to_all.22.got = f32[8,20,128]{2,1,0:T(8,128)S(1)} all-to-all(f32[8,20,128]{2,1,0:T(8,128)S(1)} %broadcast_in_dim.7), channel_id=1, replica_groups=mesh['gz'=8,'gx'=32] {'gz'}, dimensions={0} | all-to-all | bytes 163840 | tf_op jit(solution)/shard_map/all_to_all | solution.py:595
  153.0 0.6 shard_map.143
  153.6 0.7 copy.43
  (20 shorter events, 0.1 us)
Async XLA Ops:
  0.6 0.7 copy-start.3
  0.6 0.7 copy-start.5
  0.7 0.7 copy-start.4
  1.3 0.9 copy-start.1
  2.2 0.9 copy-start.2
  4.8 7.5 %copy-start.8 = (bf16[128,12]{0,1:T(8,128)(2,1)S(1)}, bf16[128,12]{0,1:T(8,128)(2,1)}, u32[]{:S(2)}) copy-start(bf16[128,12]{0,1:T(8,128)(2,1)} %param.12) | copy-start | bytes 9220
  4.8 19.9 %all-to-all-start = ((f32[8,104,128]{2,1,0:T(8,128)}), f32[8,104,128]{2,1,0:T(8,128)S(1)}, u32[]{:S(2)}, u32[]{:S(2)}) async-start(f32[8,104,128]{2,1,0:T(8,128)} %shard_map.137), calls=%async_computation | async-start | bytes 851968 | tf_op jit(solution)/shard_map/all_to_all | solution.py:530
  12.3 0.7 copy-start.10
  13.1 0.7 copy-start.9
  13.8 0.8 copy-start.7
  24.9 14.7 %collective-permute-start.1 = (f32[440,128]{1,0:T(8,128)S(1)}, f32[440,128]{1,0:T(8,128)S(1)}, u32[]{:S(2)}, u32[]{:S(2)}) collective-permute-start(f32[440,128]{1,0:T(8,128)S(1)} %get-tuple-element.26.own), channel_id=1, source_target_pairs={{0,159},{1,0},{2,1},{3,2},{4,131},{5,4},{6,5},{7,6},{8,135},{9,8},... | collective-permute-start | bytes 675848 | tf_op jit(solution)/shard_map/ppermute | solution.py:508
  31.2 12.1 %collective-permute-start = (f32[440,128]{1,0:T(8,128)S(1)}, f32[440,128]{1,0:T(8,128)S(1)}, u32[]{:S(2)}, u32[]{:S(2)}) collective-permute-start(f32[440,128]{1,0:T(8,128)S(1)} %get-tuple-element.26.own), channel_id=1, source_target_pairs={{0,1},{1,2},{2,3},{3,132},{4,5},{5,6},{6,7},{7,136},{8,9},{9,10},{... | collective-permute-start | bytes 675848 | tf_op jit(solution)/shard_map/ppermute | solution.py:508
  31.2 12.1 %copy-start.6 = (f32[128,128]{1,0:T(8,128)S(1)}, f32[128,128]{1,0:T(8,128)}, u32[]{:S(2)}) copy-start(f32[128,128]{1,0:T(8,128)} %radiation.5) | copy-start | bytes 196612
  49.2 20.8 %collective-permute-start.3 = (f32[336,128]{1,0:T(8,128)S(1)}, f32[336,128]{1,0:T(8,128)S(1)}, u32[]{:S(2)}, u32[]{:S(2)}) collective-permute-start(f32[336,128]{1,0:T(8,128)S(1)} %get-tuple-element.27.own), channel_id=1, source_target_pairs={{0,159},{1,0},{2,1},{3,2},{4,131},{5,4},{6,5},{7,6},{8,135},{9,8},... | collective-permute-start | bytes 516104 | tf_op jit(solution)/shard_map/ppermute | solution.py:508
  54.4 15.6 %collective-permute-start.2 = (f32[336,128]{1,0:T(8,128)S(1)}, f32[336,128]{1,0:T(8,128)S(1)}, u32[]{:S(2)}, u32[]{:S(2)}) collective-permute-start(f32[336,128]{1,0:T(8,128)S(1)} %get-tuple-element.27.own), channel_id=1, source_target_pairs={{0,1},{1,2},{2,3},{3,132},{4,5},{5,6},{6,7},{7,136},{8,9},{9,10},{... | collective-permute-start | bytes 516104 | tf_op jit(solution)/shard_map/ppermute | solution.py:508
  54.4 11.8 %collective-permute-start.4 = (f32[168,128]{1,0:T(8,128)S(1)}, f32[168,128]{1,0:T(8,128)S(1)}, u32[]{:S(2)}, u32[]{:S(2)}) collective-permute-start(f32[168,128]{1,0:T(8,128)S(1)} %get-tuple-element.28.next_cot), channel_id=1, source_target_pairs={{0,1},{1,2},{2,3},{3,132},{4,5},{5,6},{6,7},{7,136},{8,9},{9,10},{... | collective-permute-start | bytes 258056 | tf_op jit(solution)/shard_map/ppermute | solution.py:508
  54.4 15.6 %collective-permute-start.5 = (f32[168,128]{1,0:T(8,128)S(1)}, f32[168,128]{1,0:T(8,128)S(1)}, u32[]{:S(2)}, u32[]{:S(2)}) collective-permute-start(f32[168,128]{1,0:T(8,128)S(1)} %get-tuple-element.29.prev_cot), channel_id=1, source_target_pairs={{0,159},{1,0},{2,1},{3,2},{4,131},{5,4},{6,5},{7,6},{8,135},{9,8},... | collective-permute-start | bytes 258056 | tf_op jit(solution)/shard_map/ppermute | solution.py:508
  62.2 16.6 %collective-permute-start.8 = (f32[288,128]{1,0:T(8,128)S(1)}, f32[288,128]{1,0:T(8,128)S(1)}, u32[]{:S(2)}, u32[]{:S(2)}) collective-permute-start(f32[288,128]{1,0:T(8,128)S(1)} %get-tuple-element.36), channel_id=1, source_target_pairs={{0,1},{1,2},{2,3},{3,132},{4,5},{5,6},{6,7},{7,136},{8,9},{9,10},{... | collective-permute-start | bytes 442376 | tf_op jit(solution)/shard_map/ppermute | solution.py:508
  66.2 12.6 %collective-permute-start.9 = (f32[288,128]{1,0:T(8,128)S(1)}, f32[288,128]{1,0:T(8,128)S(1)}, u32[]{:S(2)}, u32[]{:S(2)}) collective-permute-start(f32[288,128]{1,0:T(8,128)S(1)} %get-tuple-element.37), channel_id=1, source_target_pairs={{0,159},{1,0},{2,1},{3,2},{4,131},{5,4},{6,5},{7,6},{8,135},{9,8},... | collective-permute-start | bytes 442376 | tf_op jit(solution)/shard_map/ppermute | solution.py:508
  76.8 7.1 %collective-permute-start.7 = (f32[288,128]{1,0:T(8,128)S(1)}, f32[288,128]{1,0:T(8,128)S(1)}, u32[]{:S(2)}, u32[]{:S(2)}) collective-permute-start(f32[288,128]{1,0:T(8,128)S(1)} %get-tuple-element.34), channel_id=1, source_target_pairs={{0,159},{1,0},{2,1},{3,2},{4,131},{5,4},{6,5},{7,6},{8,135},{9,8},... | collective-permute-start | bytes 442376 | tf_op jit(solution)/shard_map/ppermute | solution.py:508
  78.8 10.3 %collective-permute-start.6 = (f32[288,128]{1,0:T(8,128)S(1)}, f32[288,128]{1,0:T(8,128)S(1)}, u32[]{:S(2)}, u32[]{:S(2)}) collective-permute-start(f32[288,128]{1,0:T(8,128)S(1)} %get-tuple-element.34), channel_id=1, source_target_pairs={{0,1},{1,2},{2,3},{3,132},{4,5},{5,6},{6,7},{7,136},{8,9},{9,10},{... | collective-permute-start | bytes 442376 | tf_op jit(solution)/shard_map/ppermute | solution.py:508
  101.0 21.5 %copy-start = (bf16[256,256]{1,0:T(8,128)(2,1)S(1)}, bf16[256,256]{1,0:T(8,128)(2,1)}, u32[]{:S(2)}) copy-start(bf16[256,256]{1,0:T(8,128)(2,1)} %constant.12.clone.chosen) | copy-start | bytes 393220

commit v3 on v2

--- a/solution.py
+++ b/solution.py
@@ -18,7 +18,7 @@
 BF16 = jnp.bfloat16
 HIGHEST = lax.Precision.HIGHEST
 CHUNK = 20
-GROUP_ONE, GROUP_TWO = 4, 4
+GROUP_ONE, GROUP_TWO = 8, 4
 GROUP_B2, GROUP_B1, GROUP_B0 = (4, 2), (4, 4), (4, 2)
 PACK = 16
 
@@ -45,6 +45,11 @@
         n = value.shape[0]
         place = pl.ds(self.at(x, y) + which, n, stride=8)
         self.ref[place, :] = self.ref[place, :] + value
+
+
+def repeat(count, body):
+    for i in range(count):
+        body(i, 0)
 
 
 def dot(a, b):
@@ -202,13 +207,13 @@
 
     def rim_x(i, carry):
         first = x_lo - 2 + i * rim_group
-        first = first + jnp.where(first < 0, 0, OWN_X)
+        first = first + (0 if first < 0 else OWN_X)
         xs = [first + j for j in range(rim_group)]
         backward_tiles(w, fields, lead, xs, y_lo, n, spread, direct, None, None)
         return carry
 
-    lax.fori_loop(0, OWN_X // own_group, own_x, 0)
-    lax.fori_loop(0, (x_hi - x_lo + 4 - OWN_X) // rim_group, rim_x, 0)
+    repeat(OWN_X // own_group, own_x)
+    repeat((x_hi - x_lo + 4 - OWN_X) // rim_group, rim_x)
 
 
 def adjoint_tiles(fields, lead, x, y, n, spread, direct):
@@ -243,8 +248,9 @@
 
 
 def pick(value, chosen):
-    high, middle, low = split_three(value)
-    return dot(high, chosen) + dot(middle, chosen) + dot(low, chosen)
+    count = value.shape[0]
+    parts = dot(jnp.concatenate(split_three(value), axis=0), chosen)
+    return parts[0:count] + parts[count : 2 * count] + parts[2 * count : 3 * count]
 
 
 def first_table():
@@ -258,28 +264,34 @@
     return table
 
 
-def pack_kernel(table, state, cot, fall, live, out, left):
-    left[0:96, 0:256] = state[...].reshape(96, 256)
-    left[0:96, 256:512] = cot[...].reshape(96, 256)
-    left[96:104, :] = jnp.zeros((8, 512), F32)
-    left[96:97, 0:256] = fall[...]
-    left[97:98, 0:256] = live[...].astype(F32)
-    parts = split_three(left[...])
+def pack_kernel(table, state, cot, fall, live, out, rates, left, given):
+    left[:, 0:256] = state[...].reshape(96, 256)
+    left[:, 256:512] = cot[...].reshape(96, 256)
+    given[...] = jnp.zeros(given.shape, F32)
+    given[0:1, :] = fall[...]
+    given[1:2, :] = live[...].astype(F32)
     turn = 32 * turned_half(lax.axis_index("gx"))
     place = lax.broadcasted_iota(jnp.int32, (512, LEV), 0) ^ turn
+    parts = jnp.concatenate(split_three(left[...]), axis=0)
     for block in range(GZ):
         chosen = jnp.where(place == table[block : block + 1, :], 1.0, 0.0).astype(BF16)
-        out[block] = dot(parts[0], chosen) + dot(parts[1], chosen) + dot(parts[2], chosen)
-
-
-def turn_kernel(got, own, next_cot, prev_cot):
+        wide = dot(parts, chosen)
+        out[block] = wide[0:96] + wide[96:192] + wide[192:288]
+    mine = table[pl.ds(lax.axis_index("gz"), 1), :]
+    chosen = jnp.where(place[0:256] == mine, 1.0, 0.0).astype(BF16)
+    rates[...] = pick(given[...], chosen)[0:8]
+
+
+def turn_kernel(got, rates, to_next, to_prev):
     for which in range(NF):
         blocks = [got[k, which * 16 : which * 16 + 16, :] for k in range(GZ)]
         turned = jnp.concatenate(blocks, axis=0).T
-        own[which * 72 : which * 72 + 72, :] = turned[0:72]
-        next_cot[which * 28 : which * 28 + 28, :] = turned[100:128]
-        prev_cot[which * 28 : which * 28 + 28, :] = turned[72:100]
-    own[432:440, :] = got[0, 96:104, :]
+        to_next[which * 72 : which * 72 + 72, :] = turned[0:72]
+        to_prev[which * 72 : which * 72 + 72, :] = turned[0:72]
+        to_next[432 + which * 28 : 460 + which * 28, :] = turned[100:128]
+        to_prev[432 + which * 28 : 460 + which * 28, :] = turned[72:100]
+    to_next[600:608, :] = rates[...]
+    to_prev[600:608, :] = rates[...]
 
 
 def forward_kernel(
@@ -295,8 +307,8 @@
             columns = source[which * 72 : which * 72 + 72, :]
             state[pl.ds(place * 576 + which, 72, stride=8), :] = columns
         rows = pl.ds(place * 72, 72)
-        fall[rows, :] = jnp.broadcast_to(source[432:433, :], (LEV, LEV)).T[0:72]
-        live[rows, :] = jnp.broadcast_to(source[433:434, :], (LEV, LEV)).T[0:72]
+        fall[rows, :] = jnp.broadcast_to(source[600:601, :], (LEV, LEV)).T[0:72]
+        live[rows, :] = jnp.broadcast_to(source[601:602, :], (LEV, LEV)).T[0:72]
     s_zero = Patch(state, -4, 12, -5, 18)
     s_one = Patch(one, -2, 8, -4, 16)
     s_two = Patch(two, 0, 4, -3, 14)
@@ -307,7 +319,7 @@
             s_one.put(x, -4, center + STEP * total)
         return carry
 
-    lax.fori_loop(0, 8 // GROUP_ONE, stage_one, 0)
+    repeat(8 // GROUP_ONE, stage_one)
     xs = range(-2, 6)
     column_terms(s_zero, xs, -4, 16, fall, live, radiation, packs, False)
     add_columns(s_one, xs, -4, 16, packs, STEP)
@@ -318,7 +330,7 @@
             s_two.put(x, -3, 0.75 * s_zero.get(x, -3, 14) + 0.25 * (center + STEP * total))
         return carry
 
-    lax.fori_loop(0, 4 // GROUP_TWO, stage_two, 0)
+    repeat(4 // GROUP_TWO, stage_two)
     xs = range(4)
     column_terms(s_one, xs, -3, 14, fall, live, radiation, packs, False)
     add_columns(s_two, xs, -3, 14, packs, 0.25 * STEP)
@@ -346,7 +358,7 @@
     lead[...] = jnp.zeros(lead.shape, F32)
     for place, source in enumerate((cot_before, prev_cot, next_cot, cot_after)):
         for which in range(NF):
-            columns = source[which * 28 : which * 28 + 28, :]
+            columns = source[432 + which * 28 : 460 + which * 28, :]
             lead[pl.ds(place * 224 + which, 28, stride=8), :] = (2.0 / 3.0) * columns
     sums[...] = jnp.zeros(sums.shape, F32)
     s_zero = Patch(state, -4, 12, -5, 18)
@@ -371,7 +383,7 @@
         c_two.put(x, -2, center + STEP * result)
         return carry
 
-    lax.fori_loop(0, 4, gather, 0)
+    repeat(4, gather)
     column_terms(lam, xs, -2, 12, fall, live, radiation, packs, True)
     add_columns(c_two, xs, -2, 12, packs, STEP)
     base = Patch(known, 0, 4, 0, 8)
@@ -416,7 +428,7 @@
         lam_zero.put(x, -1, center + STEP * result)
         return carry
 
-    lax.fori_loop(0, 8, gather_one, 0)
+    repeat(8, gather_one)
     xs = range(-2, 6)
     column_terms(lam_one, xs, -1, 10, fall, live, radiation, packs, True)
     add_columns(lam_zero, xs, -1, 10, packs, STEP)
@@ -431,7 +443,7 @@
         final.put(x, 0, base.get(x, 0, 8) + center + STEP * result)
         return carry
 
-    lax.fori_loop(0, 4, gather_zero, 0)
+    repeat(4, gather_zero)
     xs = range(4)
     column_terms(lam_zero, xs, 0, 8, fall, live, radiation, packs, True)
     add_columns(final, xs, 0, 8, packs, STEP)
@@ -456,19 +468,26 @@
     return chosen
 
 
-def unpack_kernel(got, chosen, new_state, grad, chunk):
+def sum_kernel(got, out):
     total = got[0, 48:68, :]
     for block in range(1, GZ):
         total = total + got[block, 48:68, :]
-    chunk[...] = total
+    for slab in range(GX):
+        out[slab] = total
+
+
+def unpack_kernel(got, chosen, new_state, grad):
     turn = 4 * turned_half(lax.axis_index("gx"))
-    for index, out in enumerate((new_state, grad)):
-        for half in range(2):
-            lanes = slice((2 * index + half) * 32, (2 * index + half + 1) * 32)
-            row = jnp.concatenate([got[k ^ turn, 0:48, lanes] for k in range(GZ)], axis=1)
-            placed = pick(row, chosen[...])
-            for pair in range(3):
-                out[2 * pair + half] = placed[pair * 16 : pair * 16 + 16]
+    rows = []
+    for part in range(4):
+        lanes = slice(part * 32, part * 32 + 32)
+        rows.append(jnp.concatenate([got[k ^ turn, 0:48, lanes] for k in range(GZ)], axis=1))
+    placed = pick(jnp.concatenate(rows, axis=0), chosen[...])
+    for part in range(4):
+        for pair in range(3):
+            first = part * 48 + pair * 16
+            out = (new_state, grad)[part // 2]
+            out[2 * pair + part % 2] = placed[first : first + 16]
 
 
 def finish_kernel(got, grad_in, grad_mid, grad_out):
@@ -517,10 +536,10 @@
     bundle = jnp.concatenate([w_mid, w_mid.T, in_wide.T, out_wide], axis=0)
     weights = (bundle, in_wide, out_wide.T, radiation)
 
-    (packed,) = call(
+    packed, rates = call(
         pack_kernel,
-        [(GZ, 104, LEV)],
-        [(104, 512)],
+        [(GZ, 96, LEV), (8, LEV)],
+        [(96, 512), (16, 256)],
         jnp.asarray(first_table()),
         state,
         state_cot,
@@ -528,9 +547,8 @@
         active.reshape(1, 256),
     )
     got = lax.all_to_all(packed, "gz", 0, 0)
-    own, next_cot, prev_cot = call(turn_kernel, [(440, LEV), (168, LEV), (168, LEV)], [], got)
-    before, after = passed_along(own, 1), passed_along(own, -1)
-    cot_before, cot_after = passed_along(next_cot, 1), passed_along(prev_cot, -1)
+    own, own_prev = call(turn_kernel, [(608, LEV), (608, LEV)], [], got, rates)
+    before, after = passed_along(own, 1), passed_along(own_prev, -1)
     zero, fall, live, one, two, next_one, prev_one = call(
         forward_kernel,
         [(1728, LEV), (216, LEV), (216, LEV), (1024, LEV), (336, LEV), (288, LEV), (288, LEV)],
@@ -550,10 +568,10 @@
         two,
         two_before,
         two_after,
-        cot_before,
-        prev_cot,
-        next_cot,
-        cot_after,
+        before,
+        own_prev,
+        own,
+        after,
         *weights,
         zero,
         fall,
@@ -583,14 +601,15 @@
         giga=20,
     )
     got = lax.all_to_all(sent, "gz", 0, 0)
-    new_state, grad_state, chunk = call(
+    (chunks,) = call(sum_kernel, [(GX, CHUNK, LEV)], [], got)
+    new_state, grad_state = call(
         unpack_kernel,
-        [(NF, 16, 256), (NF, 16, 256), (CHUNK, LEV)],
+        [(NF, 16, 256), (NF, 16, 256)],
         [],
         got,
         jnp.asarray(last_table(), BF16),
     )
-    spread = lax.all_to_all(jnp.broadcast_to(chunk, (GX, CHUNK, LEV)), "gx", 0, 0)
+    spread = lax.all_to_all(chunks, "gx", 0, 0)
     added = jnp.sum(spread, axis=0)
     totals = lax.all_to_all(jnp.broadcast_to(added, (GZ, CHUNK, LEV)), "gz", 0, 0)
     grads = call(finish_kernel, [(128, 2 * NF), (128, LEV), (NF, LEV)], [], totals)

time: 155 us -> 150 us (0.968)
  blocking collectives: 50.7 us -> 42.1 us
  starting transfers between devices: 32.6 us -> 36.5 us
  Pallas kernels: 28.2 us -> 24.5 us
  waiting for transfers between devices: 36.4 us -> 39.6 us
    all_to_all x2 -> x1, blocking collectives: 29.2 us -> 17.6 us  [on_device(): spread = lax.all_to_all(chunks, 'gx', 0, 0)]
    all_to_all x0 -> x1, starting transfers between devices: none -> 6.34 us  [on_device(): lax.all_to_all(jnp.broadcast_to(added, (GZ, CHUNK, LEV)), 'gz', 0, 0)]
    all_to_all x0 -> x1, waiting for transfers between devices: none -> 4.39 us  [on_device(): lax.all_to_all(jnp.broadcast_to(added, (GZ, CHUNK, LEV)), 'gz', 0, 0)]
    pallas_call x7 -> x8, Pallas kernels: 28.2 us -> 24.5 us  [call(): pl.pallas_call(kernel, out_shape=[jax.ShapeDtypeStruct(shape, F32) for sh...]
    all_to_all x1, blocking collectives: 21.5 us -> 24.5 us  [on_device(): got = lax.all_to_all(sent, 'gz', 0, 0)]
    ppermute x10 -> x8, starting transfers between devices: 25 us -> 22.6 us  [passed_along(): return lax.ppermute(shard, ('gz', 'gx'), pairs)]
    ppermute x10 -> x8, waiting for transfers between devices: 26.3 us -> 24.3 us  [passed_along(): return lax.ppermute(shard, ('gz', 'gx'), pairs)]
  transfers between devices with their start and end apart: 11 -> 10, of which waited for: 6 -> 7; matrix products, arithmetic and copies ran while one was open for 0% -> 0% of each run, Pallas kernels for 4% -> 4%
where the time goes in v3:
time: 150 us
  blocking collectives  42.1 us (28%)
  waiting for transfers between devices  39.6 us (26%)
  starting transfers between devices  36.5 us (24%)
  Pallas kernels  24.5 us (16%)
  local copies, waits for them, and re-layouts  6.01 us (4%)
    all_to_all x1, blocking collectives, on_device(): got = lax.all_to_all(sent, 'gz', 0, 0)  24.5 us
    pallas_call x8, Pallas kernels, call(): pl.pallas_call(kernel, out_shape=[jax.ShapeDtypeStruct(shape, F32) for sh...  24.5 us
    ppermute x8, waiting for transfers between devices, passed_along(): return lax.ppermute(shard, ('gz', 'gx'), pairs)  24.3 us
    ppermute x8, starting transfers between devices, passed_along(): return lax.ppermute(shard, ('gz', 'gx'), pairs)  22.6 us
    all_to_all x1, blocking collectives, on_device(): spread = lax.all_to_all(chunks, 'gx', 0, 0)  17.6 us
    all_to_all x1, waiting for transfers between devices, on_device(): got = lax.all_to_all(packed, 'gz', 0, 0)  11 us
    all_to_all x1, starting transfers between devices, on_device(): got = lax.all_to_all(packed, 'gz', 0, 0)  7.53 us
    all_to_all x1, starting transfers between devices, on_device(): lax.all_to_all(jnp.broadcast_to(added, (GZ, CHUNK, LEV)), 'gz', 0, 0)  6.34 us
  transfers between devices with their start and end apart: 10, of which 7 were waited for; matrix products, arithmetic and copies ran while one was open for 0% of the time, Pallas kernels for 4%

profile of v3, /device:TPU:1, one launch (start us, length us, event | category | flops | bytes accessed | tf_op | source)
XLA Modules:
  0.0 149.5 jit_solution(8714404358293468298)
XLA Ops:
  0.6 0.0 copy-start.3
  0.7 0.7 copy-done.3
  1.3 0.0 copy-done.5
  1.3 0.0 copy-done.4
  1.3 0.9 copy-done.1
  2.2 0.9 copy-done.2
  3.1 1.5 %shard_map.137 = (f32[8,96,128]{2,1,0:T(8,128)}, f32[8,128]{1,0:T(8,128)S(1)}) custom-call(s32[8,128]{1,0:T(8,128)S(1)} %copy-done.3, f32[6,16,256]{2,1,0:T(8,128)S(1)} %copy-done.1, f32[6,16,256]{2,1,0:T(8,128)S(1)} %copy-done.2, f32[1,256]{1,0:T(1,128)S(1)} %bitcast.7, s32[1,256]{1,0:T(1,128)S(1)} %bitcast.8), custom_call_target="tpu_custom_call" | custom-call | tf_op jit(solution)/shard_map/pallas_call | solution.py:503
  4.7 7.5 %all-to-all-start = ((f32[8,96,128]{2,1,0:T(8,128)}), f32[8,96,128]{2,1,0:T(8,128)S(1)}, u32[]{:S(2)}, u32[]{:S(2)}) async-start(f32[8,96,128]{2,1,0:T(8,128)} %get-tuple-element.26), calls=%async_computation | async-start | bytes 786432 | tf_op jit(solution)/shard_map/all_to_all | solution.py:549
  12.2 0.6 copy-done.10
  12.9 0.1 slice_select_fusion
  12.9 11.0 %all-to-all-done.got = f32[8,96,128]{2,1,0:T(8,128)S(1)} async-done(((f32[8,96,128]{2,1,0:T(8,128)}), f32[8,96,128]{2,1,0:T(8,128)S(1)}, u32[]{:S(2)}, u32[]{:S(2)}) %all-to-all-start) | async-done | bytes 393248 | tf_op jit(solution)/shard_map/all_to_all | solution.py:549
  23.9 0.2 shard_map.138
  24.1 6.3 %collective-permute-start.1 = (f32[608,128]{1,0:T(8,128)S(1)}, f32[608,128]{1,0:T(8,128)S(1)}, u32[]{:S(2)}, u32[]{:S(2)}) collective-permute-start(f32[608,128]{1,0:T(8,128)S(1)} %get-tuple-element.29.prev_cot), channel_id=1, source_target_pairs={{0,159},{1,0},{2,1},{3,2},{4,131},{5,4},{6,5},{7,6},{8,135},{9,8},... | collective-permute-start | bytes 933896 | tf_op jit(solution)/shard_map/ppermute | solution.py:527
  30.3 0.0 collective-permute-start
  30.3 0.0 copy-start.9
  30.3 0.1 copy.25.w_in
  30.5 0.5 copy-done.9
  31.0 0.1 copy.23
  31.1 0.1 copy.29
  31.2 0.5 copy-done.7
  31.8 0.1 copy.22
  31.9 0.0 copy-start.6
  31.9 10.7 %collective-permute-done.1.after.cot_after = f32[608,128]{1,0:T(8,128)S(1)} collective-permute-done((f32[608,128]{1,0:T(8,128)S(1)}, f32[608,128]{1,0:T(8,128)S(1)}, u32[]{:S(2)}, u32[]{:S(2)}) %collective-permute-start.1) | collective-permute-done | bytes 311328 | tf_op jit(solution)/shard_map/ppermute | solution.py:527
  42.6 1.6 %collective-permute-done.before.cot_before = f32[608,128]{1,0:T(8,128)S(1)} collective-permute-done((f32[608,128]{1,0:T(8,128)S(1)}, f32[608,128]{1,0:T(8,128)S(1)}, u32[]{:S(2)}, u32[]{:S(2)}) %collective-permute-start) | collective-permute-done | bytes 311328 | tf_op jit(solution)/shard_map/ppermute | solution.py:527
  44.2 5.4 %shard_map.139 = (f32[1728,128]{1,0:T(8,128)S(1)}, f32[216,128]{1,0:T(8,128)S(1)}, f32[216,128]{1,0:T(8,128)S(1)}, f32[1024,128]{1,0:T(8,128)S(1)}, f32[336,128]...) custom-call(f32[608,128]{1,0:T(8,128)S(1)} %get-tuple-element.28.own.next_cot, ...), custom_call_target="tpu_custom_call" | custom-call | flops 12000000000 | bytes 1000000 | tf_op jit(solution)/shard_map/pallas_call | solution.py:503
  49.7 7.0 %collective-permute-start.3 = (f32[336,128]{1,0:T(8,128)S(1)}, f32[336,128]{1,0:T(8,128)S(1)}, u32[]{:S(2)}, u32[]{:S(2)}) collective-permute-start(f32[336,128]{1,0:T(8,128)S(1)} %get-tuple-element.30.own), channel_id=1, source_target_pairs={{0,159},{1,0},{2,1},{3,2},{4,131},{5,4},{6,5},{7,6},{8,135},{9,8},... | collective-permute-start | bytes 516104 | tf_op jit(solution)/shard_map/ppermute | solution.py:527
  56.7 0.0 collective-permute-start.2
  56.7 0.0 collective-permute-start.6
  56.7 7.8 %collective-permute-start.7 = (f32[288,128]{1,0:T(8,128)S(1)}, f32[288,128]{1,0:T(8,128)S(1)}, u32[]{:S(2)}, u32[]{:S(2)}) collective-permute-start(f32[288,128]{1,0:T(8,128)S(1)} %get-tuple-element.38), channel_id=1, source_target_pairs={{0,159},{1,0},{2,1},{3,2},{4,131},{5,4},{6,5},{7,6},{8,135},{9,8},... | collective-permute-start | bytes 442376 | tf_op jit(solution)/shard_map/ppermute | solution.py:527
  64.5 0.0 collective-permute-done.3.after
  64.5 2.8 %collective-permute-done.2.before = f32[336,128]{1,0:T(8,128)S(1)} collective-permute-done((f32[336,128]{1,0:T(8,128)S(1)}, f32[336,128]{1,0:T(8,128)S(1)}, u32[]{:S(2)}, u32[]{:S(2)}) %collective-permute-start.2) | collective-permute-done | bytes 172064 | tf_op jit(solution)/shard_map/ppermute | solution.py:527
  67.3 5.6 %shard_map.140 = (f32[384,128]{1,0:T(8,128)S(1)}, f32[288,128]{1,0:T(8,128)S(1)}, f32[256,128]{1,0:T(8,128)S(1)}, f32[256,128]{1,0:T(8,128)S(1)}, f32[160,128]{1,0:T(8,128)S(1)}) custom-call(f32[336,128]{1,0:T(8,128)S(1)} %get-tuple-element.30.own, f32[336,128]{1,0:T(8,128)S(1)} %collective-permute-done.2.before, ...), custom_call_target="tpu_custom_call" | custom-call | flops 11000000512 | bytes 1000000 | tf_op jit(solution)/shard_map/pallas_call | solution.py:503
  72.9 0.1 collective-permute-start.5
  73.0 1.5 collective-permute-start.4
  74.4 0.0 collective-permute-done.6.one_before
  74.4 0.0 collective-permute-done.7.one_after
  74.4 2.5 %collective-permute-done.5.after = f32[288,128]{1,0:T(8,128)S(1)} collective-permute-done((f32[288,128]{1,0:T(8,128)S(1)}, f32[288,128]{1,0:T(8,128)S(1)}, u32[]{:S(2)}, u32[]{:S(2)}) %collective-permute-start.5) | collective-permute-done | bytes 147488 | tf_op jit(solution)/shard_map/ppermute | solution.py:527
  77.0 6.6 %collective-permute-done.4.before = f32[288,128]{1,0:T(8,128)S(1)} collective-permute-done((f32[288,128]{1,0:T(8,128)S(1)}, f32[288,128]{1,0:T(8,128)S(1)}, u32[]{:S(2)}, u32[]{:S(2)}) %collective-permute-start.4) | collective-permute-done | bytes 147488 | tf_op jit(solution)/shard_map/ppermute | solution.py:527
  83.6 10.0 %shard_map.141 = f32[8,68,128]{2,1,0:T(8,128)S(1)} custom-call(f32[384,128]{1,0:T(8,128)S(1)} %get-tuple-element.34.own, f32[288,128]{1,0:T(8,128)S(1)} %collective-permute-done.4.before, f32[288,128]{1,0:T(8,128)S(1)} %collective-permute-done.5.after, f32[1024,128]{1,0:T(8,128)S(1)} %get-tuple-element.36.one, ...), custom_call_target="tpu_custom_call" | custom-call | flops 20000000000 | bytes 1000000 | tf_op jit(solution)/shard_map/pallas_call | solution.py:503
  93.6 24.5 %all_to_all.20.got = f32[8,68,128]{2,1,0:T(8,128)S(1)} all-to-all(f32[8,68,128]{2,1,0:T(8,128)S(1)} %shard_map.141), channel_id=1, replica_groups=mesh['gz'=8,'gx'=32] {'gz'}, dimensions={0} | all-to-all | bytes 557056 | tf_op jit(solution)/shard_map/all_to_all | solution.py:603
  118.1 17.6 %all_to_all.21 = f32[32,20,128]{2,1,0:T(8,128)S(1)} all-to-all(f32[32,20,128]{2,1,0:T(8,128)S(1)} %shard_map.143), channel_id=1, replica_groups=mesh['gz'=8,'gx'=32] {'gx'}, dimensions={0} | all-to-all | bytes 655360 | tf_op jit(solution)/shard_map/all_to_all | solution.py:612
  135.7 0.0 copy-start
  135.7 0.6 broadcast_in_dim.3
  136.4 6.3 %all-to-all-start.3 = ((f32[8,20,128]{2,1,0:T(8,128)}), f32[8,20,128]{2,1,0:T(8,128)S(1)}, u32[]{:S(2)}, u32[]{:S(2)}) async-start(f32[8,20,128]{2,1,0:T(8,128)} %broadcast_in_dim.3), calls=%async_computation.3 | async-start | bytes 196608 | tf_op jit(solution)/shard_map/all_to_all | solution.py:614
  142.7 1.1 shard_map.142
  143.8 4.4 %all-to-all-done.3.got = f32[8,20,128]{2,1,0:T(8,128)S(1)} async-done(((f32[8,20,128]{2,1,0:T(8,128)}), f32[8,20,128]{2,1,0:T(8,128)S(1)}, u32[]{:S(2)}, u32[]{:S(2)}) %all-to-all-start.3) | async-done | bytes 81952 | tf_op jit(solution)/shard_map/all_to_all | solution.py:614
  148.2 0.6 shard_map.144
  148.8 0.7 copy.28
  (17 shorter events, 0.1 us)
Async XLA Ops:
  0.6 0.7 copy-start.3
  0.6 0.7 copy-start.5
  0.7 0.7 copy-start.4
  1.3 0.9 copy-start.1
  2.2 0.9 copy-start.2
  4.7 7.5 %copy-start.8 = (bf16[128,12]{0,1:T(8,128)(2,1)S(1)}, bf16[128,12]{0,1:T(8,128)(2,1)}, u32[]{:S(2)}) copy-start(bf16[128,12]{0,1:T(8,128)(2,1)} %param.12) | copy-start | bytes 9220
  4.7 19.2 %all-to-all-start = ((f32[8,96,128]{2,1,0:T(8,128)}), f32[8,96,128]{2,1,0:T(8,128)S(1)}, u32[]{:S(2)}, u32[]{:S(2)}) async-start(f32[8,96,128]{2,1,0:T(8,128)} %get-tuple-element.26), calls=%async_computation | async-start | bytes 786432 | tf_op jit(solution)/shard_map/all_to_all | solution.py:549
  12.2 0.7 copy-start.10
  24.1 18.6 %collective-permute-start.1 = (f32[608,128]{1,0:T(8,128)S(1)}, f32[608,128]{1,0:T(8,128)S(1)}, u32[]{:S(2)}, u32[]{:S(2)}) collective-permute-start(f32[608,128]{1,0:T(8,128)S(1)} %get-tuple-element.29.prev_cot), channel_id=1, source_target_pairs={{0,159},{1,0},{2,1},{3,2},{4,131},{5,4},{6,5},{7,6},{8,135},{9,8},... | collective-permute-start | bytes 933896 | tf_op jit(solution)/shard_map/ppermute | solution.py:527
  30.3 13.9 %collective-permute-start = (f32[608,128]{1,0:T(8,128)S(1)}, f32[608,128]{1,0:T(8,128)S(1)}, u32[]{:S(2)}, u32[]{:S(2)}) collective-permute-start(f32[608,128]{1,0:T(8,128)S(1)} %get-tuple-element.28.own.next_cot), channel_id=1, source_target_pairs={{0,1},{1,2},{2,3},{3,132},{4,5},{5,6},{6,7},{7,136},{8,9},{9,10},{... | collective-permute-start | bytes 933896 | tf_op jit(solution)/shard_map/ppermute | solution.py:527
  30.3 0.7 copy-start.9
  31.0 0.8 copy-start.7
  31.9 12.3 %copy-start.6 = (f32[128,128]{1,0:T(8,128)S(1)}, f32[128,128]{1,0:T(8,128)}, u32[]{:S(2)}) copy-start(f32[128,128]{1,0:T(8,128)} %radiation.5) | copy-start | bytes 196612
  49.7 14.8 %collective-permute-start.3 = (f32[336,128]{1,0:T(8,128)S(1)}, f32[336,128]{1,0:T(8,128)S(1)}, u32[]{:S(2)}, u32[]{:S(2)}) collective-permute-start(f32[336,128]{1,0:T(8,128)S(1)} %get-tuple-element.30.own), channel_id=1, source_target_pairs={{0,159},{1,0},{2,1},{3,2},{4,131},{5,4},{6,5},{7,6},{8,135},{9,8},... | collective-permute-start | bytes 516104 | tf_op jit(solution)/shard_map/ppermute | solution.py:527
  56.7 10.6 %collective-permute-start.2 = (f32[336,128]{1,0:T(8,128)S(1)}, f32[336,128]{1,0:T(8,128)S(1)}, u32[]{:S(2)}, u32[]{:S(2)}) collective-permute-start(f32[336,128]{1,0:T(8,128)S(1)} %get-tuple-element.30.own), channel_id=1, source_target_pairs={{0,1},{1,2},{2,3},{3,132},{4,5},{5,6},{6,7},{7,136},{8,9},{9,10},{... | collective-permute-start | bytes 516104 | tf_op jit(solution)/shard_map/ppermute | solution.py:527
  56.7 17.8 %collective-permute-start.6 = (f32[288,128]{1,0:T(8,128)S(1)}, f32[288,128]{1,0:T(8,128)S(1)}, u32[]{:S(2)}, u32[]{:S(2)}) collective-permute-start(f32[288,128]{1,0:T(8,128)S(1)} %get-tuple-element.37), channel_id=1, source_target_pairs={{0,1},{1,2},{2,3},{3,132},{4,5},{5,6},{6,7},{7,136},{8,9},{9,10},{... | collective-permute-start | bytes 442376 | tf_op jit(solution)/shard_map/ppermute | solution.py:527
  56.7 17.8 %collective-permute-start.7 = (f32[288,128]{1,0:T(8,128)S(1)}, f32[288,128]{1,0:T(8,128)S(1)}, u32[]{:S(2)}, u32[]{:S(2)}) collective-permute-start(f32[288,128]{1,0:T(8,128)S(1)} %get-tuple-element.38), channel_id=1, source_target_pairs={{0,159},{1,0},{2,1},{3,2},{4,131},{5,4},{6,5},{7,6},{8,135},{9,8},... | collective-permute-start | bytes 442376 | tf_op jit(solution)/shard_map/ppermute | solution.py:527
  72.9 4.1 %collective-permute-start.5 = (f32[288,128]{1,0:T(8,128)S(1)}, f32[288,128]{1,0:T(8,128)S(1)}, u32[]{:S(2)}, u32[]{:S(2)}) collective-permute-start(f32[288,128]{1,0:T(8,128)S(1)} %get-tuple-element.35), channel_id=1, source_target_pairs={{0,159},{1,0},{2,1},{3,2},{4,131},{5,4},{6,5},{7,6},{8,135},{9,8},... | collective-permute-start | bytes 442376 | tf_op jit(solution)/shard_map/ppermute | solution.py:527
  73.0 10.6 %collective-permute-start.4 = (f32[288,128]{1,0:T(8,128)S(1)}, f32[288,128]{1,0:T(8,128)S(1)}, u32[]{:S(2)}, u32[]{:S(2)}) collective-permute-start(f32[288,128]{1,0:T(8,128)S(1)} %get-tuple-element.35), channel_id=1, source_target_pairs={{0,1},{1,2},{2,3},{3,132},{4,5},{5,6},{6,7},{7,136},{8,9},{9,10},{... | collective-permute-start | bytes 442376 | tf_op jit(solution)/shard_map/ppermute | solution.py:527
  135.7 7.0 %copy-start = (bf16[256,256]{1,0:T(8,128)(2,1)S(1)}, bf16[256,256]{1,0:T(8,128)(2,1)}, u32[]{:S(2)}) copy-start(bf16[256,256]{1,0:T(8,128)(2,1)} %constant.12.clone.chosen) | copy-start | bytes 393220
  136.4 11.8 %all-to-all-start.3 = ((f32[8,20,128]{2,1,0:T(8,128)}), f32[8,20,128]{2,1,0:T(8,128)S(1)}, u32[]{:S(2)}, u32[]{:S(2)}) async-start(f32[8,20,128]{2,1,0:T(8,128)} %broadcast_in_dim.3), calls=%async_computation.3 | async-start | bytes 196608 | tf_op jit(solution)/shard_map/all_to_all | solution.py:614

commit v4 on v3

--- a/solution.py
+++ b/solution.py
@@ -472,8 +472,8 @@
     total = got[0, 48:68, :]
     for block in range(1, GZ):
         total = total + got[block, 48:68, :]
-    for slab in range(GX):
-        out[slab] = total
+    for other in range(out.shape[0]):
+        out[other] = total
 
 
 def unpack_kernel(got, chosen, new_state, grad):
@@ -491,7 +491,7 @@
 
 
 def finish_kernel(got, grad_in, grad_mid, grad_out):
-    total = got[...].reshape(GZ * CHUNK, LEV)
+    total = (got[0:GZ] + got[GZ : 2 * GZ]).reshape(GZ * CHUNK, LEV)
     grad_mid[...] = total[0:128]
     rows = [total[128:134], total[136:142], jnp.zeros((116, LEV), F32)]
     grad_in[...] = jnp.concatenate(rows, axis=0).T[:, 0:12]
@@ -601,7 +601,7 @@
         giga=20,
     )
     got = lax.all_to_all(sent, "gz", 0, 0)
-    (chunks,) = call(sum_kernel, [(GX, CHUNK, LEV)], [], got)
+    (chunks,) = call(sum_kernel, [(16, CHUNK, LEV)], [], got)
     new_state, grad_state = call(
         unpack_kernel,
         [(NF, 16, 256), (NF, 16, 256)],
@@ -609,9 +609,15 @@
         got,
         jnp.asarray(last_table(), BF16),
     )
-    spread = lax.all_to_all(chunks, "gx", 0, 0)
-    added = jnp.sum(spread, axis=0)
-    totals = lax.all_to_all(jnp.broadcast_to(added, (GZ, CHUNK, LEV)), "gz", 0, 0)
+    level = [[8 * x + 4 * half + y for x in range(4) for y in range(4)] for half in range(2)]
+    line = [
+        [block * GX + 8 * x + 4 * half + y for half in range(2) for block in range(GZ)]
+        for x in range(4)
+        for y in range(4)
+    ]
+    added = jnp.sum(lax.all_to_all(chunks, "gx", 0, 0, axis_index_groups=level), axis=0)
+    added = jnp.broadcast_to(added, (16, CHUNK, LEV))
+    totals = lax.all_to_all(added, ("gz", "gx"), 0, 0, axis_index_groups=line)
     grads = call(finish_kernel, [(128, 2 * NF), (128, LEV), (NF, LEV)], [], totals)
     return (new_state, grad_state, *grads)
 

time: 150 us -> 146 us (0.973)
  blocking collectives: 42.1 us -> 34 us
  waiting for transfers between devices: 39.6 us -> 44.5 us
    all_to_all x1, blocking collectives: 17.6 us -> 9.55 us  [on_device(): lax.all_to_all(chunks, 'gx', 0, 0, axis_index_groups=level)]
    all_to_all x1, waiting for transfers between devices: 4.39 us -> 9.29 us  [on_device(): totals = lax.all_to_all(added, ('gz', 'gx'), 0, 0, axis_index_groups=line)]
  transfers between devices with their start and end apart: 10 -> 10, of which waited for: 7 -> 7; matrix products, arithmetic and copies ran while one was open for 0% -> 0% of each run, Pallas kernels for 4% -> 5%
where the time goes in v4:
time: 146 us; the launch traced here: 145 us
  waiting for transfers between devices  44.5 us (30%)
  starting transfers between devices  35.4 us (24%)
  blocking collectives  34 us (23%)
  Pallas kernels  24.4 us (17%)
  local copies, waits for them, and re-layouts  6.06 us (4%)
    all_to_all x1, blocking collectives, on_device(): got = lax.all_to_all(sent, 'gz', 0, 0)  24.5 us
    pallas_call x8, Pallas kernels, call(): pl.pallas_call(kernel, out_shape=[jax.ShapeDtypeStruct(shape, F32) for sh...  24.4 us
    ppermute x8, waiting for transfers between devices, passed_along(): return lax.ppermute(shard, ('gz', 'gx'), pairs)  24.3 us
    ppermute x8, starting transfers between devices, passed_along(): return lax.ppermute(shard, ('gz', 'gx'), pairs)  22.6 us
    all_to_all x1, waiting for transfers between devices, on_device(): got = lax.all_to_all(packed, 'gz', 0, 0)  11 us
    all_to_all x1, blocking collectives, on_device(): lax.all_to_all(chunks, 'gx', 0, 0, axis_index_groups=level)  9.55 us
    all_to_all x1, waiting for transfers between devices, on_device(): totals = lax.all_to_all(added, ('gz', 'gx'), 0, 0, axis_index_groups=line)  9.29 us
    all_to_all x1, starting transfers between devices, on_device(): got = lax.all_to_all(packed, 'gz', 0, 0)  7.53 us
  transfers between devices with their start and end apart: 10, of which 7 were waited for; matrix products, arithmetic and copies ran while one was open for 0% of the time, Pallas kernels for 5%

profile of v4, /device:TPU:1, one launch (start us, length us, event | category | flops | bytes accessed | tf_op | source)
XLA Modules:
  0.0 145.3 jit_solution(5185845476950038522)
XLA Ops:
  0.6 0.0 copy-start.3
  0.7 0.7 copy-done.3
  1.3 0.0 copy-done.5
  1.3 0.0 copy-done.4
  1.3 0.9 copy-done.1
  2.2 0.9 copy-done.2
  3.1 1.5 %shard_map.137 = (f32[8,96,128]{2,1,0:T(8,128)}, f32[8,128]{1,0:T(8,128)S(1)}) custom-call(s32[8,128]{1,0:T(8,128)S(1)} %copy-done.3, f32[6,16,256]{2,1,0:T(8,128)S(1)} %copy-done.1, f32[6,16,256]{2,1,0:T(8,128)S(1)} %copy-done.2, f32[1,256]{1,0:T(1,128)S(1)} %bitcast.7, s32[1,256]{1,0:T(1,128)S(1)} %bitcast.8), custom_call_target="tpu_custom_call" | custom-call | tf_op jit(solution)/shard_map/pallas_call | solution.py:503
  4.7 7.5 %all-to-all-start = ((f32[8,96,128]{2,1,0:T(8,128)}), f32[8,96,128]{2,1,0:T(8,128)S(1)}, u32[]{:S(2)}, u32[]{:S(2)}) async-start(f32[8,96,128]{2,1,0:T(8,128)} %get-tuple-element.26), calls=%async_computation | async-start | bytes 786432 | tf_op jit(solution)/shard_map/all_to_all | solution.py:549
  12.2 0.6 copy-done.10
  12.9 0.1 slice_select_fusion
  12.9 11.0 %all-to-all-done.got = f32[8,96,128]{2,1,0:T(8,128)S(1)} async-done(((f32[8,96,128]{2,1,0:T(8,128)}), f32[8,96,128]{2,1,0:T(8,128)S(1)}, u32[]{:S(2)}, u32[]{:S(2)}) %all-to-all-start) | async-done | bytes 393248 | tf_op jit(solution)/shard_map/all_to_all | solution.py:549
  23.9 0.2 shard_map.138
  24.1 6.3 %collective-permute-start.1 = (f32[608,128]{1,0:T(8,128)S(1)}, f32[608,128]{1,0:T(8,128)S(1)}, u32[]{:S(2)}, u32[]{:S(2)}) collective-permute-start(f32[608,128]{1,0:T(8,128)S(1)} %get-tuple-element.29.prev_cot), channel_id=1, source_target_pairs={{0,159},{1,0},{2,1},{3,2},{4,131},{5,4},{6,5},{7,6},{8,135},{9,8},... | collective-permute-start | bytes 933896 | tf_op jit(solution)/shard_map/ppermute | solution.py:527
  30.3 0.0 collective-permute-start
  30.3 0.0 copy-start.9
  30.3 0.1 copy.25.w_in
  30.5 0.5 copy-done.9
  31.0 0.1 copy.23
  31.1 0.1 copy.29
  31.2 0.5 copy-done.7
  31.8 0.1 copy.22
  31.9 0.0 copy-start.6
  31.9 10.7 %collective-permute-done.1.after.cot_after = f32[608,128]{1,0:T(8,128)S(1)} collective-permute-done((f32[608,128]{1,0:T(8,128)S(1)}, f32[608,128]{1,0:T(8,128)S(1)}, u32[]{:S(2)}, u32[]{:S(2)}) %collective-permute-start.1) | collective-permute-done | bytes 311328 | tf_op jit(solution)/shard_map/ppermute | solution.py:527
  42.6 1.6 %collective-permute-done.before.cot_before = f32[608,128]{1,0:T(8,128)S(1)} collective-permute-done((f32[608,128]{1,0:T(8,128)S(1)}, f32[608,128]{1,0:T(8,128)S(1)}, u32[]{:S(2)}, u32[]{:S(2)}) %collective-permute-start) | collective-permute-done | bytes 311328 | tf_op jit(solution)/shard_map/ppermute | solution.py:527
  44.2 5.4 %shard_map.139 = (f32[1728,128]{1,0:T(8,128)S(1)}, f32[216,128]{1,0:T(8,128)S(1)}, f32[216,128]{1,0:T(8,128)S(1)}, f32[1024,128]{1,0:T(8,128)S(1)}, f32[336,128]...) custom-call(f32[608,128]{1,0:T(8,128)S(1)} %get-tuple-element.28.own.next_cot, ...), custom_call_target="tpu_custom_call" | custom-call | flops 12000000000 | bytes 1000000 | tf_op jit(solution)/shard_map/pallas_call | solution.py:503
  49.7 7.0 %collective-permute-start.3 = (f32[336,128]{1,0:T(8,128)S(1)}, f32[336,128]{1,0:T(8,128)S(1)}, u32[]{:S(2)}, u32[]{:S(2)}) collective-permute-start(f32[336,128]{1,0:T(8,128)S(1)} %get-tuple-element.30.own), channel_id=1, source_target_pairs={{0,159},{1,0},{2,1},{3,2},{4,131},{5,4},{6,5},{7,6},{8,135},{9,8},... | collective-permute-start | bytes 516104 | tf_op jit(solution)/shard_map/ppermute | solution.py:527
  56.7 0.0 collective-permute-start.2
  56.7 0.0 collective-permute-start.6
  56.7 7.8 %collective-permute-start.7 = (f32[288,128]{1,0:T(8,128)S(1)}, f32[288,128]{1,0:T(8,128)S(1)}, u32[]{:S(2)}, u32[]{:S(2)}) collective-permute-start(f32[288,128]{1,0:T(8,128)S(1)} %get-tuple-element.38), channel_id=1, source_target_pairs={{0,159},{1,0},{2,1},{3,2},{4,131},{5,4},{6,5},{7,6},{8,135},{9,8},... | collective-permute-start | bytes 442376 | tf_op jit(solution)/shard_map/ppermute | solution.py:527
  64.5 0.0 collective-permute-done.3.after
  64.5 2.8 %collective-permute-done.2.before = f32[336,128]{1,0:T(8,128)S(1)} collective-permute-done((f32[336,128]{1,0:T(8,128)S(1)}, f32[336,128]{1,0:T(8,128)S(1)}, u32[]{:S(2)}, u32[]{:S(2)}) %collective-permute-start.2) | collective-permute-done | bytes 172064 | tf_op jit(solution)/shard_map/ppermute | solution.py:527
  67.3 5.6 %shard_map.140 = (f32[384,128]{1,0:T(8,128)S(1)}, f32[288,128]{1,0:T(8,128)S(1)}, f32[256,128]{1,0:T(8,128)S(1)}, f32[256,128]{1,0:T(8,128)S(1)}, f32[160,128]{1,0:T(8,128)S(1)}) custom-call(f32[336,128]{1,0:T(8,128)S(1)} %get-tuple-element.30.own, f32[336,128]{1,0:T(8,128)S(1)} %collective-permute-done.2.before, ...), custom_call_target="tpu_custom_call" | custom-call | flops 11000000512 | bytes 1000000 | tf_op jit(solution)/shard_map/pallas_call | solution.py:503
  72.9 0.1 collective-permute-start.5
  73.0 1.5 collective-permute-start.4
  74.4 0.0 collective-permute-done.6.one_before
  74.4 0.0 collective-permute-done.7.one_after
  74.4 2.5 %collective-permute-done.5.after = f32[288,128]{1,0:T(8,128)S(1)} collective-permute-done((f32[288,128]{1,0:T(8,128)S(1)}, f32[288,128]{1,0:T(8,128)S(1)}, u32[]{:S(2)}, u32[]{:S(2)}) %collective-permute-start.5) | collective-permute-done | bytes 147488 | tf_op jit(solution)/shard_map/ppermute | solution.py:527
  77.0 6.6 %collective-permute-done.4.before = f32[288,128]{1,0:T(8,128)S(1)} collective-permute-done((f32[288,128]{1,0:T(8,128)S(1)}, f32[288,128]{1,0:T(8,128)S(1)}, u32[]{:S(2)}, u32[]{:S(2)}) %collective-permute-start.4) | collective-permute-done | bytes 147488 | tf_op jit(solution)/shard_map/ppermute | solution.py:527
  83.6 10.0 %shard_map.141 = f32[8,68,128]{2,1,0:T(8,128)S(1)} custom-call(f32[384,128]{1,0:T(8,128)S(1)} %get-tuple-element.34.own, f32[288,128]{1,0:T(8,128)S(1)} %collective-permute-done.4.before, f32[288,128]{1,0:T(8,128)S(1)} %collective-permute-done.5.after, f32[1024,128]{1,0:T(8,128)S(1)} %get-tuple-element.36.one, ...), custom_call_target="tpu_custom_call" | custom-call | flops 20000000000 | bytes 1000000 | tf_op jit(solution)/shard_map/pallas_call | solution.py:503
  93.6 24.5 %all_to_all.20.got = f32[8,68,128]{2,1,0:T(8,128)S(1)} all-to-all(f32[8,68,128]{2,1,0:T(8,128)S(1)} %shard_map.141), channel_id=1, replica_groups=mesh['gz'=8,'gx'=32] {'gz'}, dimensions={0} | all-to-all | bytes 557056 | tf_op jit(solution)/shard_map/all_to_all | solution.py:603
  118.1 9.5 %all_to_all.21 = f32[16,20,128]{2,1,0:T(8,128)S(1)} all-to-all(f32[16,20,128]{2,1,0:T(8,128)S(1)} %shard_map.143), channel_id=1, replica_groups={{0,1,2,3,8,9,10,11,16,17,18,19,24,25,26,27},{4,5,6,7,12,13,14,15,20,21,..., dimensions={0} | all-to-all | bytes 327680 | tf_op jit(solution)/shard_map/all_to_all | solution.py:618
  127.7 0.7 broadcast_in_dim.3
  128.3 5.3 %all-to-all-start.3 = ((f32[16,20,128]{2,1,0:T(8,128)}), f32[16,20,128]{2,1,0:T(8,128)S(1)}, u32[]{:S(2)}, u32[]{:S(2)}) async-start(f32[16,20,128]{2,1,0:T(8,128)} %broadcast_in_dim.3), calls=%async_computation.3 | async-start | bytes 393216 | tf_op jit(solution)/shard_map/all_to_all | solution.py:620
  133.6 0.0 copy-done
  133.6 1.1 shard_map.142
  134.7 9.3 %all-to-all-done.3.got = f32[16,20,128]{2,1,0:T(8,128)S(1)} async-done(((f32[16,20,128]{2,1,0:T(8,128)}), f32[16,20,128]{2,1,0:T(8,128)S(1)}, u32[]{:S(2)}, u32[]{:S(2)}) %all-to-all-start.3) | async-done | bytes 163872 | tf_op jit(solution)/shard_map/all_to_all | solution.py:620
  144.0 0.6 shard_map.144
  144.7 0.7 copy.28
  (17 shorter events, 0.1 us)
Async XLA Ops:
  0.6 0.7 copy-start.3
  0.6 0.7 copy-start.5
  0.7 0.7 copy-start.4
  1.3 0.9 copy-start.1
  2.2 0.9 copy-start.2
  4.7 7.5 %copy-start.8 = (bf16[128,12]{0,1:T(8,128)(2,1)S(1)}, bf16[128,12]{0,1:T(8,128)(2,1)}, u32[]{:S(2)}) copy-start(bf16[128,12]{0,1:T(8,128)(2,1)} %param.12) | copy-start | bytes 9220
  4.7 19.2 %all-to-all-start = ((f32[8,96,128]{2,1,0:T(8,128)}), f32[8,96,128]{2,1,0:T(8,128)S(1)}, u32[]{:S(2)}, u32[]{:S(2)}) async-start(f32[8,96,128]{2,1,0:T(8,128)} %get-tuple-element.26), calls=%async_computation | async-start | bytes 786432 | tf_op jit(solution)/shard_map/all_to_all | solution.py:549
  12.2 0.7 copy-start.10
  24.1 18.6 %collective-permute-start.1 = (f32[608,128]{1,0:T(8,128)S(1)}, f32[608,128]{1,0:T(8,128)S(1)}, u32[]{:S(2)}, u32[]{:S(2)}) collective-permute-start(f32[608,128]{1,0:T(8,128)S(1)} %get-tuple-element.29.prev_cot), channel_id=1, source_target_pairs={{0,159},{1,0},{2,1},{3,2},{4,131},{5,4},{6,5},{7,6},{8,135},{9,8},... | collective-permute-start | bytes 933896 | tf_op jit(solution)/shard_map/ppermute | solution.py:527
  30.3 13.9 %collective-permute-start = (f32[608,128]{1,0:T(8,128)S(1)}, f32[608,128]{1,0:T(8,128)S(1)}, u32[]{:S(2)}, u32[]{:S(2)}) collective-permute-start(f32[608,128]{1,0:T(8,128)S(1)} %get-tuple-element.28.own.next_cot), channel_id=1, source_target_pairs={{0,1},{1,2},{2,3},{3,132},{4,5},{5,6},{6,7},{7,136},{8,9},{9,10},{... | collective-permute-start | bytes 933896 | tf_op jit(solution)/shard_map/ppermute | solution.py:527
  30.3 0.7 copy-start.9
  31.0 0.8 copy-start.7
  31.9 12.3 %copy-start.6 = (f32[128,128]{1,0:T(8,128)S(1)}, f32[128,128]{1,0:T(8,128)}, u32[]{:S(2)}) copy-start(f32[128,128]{1,0:T(8,128)} %radiation.5) | copy-start | bytes 196612
  49.7 14.8 %collective-permute-start.3 = (f32[336,128]{1,0:T(8,128)S(1)}, f32[336,128]{1,0:T(8,128)S(1)}, u32[]{:S(2)}, u32[]{:S(2)}) collective-permute-start(f32[336,128]{1,0:T(8,128)S(1)} %get-tuple-element.30.own), channel_id=1, source_target_pairs={{0,159},{1,0},{2,1},{3,2},{4,131},{5,4},{6,5},{7,6},{8,135},{9,8},... | collective-permute-start | bytes 516104 | tf_op jit(solution)/shard_map/ppermute | solution.py:527
  56.7 10.6 %collective-permute-start.2 = (f32[336,128]{1,0:T(8,128)S(1)}, f32[336,128]{1,0:T(8,128)S(1)}, u32[]{:S(2)}, u32[]{:S(2)}) collective-permute-start(f32[336,128]{1,0:T(8,128)S(1)} %get-tuple-element.30.own), channel_id=1, source_target_pairs={{0,1},{1,2},{2,3},{3,132},{4,5},{5,6},{6,7},{7,136},{8,9},{9,10},{... | collective-permute-start | bytes 516104 | tf_op jit(solution)/shard_map/ppermute | solution.py:527
  56.7 17.8 %collective-permute-start.6 = (f32[288,128]{1,0:T(8,128)S(1)}, f32[288,128]{1,0:T(8,128)S(1)}, u32[]{:S(2)}, u32[]{:S(2)}) collective-permute-start(f32[288,128]{1,0:T(8,128)S(1)} %get-tuple-element.37), channel_id=1, source_target_pairs={{0,1},{1,2},{2,3},{3,132},{4,5},{5,6},{6,7},{7,136},{8,9},{9,10},{... | collective-permute-start | bytes 442376 | tf_op jit(solution)/shard_map/ppermute | solution.py:527
  56.7 17.8 %collective-permute-start.7 = (f32[288,128]{1,0:T(8,128)S(1)}, f32[288,128]{1,0:T(8,128)S(1)}, u32[]{:S(2)}, u32[]{:S(2)}) collective-permute-start(f32[288,128]{1,0:T(8,128)S(1)} %get-tuple-element.38), channel_id=1, source_target_pairs={{0,159},{1,0},{2,1},{3,2},{4,131},{5,4},{6,5},{7,6},{8,135},{9,8},... | collective-permute-start | bytes 442376 | tf_op jit(solution)/shard_map/ppermute | solution.py:527
  72.9 4.1 %collective-permute-start.5 = (f32[288,128]{1,0:T(8,128)S(1)}, f32[288,128]{1,0:T(8,128)S(1)}, u32[]{:S(2)}, u32[]{:S(2)}) collective-permute-start(f32[288,128]{1,0:T(8,128)S(1)} %get-tuple-element.35), channel_id=1, source_target_pairs={{0,159},{1,0},{2,1},{3,2},{4,131},{5,4},{6,5},{7,6},{8,135},{9,8},... | collective-permute-start | bytes 442376 | tf_op jit(solution)/shard_map/ppermute | solution.py:527
  73.0 10.6 %collective-permute-start.4 = (f32[288,128]{1,0:T(8,128)S(1)}, f32[288,128]{1,0:T(8,128)S(1)}, u32[]{:S(2)}, u32[]{:S(2)}) collective-permute-start(f32[288,128]{1,0:T(8,128)S(1)} %get-tuple-element.35), channel_id=1, source_target_pairs={{0,1},{1,2},{2,3},{3,132},{4,5},{5,6},{6,7},{7,136},{8,9},{9,10},{... | collective-permute-start | bytes 442376 | tf_op jit(solution)/shard_map/ppermute | solution.py:527
  128.3 5.3 %copy-start = (bf16[256,256]{1,0:T(8,128)(2,1)S(1)}, bf16[256,256]{1,0:T(8,128)(2,1)}, u32[]{:S(2)}) copy-start(bf16[256,256]{1,0:T(8,128)(2,1)} %constant.12.clone.chosen) | copy-start | bytes 393220
  128.3 15.7 %all-to-all-start.3 = ((f32[16,20,128]{2,1,0:T(8,128)}), f32[16,20,128]{2,1,0:T(8,128)S(1)}, u32[]{:S(2)}, u32[]{:S(2)}) async-start(f32[16,20,128]{2,1,0:T(8,128)} %broadcast_in_dim.3), calls=%async_computation.3 | async-start | bytes 393216 | tf_op jit(solution)/shard_map/all_to_all | solution.py:620

commit v5 on v4

--- a/solution.py
+++ b/solution.py
@@ -476,6 +476,14 @@
         out[other] = total
 
 
+def add_kernel(got, out):
+    total = got[0]
+    for other in range(1, got.shape[0]):
+        total = total + got[other]
+    for other in range(out.shape[0]):
+        out[other] = total
+
+
 def unpack_kernel(got, chosen, new_state, grad):
     turn = 4 * turned_half(lax.axis_index("gx"))
     rows = []
@@ -615,8 +623,8 @@
         for x in range(4)
         for y in range(4)
     ]
-    added = jnp.sum(lax.all_to_all(chunks, "gx", 0, 0, axis_index_groups=level), axis=0)
-    added = jnp.broadcast_to(added, (16, CHUNK, LEV))
+    chunks = lax.all_to_all(chunks, "gx", 0, 0, axis_index_groups=level)
+    (added,) = call(add_kernel, [(16, CHUNK, LEV)], [], chunks)
     totals = lax.all_to_all(added, ("gz", "gx"), 0, 0, axis_index_groups=line)
     grads = call(finish_kernel, [(128, 2 * NF), (128, LEV), (NF, LEV)], [], totals)
     return (new_state, grad_state, *grads)

time: 146 us -> 146 us (level)
    pallas_call x8 -> x9, Pallas kernels: 24.4 us -> 25.2 us  [call(): pl.pallas_call(kernel, out_shape=[jax.ShapeDtypeStruct(shape, F32) for sh...]
where the time goes in v5:
time: 146 us; the launch traced here: 145 us
  waiting for transfers between devices  44.5 us (30%)
  starting transfers between devices  35.4 us (24%)
  blocking collectives  34 us (23%)
  Pallas kernels  25.2 us (17%)
  local copies, waits for them, and re-layouts  5.37 us (4%)
    pallas_call x9, Pallas kernels, call(): pl.pallas_call(kernel, out_shape=[jax.ShapeDtypeStruct(shape, F32) for sh...  25.2 us
    all_to_all x1, blocking collectives, on_device(): got = lax.all_to_all(sent, 'gz', 0, 0)  24.5 us
    ppermute x8, waiting for transfers between devices, passed_along(): return lax.ppermute(shard, ('gz', 'gx'), pairs)  24.3 us
    ppermute x8, starting transfers between devices, passed_along(): return lax.ppermute(shard, ('gz', 'gx'), pairs)  22.6 us
    all_to_all x1, waiting for transfers between devices, on_device(): got = lax.all_to_all(packed, 'gz', 0, 0)  11 us
    all_to_all x1, blocking collectives, on_device(): chunks = lax.all_to_all(chunks, 'gx', 0, 0, axis_index_groups=level)  9.55 us
    all_to_all x1, waiting for transfers between devices, on_device(): totals = lax.all_to_all(added, ('gz', 'gx'), 0, 0, axis_index_groups=line)  9.29 us
    all_to_all x1, starting transfers between devices, on_device(): got = lax.all_to_all(packed, 'gz', 0, 0)  7.53 us
  transfers between devices with their start and end apart: 10, of which 7 were waited for; matrix products, arithmetic and copies ran while one was open for 0% of the time, Pallas kernels for 5%

profile of v5, /device:TPU:1, one launch (start us, length us, event | category | flops | bytes accessed | tf_op | source)
XLA Modules:
  0.0 145.3 jit_solution(14537241883936155789)
XLA Ops:
  0.6 0.0 copy-start.3
  0.6 0.0 copy-start.5
  0.7 0.7 copy-done.3
  1.3 0.0 copy-done.5
  1.3 0.0 copy-done.4
  1.3 0.9 copy-done.1
  2.2 0.9 copy-done.2
  3.1 1.5 %shard_map.137 = (f32[8,96,128]{2,1,0:T(8,128)}, f32[8,128]{1,0:T(8,128)S(1)}) custom-call(s32[8,128]{1,0:T(8,128)S(1)} %copy-done.3, f32[6,16,256]{2,1,0:T(8,128)S(1)} %copy-done.1, f32[6,16,256]{2,1,0:T(8,128)S(1)} %copy-done.2, f32[1,256]{1,0:T(1,128)S(1)} %bitcast.7, s32[1,256]{1,0:T(1,128)S(1)} %bitcast.8), custom_call_target="tpu_custom_call" | custom-call | tf_op jit(solution)/shard_map/pallas_call | solution.py:511
  4.7 7.5 %all-to-all-start = ((f32[8,96,128]{2,1,0:T(8,128)}), f32[8,96,128]{2,1,0:T(8,128)S(1)}, u32[]{:S(2)}, u32[]{:S(2)}) async-start(f32[8,96,128]{2,1,0:T(8,128)} %get-tuple-element.26), calls=%async_computation | async-start | bytes 786432 | tf_op jit(solution)/shard_map/all_to_all | solution.py:557
  12.2 0.6 copy-done.10
  12.9 0.1 slice_select_fusion
  12.9 11.0 %all-to-all-done.got = f32[8,96,128]{2,1,0:T(8,128)S(1)} async-done(((f32[8,96,128]{2,1,0:T(8,128)}), f32[8,96,128]{2,1,0:T(8,128)S(1)}, u32[]{:S(2)}, u32[]{:S(2)}) %all-to-all-start) | async-done | bytes 393248 | tf_op jit(solution)/shard_map/all_to_all | solution.py:557
  23.9 0.2 shard_map.138
  24.1 6.3 %collective-permute-start.1 = (f32[608,128]{1,0:T(8,128)S(1)}, f32[608,128]{1,0:T(8,128)S(1)}, u32[]{:S(2)}, u32[]{:S(2)}) collective-permute-start(f32[608,128]{1,0:T(8,128)S(1)} %get-tuple-element.29.prev_cot), channel_id=1, source_target_pairs={{0,159},{1,0},{2,1},{3,2},{4,131},{5,4},{6,5},{7,6},{8,135},{9,8},... | collective-permute-start | bytes 933896 | tf_op jit(solution)/shard_map/ppermute | solution.py:535
  30.3 0.0 collective-permute-start
  30.3 0.0 copy-start.9
  30.3 0.1 copy.25.w_in
  30.5 0.5 copy-done.9
  31.0 0.1 copy.23
  31.2 0.1 copy.29
  31.2 0.5 copy-done.7
  31.8 0.1 copy.22
  31.9 0.0 copy-start.6
  31.9 10.7 %collective-permute-done.1.after.cot_after = f32[608,128]{1,0:T(8,128)S(1)} collective-permute-done((f32[608,128]{1,0:T(8,128)S(1)}, f32[608,128]{1,0:T(8,128)S(1)}, u32[]{:S(2)}, u32[]{:S(2)}) %collective-permute-start.1) | collective-permute-done | bytes 311328 | tf_op jit(solution)/shard_map/ppermute | solution.py:535
  42.6 1.6 %collective-permute-done.before.cot_before = f32[608,128]{1,0:T(8,128)S(1)} collective-permute-done((f32[608,128]{1,0:T(8,128)S(1)}, f32[608,128]{1,0:T(8,128)S(1)}, u32[]{:S(2)}, u32[]{:S(2)}) %collective-permute-start) | collective-permute-done | bytes 311328 | tf_op jit(solution)/shard_map/ppermute | solution.py:535
  44.3 5.4 %shard_map.139 = (f32[1728,128]{1,0:T(8,128)S(1)}, f32[216,128]{1,0:T(8,128)S(1)}, f32[216,128]{1,0:T(8,128)S(1)}, f32[1024,128]{1,0:T(8,128)S(1)}, f32[336,128]...) custom-call(f32[608,128]{1,0:T(8,128)S(1)} %get-tuple-element.28.own.next_cot, ...), custom_call_target="tpu_custom_call" | custom-call | flops 12000000000 | bytes 1000000 | tf_op jit(solution)/shard_map/pallas_call | solution.py:511
  49.7 7.0 %collective-permute-start.3 = (f32[336,128]{1,0:T(8,128)S(1)}, f32[336,128]{1,0:T(8,128)S(1)}, u32[]{:S(2)}, u32[]{:S(2)}) collective-permute-start(f32[336,128]{1,0:T(8,128)S(1)} %get-tuple-element.30.own), channel_id=1, source_target_pairs={{0,159},{1,0},{2,1},{3,2},{4,131},{5,4},{6,5},{7,6},{8,135},{9,8},... | collective-permute-start | bytes 516104 | tf_op jit(solution)/shard_map/ppermute | solution.py:535
  56.7 0.0 collective-permute-start.2
  56.7 0.0 collective-permute-start.6
  56.7 7.8 %collective-permute-start.7 = (f32[288,128]{1,0:T(8,128)S(1)}, f32[288,128]{1,0:T(8,128)S(1)}, u32[]{:S(2)}, u32[]{:S(2)}) collective-permute-start(f32[288,128]{1,0:T(8,128)S(1)} %get-tuple-element.38), channel_id=1, source_target_pairs={{0,159},{1,0},{2,1},{3,2},{4,131},{5,4},{6,5},{7,6},{8,135},{9,8},... | collective-permute-start | bytes 442376 | tf_op jit(solution)/shard_map/ppermute | solution.py:535
  64.5 0.0 collective-permute-done.3.after
  64.5 2.8 %collective-permute-done.2.before = f32[336,128]{1,0:T(8,128)S(1)} collective-permute-done((f32[336,128]{1,0:T(8,128)S(1)}, f32[336,128]{1,0:T(8,128)S(1)}, u32[]{:S(2)}, u32[]{:S(2)}) %collective-permute-start.2) | collective-permute-done | bytes 172064 | tf_op jit(solution)/shard_map/ppermute | solution.py:535
  67.3 5.6 %shard_map.140 = (f32[384,128]{1,0:T(8,128)S(1)}, f32[288,128]{1,0:T(8,128)S(1)}, f32[256,128]{1,0:T(8,128)S(1)}, f32[256,128]{1,0:T(8,128)S(1)}, f32[160,128]{1,0:T(8,128)S(1)}) custom-call(f32[336,128]{1,0:T(8,128)S(1)} %get-tuple-element.30.own, f32[336,128]{1,0:T(8,128)S(1)} %collective-permute-done.2.before, ...), custom_call_target="tpu_custom_call" | custom-call | flops 11000000512 | bytes 1000000 | tf_op jit(solution)/shard_map/pallas_call | solution.py:511
  72.9 0.1 collective-permute-start.5
  73.0 1.5 collective-permute-start.4
  74.4 0.0 collective-permute-done.6.one_before
  74.5 0.0 collective-permute-done.7.one_after
  74.5 2.5 %collective-permute-done.5.after = f32[288,128]{1,0:T(8,128)S(1)} collective-permute-done((f32[288,128]{1,0:T(8,128)S(1)}, f32[288,128]{1,0:T(8,128)S(1)}, u32[]{:S(2)}, u32[]{:S(2)}) %collective-permute-start.5) | collective-permute-done | bytes 147488 | tf_op jit(solution)/shard_map/ppermute | solution.py:535
  77.0 6.6 %collective-permute-done.4.before = f32[288,128]{1,0:T(8,128)S(1)} collective-permute-done((f32[288,128]{1,0:T(8,128)S(1)}, f32[288,128]{1,0:T(8,128)S(1)}, u32[]{:S(2)}, u32[]{:S(2)}) %collective-permute-start.4) | collective-permute-done | bytes 147488 | tf_op jit(solution)/shard_map/ppermute | solution.py:535
  83.6 10.0 %shard_map.141 = f32[8,68,128]{2,1,0:T(8,128)S(1)} custom-call(f32[384,128]{1,0:T(8,128)S(1)} %get-tuple-element.34.own, f32[288,128]{1,0:T(8,128)S(1)} %collective-permute-done.4.before, f32[288,128]{1,0:T(8,128)S(1)} %collective-permute-done.5.after, f32[1024,128]{1,0:T(8,128)S(1)} %get-tuple-element.36.one, ...), custom_call_target="tpu_custom_call" | custom-call | flops 20000000000 | bytes 1000000 | tf_op jit(solution)/shard_map/pallas_call | solution.py:511
  93.6 24.5 %all_to_all.20.got = f32[8,68,128]{2,1,0:T(8,128)S(1)} all-to-all(f32[8,68,128]{2,1,0:T(8,128)S(1)} %shard_map.141), channel_id=1, replica_groups=mesh['gz'=8,'gx'=32] {'gz'}, dimensions={0} | all-to-all | bytes 557056 | tf_op jit(solution)/shard_map/all_to_all | solution.py:611
  118.1 9.5 %all_to_all.21.got = f32[16,20,128]{2,1,0:T(8,128)S(1)} all-to-all(f32[16,20,128]{2,1,0:T(8,128)S(1)} %shard_map.143), channel_id=1, replica_groups={{0,1,2,3,8,9,10,11,16,17,18,19,24,25,26,27},{4,5,6,7,12,13,14,15,20,21,..., dimensions={0} | all-to-all | bytes 327680 | tf_op jit(solution)/shard_map/all_to_all | solution.py:626
  127.6 0.7 shard_map.144
  128.3 5.3 %all-to-all-start.3 = ((f32[16,20,128]{2,1,0:T(8,128)}), f32[16,20,128]{2,1,0:T(8,128)S(1)}, u32[]{:S(2)}, u32[]{:S(2)}) async-start(f32[16,20,128]{2,1,0:T(8,128)} %shard_map.144), calls=%async_computation.3 | async-start | bytes 393216 | tf_op jit(solution)/shard_map/all_to_all | solution.py:628
  133.6 1.1 shard_map.142
  134.7 9.3 %all-to-all-done.3.got = f32[16,20,128]{2,1,0:T(8,128)S(1)} async-done(((f32[16,20,128]{2,1,0:T(8,128)}), f32[16,20,128]{2,1,0:T(8,128)S(1)}, u32[]{:S(2)}, u32[]{:S(2)}) %all-to-all-start.3) | async-done | bytes 163872 | tf_op jit(solution)/shard_map/all_to_all | solution.py:628
  144.0 0.6 shard_map.145
  144.7 0.7 copy.28
  (16 shorter events, 0.1 us)
Async XLA Ops:
  0.6 0.7 copy-start.3
  0.6 0.7 copy-start.5
  0.7 0.7 copy-start.4
  1.3 0.9 copy-start.1
  2.2 0.9 copy-start.2
  4.7 7.5 %copy-start.8 = (bf16[128,12]{0,1:T(8,128)(2,1)S(1)}, bf16[128,12]{0,1:T(8,128)(2,1)}, u32[]{:S(2)}) copy-start(bf16[128,12]{0,1:T(8,128)(2,1)} %param.12) | copy-start | bytes 9220
  4.7 19.2 %all-to-all-start = ((f32[8,96,128]{2,1,0:T(8,128)}), f32[8,96,128]{2,1,0:T(8,128)S(1)}, u32[]{:S(2)}, u32[]{:S(2)}) async-start(f32[8,96,128]{2,1,0:T(8,128)} %get-tuple-element.26), calls=%async_computation | async-start | bytes 786432 | tf_op jit(solution)/shard_map/all_to_all | solution.py:557
  12.2 0.7 copy-start.10
  24.1 18.6 %collective-permute-start.1 = (f32[608,128]{1,0:T(8,128)S(1)}, f32[608,128]{1,0:T(8,128)S(1)}, u32[]{:S(2)}, u32[]{:S(2)}) collective-permute-start(f32[608,128]{1,0:T(8,128)S(1)} %get-tuple-element.29.prev_cot), channel_id=1, source_target_pairs={{0,159},{1,0},{2,1},{3,2},{4,131},{5,4},{6,5},{7,6},{8,135},{9,8},... | collective-permute-start | bytes 933896 | tf_op jit(solution)/shard_map/ppermute | solution.py:535
  30.3 13.9 %collective-permute-start = (f32[608,128]{1,0:T(8,128)S(1)}, f32[608,128]{1,0:T(8,128)S(1)}, u32[]{:S(2)}, u32[]{:S(2)}) collective-permute-start(f32[608,128]{1,0:T(8,128)S(1)} %get-tuple-element.28.own.next_cot), channel_id=1, source_target_pairs={{0,1},{1,2},{2,3},{3,132},{4,5},{5,6},{6,7},{7,136},{8,9},{9,10},{... | collective-permute-start | bytes 933896 | tf_op jit(solution)/shard_map/ppermute | solution.py:535
  30.3 0.7 copy-start.9
  31.0 0.8 copy-start.7
  31.9 12.3 %copy-start.6 = (f32[128,128]{1,0:T(8,128)S(1)}, f32[128,128]{1,0:T(8,128)}, u32[]{:S(2)}) copy-start(f32[128,128]{1,0:T(8,128)} %radiation.5) | copy-start | bytes 196612
  49.7 14.8 %collective-permute-start.3 = (f32[336,128]{1,0:T(8,128)S(1)}, f32[336,128]{1,0:T(8,128)S(1)}, u32[]{:S(2)}, u32[]{:S(2)}) collective-permute-start(f32[336,128]{1,0:T(8,128)S(1)} %get-tuple-element.30.own), channel_id=1, source_target_pairs={{0,159},{1,0},{2,1},{3,2},{4,131},{5,4},{6,5},{7,6},{8,135},{9,8},... | collective-permute-start | bytes 516104 | tf_op jit(solution)/shard_map/ppermute | solution.py:535
  56.7 10.6 %collective-permute-start.2 = (f32[336,128]{1,0:T(8,128)S(1)}, f32[336,128]{1,0:T(8,128)S(1)}, u32[]{:S(2)}, u32[]{:S(2)}) collective-permute-start(f32[336,128]{1,0:T(8,128)S(1)} %get-tuple-element.30.own), channel_id=1, source_target_pairs={{0,1},{1,2},{2,3},{3,132},{4,5},{5,6},{6,7},{7,136},{8,9},{9,10},{... | collective-permute-start | bytes 516104 | tf_op jit(solution)/shard_map/ppermute | solution.py:535
  56.7 17.8 %collective-permute-start.6 = (f32[288,128]{1,0:T(8,128)S(1)}, f32[288,128]{1,0:T(8,128)S(1)}, u32[]{:S(2)}, u32[]{:S(2)}) collective-permute-start(f32[288,128]{1,0:T(8,128)S(1)} %get-tuple-element.37), channel_id=1, source_target_pairs={{0,1},{1,2},{2,3},{3,132},{4,5},{5,6},{6,7},{7,136},{8,9},{9,10},{... | collective-permute-start | bytes 442376 | tf_op jit(solution)/shard_map/ppermute | solution.py:535
  56.7 17.8 %collective-permute-start.7 = (f32[288,128]{1,0:T(8,128)S(1)}, f32[288,128]{1,0:T(8,128)S(1)}, u32[]{:S(2)}, u32[]{:S(2)}) collective-permute-start(f32[288,128]{1,0:T(8,128)S(1)} %get-tuple-element.38), channel_id=1, source_target_pairs={{0,159},{1,0},{2,1},{3,2},{4,131},{5,4},{6,5},{7,6},{8,135},{9,8},... | collective-permute-start | bytes 442376 | tf_op jit(solution)/shard_map/ppermute | solution.py:535
  72.9 4.1 %collective-permute-start.5 = (f32[288,128]{1,0:T(8,128)S(1)}, f32[288,128]{1,0:T(8,128)S(1)}, u32[]{:S(2)}, u32[]{:S(2)}) collective-permute-start(f32[288,128]{1,0:T(8,128)S(1)} %get-tuple-element.35), channel_id=1, source_target_pairs={{0,159},{1,0},{2,1},{3,2},{4,131},{5,4},{6,5},{7,6},{8,135},{9,8},... | collective-permute-start | bytes 442376 | tf_op jit(solution)/shard_map/ppermute | solution.py:535
  73.0 10.6 %collective-permute-start.4 = (f32[288,128]{1,0:T(8,128)S(1)}, f32[288,128]{1,0:T(8,128)S(1)}, u32[]{:S(2)}, u32[]{:S(2)}) collective-permute-start(f32[288,128]{1,0:T(8,128)S(1)} %get-tuple-element.35), channel_id=1, source_target_pairs={{0,1},{1,2},{2,3},{3,132},{4,5},{5,6},{6,7},{7,136},{8,9},{9,10},{... | collective-permute-start | bytes 442376 | tf_op jit(solution)/shard_map/ppermute | solution.py:535
  128.3 5.3 %copy-start = (bf16[256,256]{1,0:T(8,128)(2,1)S(1)}, bf16[256,256]{1,0:T(8,128)(2,1)}, u32[]{:S(2)}) copy-start(bf16[256,256]{1,0:T(8,128)(2,1)} %constant.10.clone.chosen) | copy-start | bytes 393220
  128.3 15.7 %all-to-all-start.3 = ((f32[16,20,128]{2,1,0:T(8,128)}), f32[16,20,128]{2,1,0:T(8,128)S(1)}, u32[]{:S(2)}, u32[]{:S(2)}) async-start(f32[16,20,128]{2,1,0:T(8,128)} %shard_map.144), calls=%async_computation.3 | async-start | bytes 393216 | tf_op jit(solution)/shard_map/all_to_all | solution.py:628
